TPU v7x, 32 devices: a whole 2x2x4 slice. The times are simulated.
32 devices in a mesh: groups: 2 (over x), tile: 16 (over z, y, core).
Axes of the slice: x: 2, y: 2, z: 4, core: 2. Of those that a mesh axis runs over, the one named last changes fastest.
Arguments:
- features: bfloat16 [2, 192, 160, 256], P('groups', 'tile'), parts along dimension 0, may hold values from -6 to 6
- cotangent: bfloat16 [2, 192, 160, 256], P('groups', 'tile'), parts along dimension 0, may hold values from -6 to 6
- weight_one: bfloat16 [256, 9, 256], replicated, may hold values from -0.125 to 0.125
- weight_two: bfloat16 [256, 9, 256], replicated, may hold values from -0.125 to 0.125
Outputs:
- block_out: bfloat16 [2, 192, 160, 256], P('groups', 'tile'), parts along dimension 0
- input_grad: bfloat16 [2, 192, 160, 256], P('groups', 'tile'), parts along dimension 0
- grad_one: float32 [256, 18, 256], P('tile', 'groups'), parts along dimension 1
- grad_two: float32 [256, 18, 256], P('tile', 'groups'), parts along dimension 1
There are 2 independent parts, one for each index of `groups`. A program takes and returns all parts, laid end to end along the dimension named above; an argument that names none is the same for every part. Nothing has to cross between parts.
All inputs are finite; a program needn't handle non-finite values.
Results may differ from a plain program's by a relative error of at most 0.0032.
Values may be sent and summed in bfloat16 or wider, within the bound.
No kernel may reach another device: no remote copies, remote signals or barrier semaphores. Data moves between devices by JAX's collectives and lax.ppermute only.
A program may use at most 128 MiB of HBM per device.

v0:
```python
import jax
import jax.numpy as jnp
from jax import lax
from jax.sharding import PartitionSpec as P


def extended_2(shard, sides, width):
    for axis, dim in sides:
        size, length = (lax.axis_size(axis), shard.shape[dim])
        up = [(i, (i + 1) % size) for i in range(size - 1)]
        down = [(j, i) for i, j in up]
        last = lax.slice_in_dim(shard, length - width, length, axis=dim)
        leading = lax.slice_in_dim(shard, 0, width, axis=dim)
        before = lax.ppermute(last, axis, up)
        after = lax.ppermute(leading, axis, down)
        shard = jnp.concatenate([before, shard, after], axis=dim)
    return shard


def pad_columns(field):
    return jnp.pad(field, ((0, 0), (0, 0), (1, 1), (0, 0)))


def band_forward(extended, kernel, row_count):
    col_count = extended.shape[2] - 2
    total = jnp.zeros((extended.shape[0], row_count, col_count, kernel.shape[2]), jnp.float32)
    for tap_index in range(9):
        row_shift = tap_index // 3 - 1
        col_shift = tap_index % 3 - 1
        piece = extended[
            :,
            1 + row_shift : 1 + row_shift + row_count,
            1 + col_shift : 1 + col_shift + col_count,
            :,
        ]
        total = total + jnp.einsum(
            "brwi,io->brwo", piece, kernel[:, tap_index, :], preferred_element_type=jnp.float32
        )
    return total


def band_transpose(extended, kernel, row_count):
    col_count = extended.shape[2] - 2
    total = jnp.zeros((extended.shape[0], row_count, col_count, kernel.shape[0]), jnp.float32)
    for tap_index in range(9):
        row_shift = tap_index // 3 - 1
        col_shift = tap_index % 3 - 1
        piece = extended[
            :,
            1 - row_shift : 1 - row_shift + row_count,
            1 - col_shift : 1 - col_shift + col_count,
            :,
        ]
        total = total + jnp.einsum(
            "brwo,io->brwi", piece, kernel[:, tap_index, :], preferred_element_type=jnp.float32
        )
    return total


def kernel_term(extended, grad, scale):
    row_count = grad.shape[1]
    col_count = grad.shape[2]
    taps = []
    for tap_index in range(9):
        row_shift = tap_index // 3 - 1
        col_shift = tap_index % 3 - 1
        piece = extended[
            :,
            1 + row_shift : 1 + row_shift + row_count,
            1 + col_shift : 1 + col_shift + col_count,
            :,
        ]
        taps.append(jnp.einsum("brwi,brwo->io", piece, grad, preferred_element_type=jnp.float32))
    return jnp.stack(taps, axis=1) * scale


def body(features, cotangent, weight_one, weight_two):
    batch_count, row_count, col_count, channel_count = features.shape
    tile_count = lax.axis_size("tile")
    scale = float(batch_count * row_count * tile_count * col_count) ** (-0.5)
    input_deep = pad_columns(extended_2(features, (("tile", 1),), 2))
    pre_ext = band_forward(input_deep, weight_one, row_count + 2)
    global_row = lax.axis_index("tile") * row_count + jnp.arange(row_count + 2, dtype=jnp.int32) - 1
    inside = (global_row >= 0) & (global_row < row_count * tile_count)
    hidden_wide = jnp.where(inside[None, :, None, None], jax.nn.silu(pre_ext), 0.0).astype(
        jnp.bfloat16
    )
    hidden_ext = pad_columns(hidden_wide)
    pre = pre_ext[:, 1 : row_count + 1]
    input_ext = input_deep[:, 1 : row_count + 3]
    block_out = (
        features.astype(jnp.float32) + band_forward(hidden_ext, weight_two, row_count)
    ).astype(jnp.bfloat16)
    cot_ext = pad_columns(extended_2(cotangent, (("tile", 1),), 1))
    hidden_grad = band_transpose(cot_ext, weight_two, row_count)
    sigma = jax.nn.sigmoid(pre)
    slope = (hidden_grad * sigma * (1.0 + pre * (1.0 - sigma))).astype(jnp.bfloat16)
    slope_ext = pad_columns(extended_2(slope, (("tile", 1),), 1))
    input_grad = (
        cotangent.astype(jnp.float32) + band_transpose(slope_ext, weight_one, row_count)
    ).astype(jnp.bfloat16)
    term_one = kernel_term(input_ext, slope, scale)
    term_two = kernel_term(hidden_ext, cotangent, scale)
    grad_one, grad_two = (
        lax.psum_scatter(term_one, "tile", scatter_dimension=0, tiled=True),
        lax.psum_scatter(term_two, "tile", scatter_dimension=0, tiled=True),
    )
    return (block_out, input_grad, grad_one, grad_two)


def solution(mesh):
    in_specs = (P("groups", "tile", None, None), P("groups", "tile", None, None), P(), P())
    out_specs = (
        P("groups", "tile", None, None),
        P("groups", "tile", None, None),
        P("tile", "groups", None),
        P("tile", "groups", None),
    )
    return jax.shard_map(body, mesh=mesh, in_specs=in_specs, out_specs=out_specs, check_vma=False)
```

profile of v0, /device:TPU:0, one launch (start us, length us, event | category | flops | bytes accessed | tf_op | source)
XLA Modules:
  0.0 191.2 jit_solution(103128488341649687)
XLA Ops:
  8.3 2.4 %collective-permute-start = (bf16[1,2,160,256]{3,2,1,0:T(8,128)(2,1)S(1)}, bf16[1,2,160,256]{3,2,1,0:T(8,128)(2,1)S(1)}, u32[]{:S(2)}, u32[]{:S(2)}) collective-permute-start(bf16[1,2,160,256]{3,2,1,0:T(8,128)(2,1)S(1)} %get-tuple-element.11), channel_id=1, source_target_pairs={{0,1},{1,2},{2,3},{3,4},{4,5},{5,6},{6,7},{7,8},{8,9},{9,10},{10,1... | collective-permute-start | bytes 491528 | tf_op jit(solution)/shard_map/ppermute | solution.py:14
  10.7 1.3 collective-permute-start.1
  13.0 5.1 %collective-permute-start.2 = (bf16[1,1,160,256]{3,2,1,0:T(8,128)(2,1)S(1)}, bf16[1,1,160,256]{3,2,1,0:T(8,128)(2,1)S(1)}, u32[]{:S(2)}, u32[]{:S(2)}) collective-permute-start(bf16[1,1,160,256]{3,2,1,0:T(8,128)(2,1)S(1)} %get-tuple-element.6), channel_id=1, source_target_pairs={{0,1},{1,2},{2,3},{3,4},{4,5},{5,6},{6,7},{7,8},{8,9},{9,10},{10,1... | collective-permute-start | bytes 245768 | tf_op jit(solution)/shard_map/ppermute | solution.py:14
  18.1 1.3 collective-permute-start.3
  19.4 2.7 %fusion.107 = f32[12,160,256]{2,1,0:T(8,128)} fusion(bf16[1,12,160,256]{3,2,1,0:T(8,128)(2,1)S(1)} %copy-done, bf16[256,9,256]{2,0,1:T(8,128)(2,1)} %param.7), kind=kOutput, calls=%fused_computation.152 | convolution fusion | flops 251658240 | bytes 3080192 | tf_op jit(solution)/shard_map/brwo,io->brwi/dot_general | solution.py:54
  23.4 1.8 fusion.67
  25.1 1.8 fusion.71
  27.0 1.8 fusion.72
  28.8 1.8 fusion.73
  30.5 1.7 fusion.74
  32.2 1.8 fusion.79
  34.0 1.7 fusion.76
  41.0 1.2 add_add_fusion
  48.0 1.7 broadcast_multiply_fusion
  50.0 6.9 %fusion.3 = bf16[1,12,160,256]{3,2,1,0:T(8,128)(2,1)S(1)} fusion(f32[1,14,160,256]{3,2,1,0:T(8,128)} %bitcast.406, f32[12,160,256]{2,1,0:T(8,128)} %fusion.67, f32[12,160,256]{2,1,0:T(8,128)} %fusion.71, f32[12,160,256]{2,1,0:T(8,128)} %fusion.72, f32[12,160,256]{2,1,0:T(8,128)} %fusion.107, f32[12,160,256]{2,1,0:T(8,128)} %fusion.73, ...), kind=kOutput, calls=%fused_computation.9 | convolution fusion | flops 260505600 | bytes 19873792 | tf_op jit(solution)/shard_map/brwo,io->brwi/dot_general | solution.py:54
  62.5 1.3 collective-permute-start.5
  63.8 5.9 %collective-permute-start.4 = (bf16[1,1,160,256]{3,2,1,0:T(8,128)(2,1)}, bf16[1,1,160,256]{3,2,1,0:T(8,128)(2,1)}, u32[]{:S(2)}, u32[]{:S(2)}) collective-permute-start(bf16[1,1,160,256]{3,2,1,0:T(8,128)(2,1)} %get-tuple-element.4), channel_id=1, source_target_pairs={{0,1},{1,2},{2,3},{3,4},{4,5},{5,6},{6,7},{7,8},{8,9},{9,10},{10,1... | collective-permute-start | bytes 245768 | tf_op jit(solution)/shard_map/ppermute | solution.py:14
  72.0 1.8 fusion.112
  73.8 1.7 fusion.115
  75.6 1.7 fusion.118
  77.3 1.7 fusion.121
  79.0 1.7 fusion.124
  80.7 1.7 fusion.132
  82.4 1.7 fusion.133
  84.1 1.7 fusion.134
  85.9 1.6 broadcast_multiply_fusion.1
  87.5 1.2 copy-done.6
  88.7 7.8 %fusion.4 = bf16[1,12,160,256]{3,2,1,0:T(8,128)(2,1)} fusion(f32[12,160,256]{2,1,0:T(8,128)} %fusion.134, f32[12,160,256]{2,1,0:T(8,128)} %fusion.112, f32[12,160,256]{2,1,0:T(8,128)} %fusion.115, f32[12,160,256]{2,1,0:T(8,128)} %fusion.133, f32[12,160,256]{2,1,0:T(8,128)} %fusion.118, f32[12,160,256]{2,1,0:T(8,128)} %fusion.121, ...), kind=kOutput, calls=%fused_computation.11 | convolution fusion | flops 257064960 | bytes 18972672 | tf_op jit(solution)/shard_map/brwi,io->brwo/dot_general | solution.py:36
  97.0 1.2 select_maximum_fusion
  101.5 3.0 %fusion.1 = bf16[1,12,160,256]{3,2,1,0:T(8,128)(2,1)} fusion(f32[12,160,256]{2,1,0:T(8,128)S(1)} %fusion.54, f32[12,160,256]{2,1,0:T(8,128)S(1)} %fusion.58, f32[12,160,256]{2,1,0:T(8,128)S(1)} %fusion.59, f32[12,160,256]{2,1,0:T(8,128)S(1)} %fusion.96, f32[12,160,256]{2,1,0:T(8,128)S(1)} %fusion.60, f32[12,160,256]{2,1,0:T(8,128)S(1)} %fusion.61, ...), kind=kOutput, calls=%fused_computation.6 | convolution fusion | flops 257556480 | bytes 18890752 | tf_op jit(solution)/shard_map/brwo,io->brwi/dot_general | solution.py:54
  104.4 13.3 %reduce-scatter.5.cloned.1.call-done = f32[16,9,256]{2,0,1:T(8,128)} async-done(((f32[256,9,256]{2,0,1:T(8,128)}), f32[16,9,256]{2,0,1:T(8,128)}) %reduce-scatter.5.cloned.1.call-update) | async-done | bytes 147472 | tf_op jit(solution)/shard_map/reduce_scatter | solution.py:106
  117.8 66.6 %reduce-scatter.3.cloned.1.call-done = f32[16,9,256]{2,0,1:T(8,128)} async-done(((f32[256,9,256]{2,0,1:T(8,128)}), f32[16,9,256]{2,0,1:T(8,128)}) %reduce-scatter.3.cloned.1.call-update) | async-done | bytes 147472 | tf_op jit(solution)/shard_map/reduce_scatter | solution.py:105
  (82 shorter events, 25.9 us)
Async XLA Ops:
  7.2 12.3 %copy-start = (bf16[1,12,160,256]{3,2,1,0:T(8,128)(2,1)S(1)}, bf16[1,12,160,256]{3,2,1,0:T(8,128)(2,1)}, u32[]{:S(2)}) copy-start(bf16[1,12,160,256]{3,2,1,0:T(8,128)(2,1)} %param.5) | copy-start | bytes 2949124
  7.2 110.6 %reduce-scatter.5.cloned.1.call-start = ((), (), s32[]{:S(2)}) async-start(), calls=%async_computation.3 | async-start | bytes 2506752 | tf_op jit(solution)/shard_map/reduce_scatter | solution.py:106
  8.3 27.4 %collective-permute-start = (bf16[1,2,160,256]{3,2,1,0:T(8,128)(2,1)S(1)}, bf16[1,2,160,256]{3,2,1,0:T(8,128)(2,1)S(1)}, u32[]{:S(2)}, u32[]{:S(2)}) collective-permute-start(bf16[1,2,160,256]{3,2,1,0:T(8,128)(2,1)S(1)} %get-tuple-element.11), channel_id=1, source_target_pairs={{0,1},{1,2},{2,3},{3,4},{4,5},{5,6},{6,7},{7,8},{8,9},{9,10},{10,1... | collective-permute-start | bytes 491528 | tf_op jit(solution)/shard_map/ppermute | solution.py:14
  10.7 25.3 %collective-permute-start.1 = (bf16[1,2,160,256]{3,2,1,0:T(8,128)(2,1)S(1)}, bf16[1,2,160,256]{3,2,1,0:T(8,128)(2,1)S(1)}, u32[]{:S(2)}, u32[]{:S(2)}) collective-permute-start(bf16[1,2,160,256]{3,2,1,0:T(8,128)(2,1)S(1)} %get-tuple-element.12), channel_id=1, source_target_pairs={{1,0},{2,1},{3,2},{4,3},{5,4},{6,5},{7,6},{8,7},{9,8},{10,9},{11,1... | collective-permute-start | bytes 491528 | tf_op jit(solution)/shard_map/ppermute | solution.py:15
  13.0 9.1 %collective-permute-start.2 = (bf16[1,1,160,256]{3,2,1,0:T(8,128)(2,1)S(1)}, bf16[1,1,160,256]{3,2,1,0:T(8,128)(2,1)S(1)}, u32[]{:S(2)}, u32[]{:S(2)}) collective-permute-start(bf16[1,1,160,256]{3,2,1,0:T(8,128)(2,1)S(1)} %get-tuple-element.6), channel_id=1, source_target_pairs={{0,1},{1,2},{2,3},{3,4},{4,5},{5,6},{6,7},{7,8},{8,9},{9,10},{10,1... | collective-permute-start | bytes 245768 | tf_op jit(solution)/shard_map/ppermute | solution.py:14
  18.1 4.4 %collective-permute-start.3 = (bf16[1,1,160,256]{3,2,1,0:T(8,128)(2,1)S(1)}, bf16[1,1,160,256]{3,2,1,0:T(8,128)(2,1)S(1)}, u32[]{:S(2)}, u32[]{:S(2)}) collective-permute-start(bf16[1,1,160,256]{3,2,1,0:T(8,128)(2,1)S(1)} %get-tuple-element.7), channel_id=1, source_target_pairs={{1,0},{2,1},{3,2},{4,3},{5,4},{6,5},{7,6},{8,7},{9,8},{10,9},{11,1... | collective-permute-start | bytes 245768 | tf_op jit(solution)/shard_map/ppermute | solution.py:15
  22.1 1.3 copy-start.9
  34.0 1.7 copy-start.4
  35.8 1.4 copy-start.7
  36.0 4.5 %copy-start.13 = (bf16[1,14,160,256]{3,2,1,0:T(8,128)(2,1)}, bf16[1,14,160,256]{3,2,1,0:T(8,128)(2,1)S(1)}, u32[]{:S(2)}) copy-start(bf16[1,14,160,256]{3,2,1,0:T(8,128)(2,1)S(1)} %get-tuple-element.8) | copy-start | bytes 3440644
  36.1 4.0 %copy-start.11 = (bf16[1,14,160,256]{3,2,1,0:T(8,128)(2,1)}, bf16[1,14,160,256]{3,2,1,0:T(8,128)(2,1)S(1)}, u32[]{:S(2)}) copy-start(bf16[1,14,160,256]{3,2,1,0:T(8,128)(2,1)S(1)} %get-tuple-element.16) | copy-start | bytes 3440644
  42.2 1.4 copy-start.3
  49.8 134.6 %reduce-scatter.3.cloned.1.call-start = ((), (), s32[]{:S(2)}) async-start(), calls=%async_computation.2 | async-start | bytes 2506752 | tf_op jit(solution)/shard_map/reduce_scatter | solution.py:105
  56.9 13.8 %copy-start.1 = (bf16[1,12,160,256]{3,2,1,0:T(8,128)(2,1)}, bf16[1,12,160,256]{3,2,1,0:T(8,128)(2,1)S(1)}, u32[]{:S(2)}) copy-start(bf16[1,12,160,256]{3,2,1,0:T(8,128)(2,1)S(1)} %fusion.3) | copy-start | bytes 2949124
  56.9 1.6 copy-start.14
  59.5 1.2 copy-start.5
  62.5 34.5 %collective-permute-start.5 = (bf16[1,1,160,256]{3,2,1,0:T(8,128)(2,1)}, bf16[1,1,160,256]{3,2,1,0:T(8,128)(2,1)S(1)}, u32[]{:S(2)}, u32[]{:S(2)}) collective-permute-start(bf16[1,1,160,256]{3,2,1,0:T(8,128)(2,1)} %get-tuple-element.5), channel_id=1, source_target_pairs={{1,0},{2,1},{3,2},{4,3},{5,4},{6,5},{7,6},{8,7},{9,8},{10,9},{11,1... | collective-permute-start | bytes 245768 | tf_op jit(solution)/shard_map/ppermute | solution.py:15
  63.8 6.5 %copy-start.12 = (bf16[1,14,160,256]{3,2,1,0:T(8,128)(2,1)S(1)}, bf16[1,14,160,256]{3,2,1,0:T(8,128)(2,1)}, u32[]{:S(2)}) copy-start(bf16[1,14,160,256]{3,2,1,0:T(8,128)(2,1)} %copy-done.11) | copy-start | bytes 3440644
  63.8 33.2 %collective-permute-start.4 = (bf16[1,1,160,256]{3,2,1,0:T(8,128)(2,1)}, bf16[1,1,160,256]{3,2,1,0:T(8,128)(2,1)}, u32[]{:S(2)}, u32[]{:S(2)}) collective-permute-start(bf16[1,1,160,256]{3,2,1,0:T(8,128)(2,1)} %get-tuple-element.4), channel_id=1, source_target_pairs={{0,1},{1,2},{2,3},{3,4},{4,5},{5,6},{6,7},{7,8},{8,9},{9,10},{10,1... | collective-permute-start | bytes 245768 | tf_op jit(solution)/shard_map/ppermute | solution.py:14
  70.7 1.3 copy-start.10
  87.5 1.2 copy-start.6
  88.7 7.8 %copy-start.2 = (bf16[1,12,160,256]{3,2,1,0:T(8,128)(2,1)S(1)}, bf16[1,12,160,256]{3,2,1,0:T(8,128)(2,1)}, u32[]{:S(2)}) copy-start(bf16[1,12,160,256]{3,2,1,0:T(8,128)(2,1)} %copy-done.1) | copy-start | bytes 2949124
  88.7 7.8 %copy-start.8 = (bf16[256,9,256]{2,0,1:T(8,128)(2,1)S(1)}, bf16[256,9,256]{2,0,1:T(8,128)(2,1)}, u32[]{:S(2)}) copy-start(bf16[256,9,256]{2,0,1:T(8,128)(2,1)} %param.6) | copy-start | bytes 3538948
Sparse Core Ops, SparseCore 0:
  49.9 67.8 reduce-scatter.4
  122.1 62.1 reduce-scatter.2
where the time goes:
time: 192 us; the launch traced here: 191 us
  waiting for transfers between devices  80.4 us (42%)
  matrix products  63.9 us (33%)
  starting transfers between devices  17.6 us (9%)
  between operations  14.5 us (8%)
  local copies, waits for them, and re-layouts  9.13 us (5%)
  other arithmetic  5.66 us (3%)
    reduce_scatter x1, waiting for transfers between devices, body(): lax.psum_scatter(term_one, 'tile', scatter_dimension=0, tiled=True)  66.6 us
    dot_general x18, matrix products, band_transpose(): jnp.einsum('brwo,io->brwi', piece, kernel[:, tap_index, :], preferred_ele...  28.5 us
    dot_general x18, matrix products, band_forward(): jnp.einsum('brwi,io->brwo', piece, kernel[:, tap_index, :], preferred_ele...  26.6 us
    ppermute x3, starting transfers between devices, extended_2(): before = lax.ppermute(last, axis, up)  13.5 us
    reduce_scatter x1, waiting for transfers between devices, body(): lax.psum_scatter(term_two, 'tile', scatter_dimension=0, tiled=True)  13.3 us
    dot_general x18, matrix products, kernel_term(): jnp.einsum('brwi,brwo->io', piece, grad, preferred_element_type=jnp.float32)  8.8 us
    unnamed x31, local copies, waits for them, and re-layouts  6.14 us
    ppermute x3, starting transfers between devices, extended_2(): after = lax.ppermute(leading, axis, down)  3.86 us
  transfers between devices with their start and end apart: 8, of which 3 were waited for; matrix products, arithmetic and copies ran while one was open for 31% of the time, Pallas kernels for 0%

commit v1 on v0

v1 whole, which is shorter than its diff:
```python
import functools

import jax
import jax.numpy as jnp
from jax import lax
from jax.experimental import pallas as pl
from jax.experimental.pallas import tpu as pltpu
from jax.sharding import PartitionSpec as P

F32 = jnp.float32
BF16 = jnp.bfloat16
WHOLE = pl.BlockSpec(memory_space=pltpu.VMEM)
LIMIT = 40 << 20


def run(kernel, outs, args, scratch=(), flops=0):
    nbytes = sum(a.size * a.dtype.itemsize for a in list(args) + list(outs))
    return pl.pallas_call(
        kernel,
        out_shape=outs,
        in_specs=[WHOLE] * len(args),
        out_specs=tuple(WHOLE for _ in outs),
        scratch_shapes=list(scratch),
        compiler_params=pltpu.CompilerParams(vmem_limit_bytes=LIMIT),
        cost_estimate=pl.CostEstimate(flops=flops, bytes_accessed=nbytes, transcendentals=0),
    )(*args)


def struct(shape, dtype):
    return jax.ShapeDtypeStruct(shape, dtype)


def pack_kernel(f_first, c_first, f_last, c_last, first, last):
    first[0:2] = f_first[...]
    first[2:4] = c_first[...]
    last[0:2] = f_last[...]
    last[2:4] = c_last[...]


def pack(features, cotangent):
    rows, cols, chans = features.shape
    block = (2, cols, chans)
    end = rows // 2 - 1
    first = pl.BlockSpec(block, lambda i: (0, 0, 0))
    last = pl.BlockSpec(block, lambda i: (end, 0, 0))
    out = struct((4, cols, chans), BF16)
    whole = pl.BlockSpec((4, cols, chans), lambda i: (0, 0, 0))
    return pl.pallas_call(
        pack_kernel,
        grid=(1,),
        out_shape=(out, out),
        in_specs=[first, first, last, last],
        out_specs=(whole, whole),
        compiler_params=pltpu.CompilerParams(vmem_limit_bytes=8 << 20),
    )(features, cotangent, features, cotangent)


def put_windows(dst, row, value, sign):
    cols, chans = value.shape
    wide = value.astype(F32)
    index = lax.broadcasted_iota(jnp.int32, (cols, chans), 0)
    before = jnp.where(index == 0, 0.0, pltpu.roll(wide, 1, 0)).astype(BF16)
    after = jnp.where(index == cols - 1, 0.0, pltpu.roll(wide, cols - 1, 0)).astype(BF16)
    here = pl.ds(pl.multiple_of(row * cols, cols), cols)
    low, high = (before, after) if sign > 0 else (after, before)
    dst[here, 0:chans] = low
    dst[here, chans : 2 * chans] = value
    dst[here, 2 * chans : 3 * chans] = high


def fill(dst, base, count, source, first, sign):
    def step(k, carry):
        put_windows(dst, base + k, source[first + k], sign)
        return carry

    lax.fori_loop(0, count, step, 0)


def conv_rows(win, weight, start, size, cols):
    left = jnp.concatenate(
        [win[pl.ds(pl.multiple_of(start + a * cols, cols), size), :] for a in range(3)], axis=1
    )
    return jnp.dot(left, weight[...], preferred_element_type=F32)


def conv_t_rows(win, weight, start, size, cols, chans):
    total = None
    for a in range(3):
        left = win[pl.ds(pl.multiple_of(start + (2 - a) * cols, cols), size), :]
        for b in range(3):
            tap = (a * 3 + b) * chans
            part = lax.dot_general(
                left[:, b * chans : (b + 1) * chans],
                weight[tap : tap + chans, :],
                (((1,), (1,)), ((), ())),
                preferred_element_type=F32,
            )
            total = part if total is None else total + part
    return total


def bit_order(count, order):
    bits = [b for b in order[1:]]
    return bits


def slot_static(j, bits):
    s = 0
    for b in bits:
        s = s * 2 + ((j >> b) & 1)
    return s


def slot_dynamic(me, bits):
    s = jnp.int32(0)
    for b in bits:
        s = s * 2 + ((me >> b) & 1)
    return s


def store_terms(tap, value, keep, send, me, n, order, scale):
    rows = value.shape[0] // n
    value = value * scale
    bits = bit_order(n, order)
    mine = slot_dynamic(me, bits)
    flip = ((me >> order[0]) & 1) == 1
    for j in range(n):
        if (j >> order[0]) & 1:
            continue
        other = j ^ (1 << order[0])
        low = value[j * rows : (j + 1) * rows]
        high = value[other * rows : (other + 1) * rows]
        slot = slot_static(j, bits) ^ mine
        keep[slot, tap] = jnp.where(flip, high, low)
        send[slot, tap] = jnp.where(flip, low, high).astype(BF16)


def kernel_terms(left, win, keep, send, me, n, order, scale, cols, size):
    chans = left.shape[1]
    for a in range(3):
        right = win[(2 - a) * cols : (2 - a) * cols + size, :]
        out = lax.dot_general(left, right, (((0,), (0,)), ((), ())), preferred_element_type=F32)
        for b in range(3):
            store_terms(
                a * 3 + b, out[:, b * chans : (b + 1) * chans], keep, send, me, n, order, scale
            )


def forward_kernel(n, order, scale, me_ref, f, up, down, c, w, hid, fac, keep, send, xs, cs):
    rows, cols, chans = f.shape
    me = me_ref[0]
    fill(xs, 0, 2, up, 0, 1)
    fill(xs, 2, rows, f, 0, 1)
    fill(xs, rows + 2, 2, down, 0, 1)
    fill(cs, 0, 1, up, 3, -1)
    fill(cs, 1, rows, c, 0, -1)
    fill(cs, rows + 1, 1, down, 2, -1)
    half = (rows + 2) // 2
    size = half * cols

    def step(k, carry):
        start = k * size
        pre = conv_rows(xs, w, start, size, cols)
        sigma = jax.nn.sigmoid(pre)
        here = pl.ds(pl.multiple_of(start, cols), size)
        hid[here, :] = (pre * sigma).astype(BF16)
        fac[here, :] = sigma * (1.0 + pre * (1.0 - sigma))
        return carry

    lax.fori_loop(0, 2, step, 0)

    @pl.when(me == 0)
    def _():
        hid[0:cols, :] = jnp.zeros((cols, chans), BF16)
        fac[0:cols, :] = jnp.zeros((cols, chans), F32)

    @pl.when(me == n - 1)
    def _():
        hid[(rows + 1) * cols : (rows + 2) * cols, :] = jnp.zeros((cols, chans), BF16)
        fac[(rows + 1) * cols : (rows + 2) * cols, :] = jnp.zeros((cols, chans), F32)

    own = hid[cols : (rows + 1) * cols, :]
    kernel_terms(own, cs, keep, send, me, n, order, scale, cols, rows * cols)


def slope_kernel(n, order, scale, me_ref, c, up, down, f, fac, w, slope, keep, send, cs, ss):
    rows, cols, chans = c.shape
    me = me_ref[0]
    fill(cs, 0, 2, up, 2, -1)
    fill(cs, 2, rows, c, 0, -1)
    fill(cs, rows + 2, 2, down, 2, -1)
    half = (rows + 2) // 2
    size = half * cols

    def step(k, carry):
        start = k * size
        grad = conv_t_rows(cs, w, start, size, cols, chans)
        here = pl.ds(pl.multiple_of(start, cols), size)
        slope[here, :] = (grad * fac[here, :]).astype(BF16)
        return carry

    lax.fori_loop(0, 2, step, 0)

    def widen(k, carry):
        here = pl.ds(pl.multiple_of(k * cols, cols), cols)
        put_windows(ss, k, slope[here, :], -1)
        return carry

    lax.fori_loop(0, rows + 2, widen, 0)
    own = f[...].reshape(rows * cols, chans)
    kernel_terms(own, ss, keep, send, me, n, order, scale, cols, rows * cols)


def outputs_kernel(hid, slope, f, c, w_one, w_two, block_out, input_grad, hs, ss):
    rows, cols, chans = f.shape

    def widen(k, carry):
        here = pl.ds(pl.multiple_of(k * cols, cols), cols)
        put_windows(hs, k, hid[here, :], 1)
        put_windows(ss, k, slope[here, :], -1)
        return carry

    lax.fori_loop(0, rows + 2, widen, 0)
    half = rows // 2
    size = half * cols

    def step(k, carry):
        start = k * size
        here = pl.ds(k * half, half)
        out = conv_rows(hs, w_two, start, size, cols)
        block_out[here] = (f[here].astype(F32) + out.reshape(half, cols, chans)).astype(BF16)
        out = conv_t_rows(ss, w_one, start, size, cols, chans)
        input_grad[here] = (c[here].astype(F32) + out.reshape(half, cols, chans)).astype(BF16)
        return carry

    lax.fori_loop(0, 2, step, 0)


def halve(keep, send, order, n):
    for stage, bit in enumerate(order):
        pairs = [(i, i ^ (1 << bit)) for i in range(n)]
        got = lax.ppermute(send, "tile", pairs)
        total = keep + got.astype(F32)
        half = total.shape[0] // 2
        if half:
            keep, send = total[:half], total[half:].astype(BF16)
        else:
            return jnp.swapaxes(total[0], 0, 1)


def body(features, cotangent, weight_one, weight_two):
    _, rows, cols, chans = features.shape
    n = lax.axis_size("tile")
    scale = float(rows * n * cols) ** (-0.5)
    me = lax.axis_index("tile").astype(jnp.int32).reshape(1)
    f, c = features[0], cotangent[0]
    taps = weight_one.shape[1]
    w_one = jnp.swapaxes(weight_one, 0, 1).reshape(taps * chans, chans)
    w_two = jnp.swapaxes(weight_two, 0, 1).reshape(taps * chans, chans)

    first, last = pack(f, c)
    up = lax.ppermute(last, "tile", [(i, i + 1) for i in range(n - 1)])
    down = lax.ppermute(first, "tile", [(i + 1, i) for i in range(n - 1)])

    bits = n.bit_length() - 1
    order_two = list(range(bits))
    order_one = [0, 2, 1] + list(range(3, bits)) if bits > 2 else order_two
    block = chans // n
    term = (n // 2, taps, block, chans)
    ext = (rows + 2) * cols
    flops = 2 * 9 * rows * cols * chans * chans
    smem = pl.BlockSpec(memory_space=pltpu.SMEM)

    def call(kernel, args, outs, scratch, work):
        return pl.pallas_call(
            kernel,
            out_shape=outs,
            in_specs=[smem] + [WHOLE] * len(args),
            out_specs=tuple(WHOLE for _ in outs),
            scratch_shapes=scratch,
            compiler_params=pltpu.CompilerParams(vmem_limit_bytes=LIMIT),
            cost_estimate=pl.CostEstimate(flops=work, bytes_accessed=8 << 20, transcendentals=0),
        )(me, *args)

    wide = 3 * chans
    hid, fac, keep_two, send_two = call(
        functools.partial(forward_kernel, n, order_two, scale),
        (f, up, down, c, w_one),
        (struct((ext, chans), BF16), struct((ext, chans), F32), struct(term, F32), struct(term, BF16)),
        [pltpu.VMEM(((rows + 4) * cols, wide), BF16), pltpu.VMEM((ext, wide), BF16)],
        2 * flops,
    )
    slope, keep_one, send_one = call(
        functools.partial(slope_kernel, n, order_one, scale),
        (c, up, down, f, fac, w_two),
        (struct((ext, chans), BF16), struct(term, F32), struct(term, BF16)),
        [pltpu.VMEM(((rows + 4) * cols, wide), BF16), pltpu.VMEM((ext, wide), BF16)],
        2 * flops,
    )
    block_out, input_grad = run(
        outputs_kernel,
        (struct(f.shape, BF16), struct(f.shape, BF16)),
        (hid, slope, f, c, w_one, w_two),
        [pltpu.VMEM((ext, wide), BF16), pltpu.VMEM((ext, wide), BF16)],
        2 * flops,
    )
    grad_two = halve(keep_two, send_two, order_two, n)
    grad_one = halve(keep_one, send_one, order_one, n)
    return (block_out[None], input_grad[None], grad_one, grad_two)


def solution(mesh):
    in_specs = (P("groups", "tile", None, None), P("groups", "tile", None, None), P(), P())
    out_specs = (
        P("groups", "tile", None, None),
        P("groups", "tile", None, None),
        P("tile", "groups", None),
        P("tile", "groups", None),
    )
    return jax.shard_map(body, mesh=mesh, in_specs=in_specs, out_specs=out_specs, check_vma=False)
```

time: 192 us -> 61.8 us (0.32)
  waiting for transfers between devices: 80.4 us -> 13.4 us
  matrix products: 63.9 us -> 0 us
  Pallas kernels: 0 us -> 24.1 us
  between operations: 14.5 us -> 0.79 us
  local copies, waits for them, and re-layouts: 9.13 us -> 2.56 us
  other arithmetic: 5.66 us -> 1.99 us
    reduce_scatter x2 -> x0, waiting for transfers between devices: 79.9 us -> none  [the longest x1 66.6 us: body(): lax.psum_scatter(term_one, 'tile', scatter_dimension=0, tiled=True)]
    dot_general x54 -> x0, matrix products: 63.9 us -> none  [the longest x18 28.5 us: band_transpose(): jnp.einsum('brwo,io->brwi', piece, kernel[:, tap_index, :], preferred_ele...]
    pallas_call x0 -> x4, Pallas kernels: none -> 24.1 us  [the longest x2 15.9 us: call(): pl.pallas_call(kernel, out_shape=outs, in_specs=[smem] + [WHOLE] * len(ar...]
    ppermute x6 -> x10, waiting for transfers between devices: 0.43 us -> 13.4 us  [the longest x8 8.76 us: halve(): got = lax.ppermute(send, 'tile', pairs)]
    unnamed x31 -> x12, local copies, waits for them, and re-layouts: 6.14 us -> 2.41 us
    mul x2 -> x0, other arithmetic: 3.36 us -> none  [kernel_term(): return jnp.stack(taps, axis=1) * scale]
    slice x3 -> x6, local copies, waits for them, and re-layouts: 2.71 us -> 0.14 us  [halve(): keep, send = (total[:half], total[half:].astype(BF16))]
    ppermute x6 -> x10, starting transfers between devices: 17.4 us -> 18.7 us  [the longest x8 14.9 us: halve(): got = lax.ppermute(send, 'tile', pairs)]
  transfers between devices with their start and end apart: 8 -> 10, of which waited for: 3 -> 5; matrix products, arithmetic and copies ran while one was open for 31% -> 2% of each run, Pallas kernels for 0% -> 25%
where the time goes in v1:
time: 61.8 us; the launch traced here: 61.5 us
  Pallas kernels  24.1 us (39%)
  starting transfers between devices  18.7 us (30%)
  waiting for transfers between devices  13.4 us (22%)
  local copies, waits for them, and re-layouts  2.56 us (4%)
  other arithmetic  1.99 us (3%)
  between operations  0.79 us (1%)
    pallas_call x2, Pallas kernels, call(): pl.pallas_call(kernel, out_shape=outs, in_specs=[smem] + [WHOLE] * len(ar...  15.9 us
    ppermute x8, starting transfers between devices, halve(): got = lax.ppermute(send, 'tile', pairs)  14.9 us
    ppermute x8, waiting for transfers between devices, halve(): got = lax.ppermute(send, 'tile', pairs)  8.76 us
    pallas_call x1, Pallas kernels, run(): pl.pallas_call(kernel, out_shape=outs, in_specs=[WHOLE] * len(args), out_...  7.28 us
    ppermute x1, waiting for transfers between devices, body(): down = lax.ppermute(first, 'tile', [(i + 1, i) for i in range(n - 1)])  4.54 us
    ppermute x1, starting transfers between devices, body(): up = lax.ppermute(last, 'tile', [(i, i + 1) for i in range(n - 1)])  2.54 us
    unnamed x12, local copies, waits for them, and re-layouts  2.41 us
    transpose x2, other arithmetic, halve(): return jnp.swapaxes(total[0], 0, 1)  1.36 us
  transfers between devices with their start and end apart: 10, of which 5 were waited for; matrix products, arithmetic and copies ran while one was open for 2% of the time, Pallas kernels for 25%

profile of v1, /device:TPU:0, one launch (start us, length us, event | category | flops | bytes accessed | tf_op | source)
XLA Modules:
  0.0 61.5 jit_solution(912151369706470532)
XLA Ops:
  0.6 1.2 %copy-done = bf16[1,12,160,256]{3,2,1,0:T(8,128)(2,1)S(1)} copy-done((bf16[1,12,160,256]{3,2,1,0:T(8,128)(2,1)S(1)}, bf16[1,12,160,256]{3,2,1,0:T(8,128)(2,1)}, u32[]{:S(2)}) %copy-start) | copy-done | bytes 983064
  1.8 1.2 %copy-done.2 = bf16[1,12,160,256]{3,2,1,0:T(8,128)(2,1)S(1)} copy-done((bf16[1,12,160,256]{3,2,1,0:T(8,128)(2,1)S(1)}, bf16[1,12,160,256]{3,2,1,0:T(8,128)(2,1)}, u32[]{:S(2)}) %copy-start.2) | copy-done | bytes 983064
  3.0 0.9 %shard_map.75 = (bf16[4,160,256]{2,1,0:T(8,128)(2,1)}, bf16[4,160,256]{2,1,0:T(8,128)(2,1)}) custom-call(bf16[12,160,256]{2,1,0:T(8,128)(2,1)S(1)} %bitcast.19, bf16[12,160,256]{2,1,0:T(8,128)(2,1)S(1)} %bitcast.24, bf16[12,160,256]{2,1,0:T(8,128)(2,1)S(1)} %bitcast.20, bf16[12,160,256]{2,1,0:T(8,128)(2,1)S(1)} %bitcast.25), custom_call_target="tpu_custom_call" | custom-call | tf_op jit(solution)/shard_map/pallas_call | solution.py:48
  3.9 2.5 %collective-permute-start = (bf16[4,160,256]{2,1,0:T(8,128)(2,1)}, bf16[4,160,256]{2,1,0:T(8,128)(2,1)S(1)}, u32[]{:S(2)}, u32[]{:S(2)}) collective-permute-start(bf16[4,160,256]{2,1,0:T(8,128)(2,1)} %get-tuple-element.15), channel_id=1, source_target_pairs={{0,1},{1,2},{2,3},{3,4},{4,5},{5,6},{6,7},{7,8},{8,9},{9,10},{10,1... | collective-permute-start | bytes 983048 | tf_op jit(solution)/shard_map/ppermute | solution.py:262
  6.5 1.3 %collective-permute-start.1 = (bf16[4,160,256]{2,1,0:T(8,128)(2,1)}, bf16[4,160,256]{2,1,0:T(8,128)(2,1)}, u32[]{:S(2)}, u32[]{:S(2)}) collective-permute-start(bf16[4,160,256]{2,1,0:T(8,128)(2,1)} %get-tuple-element.16), channel_id=1, source_target_pairs={{1,0},{2,1},{3,2},{4,3},{5,4},{6,5},{7,6},{8,7},{9,8},{10,9},{11,1... | collective-permute-start | bytes 983048 | tf_op jit(solution)/shard_map/ppermute | solution.py:263
  7.8 0.1 collective-permute-done.up
  7.9 4.5 %collective-permute-done.1.down = bf16[4,160,256]{2,1,0:T(8,128)(2,1)} collective-permute-done((bf16[4,160,256]{2,1,0:T(8,128)(2,1)}, bf16[4,160,256]{2,1,0:T(8,128)(2,1)}, u32[]{:S(2)}, u32[]{:S(2)}) %collective-permute-start.1) | collective-permute-done | bytes 327712 | tf_op jit(solution)/shard_map/ppermute | solution.py:263
  12.4 0.0 copy-start.5
  12.5 8.0 %shard_map.76 = (bf16[2240,256]{1,0:T(8,128)(2,1)S(1)}, f32[2240,256]{1,0:T(8,128)S(1)}, f32[8,9,16,256]{3,2,1,0:T(8,128)S(1)}, bf16[8,9,16,256]{3,2,1,0:T(8,128)(2,1)S(1)}) custom-call(s32[1]{0:T(128)} %bitcast.me_ref, bf16[12,160,256]{2,1,0:T(8,128)(2,1)S(1)} %bitcast.21, bf16[4,160,256]{2,1,0:T(8,128)(2,1)S(1)} %collective-permute-done.up, ...), custom_call_target="tpu_custom_call" | custom-call | flops 4529848320 | bytes 8388608 | tf_op jit(solution)/shard_map/pallas_call | solution.py:275
  20.5 5.4 %collective-permute-start.6 = (bf16[8,9,16,256]{3,2,1,0:T(8,128)(2,1)S(1)}, bf16[8,9,16,256]{3,2,1,0:T(8,128)(2,1)S(1)}, u32[]{:S(2)}, u32[]{:S(2)}) collective-permute-start(bf16[8,9,16,256]{3,2,1,0:T(8,128)(2,1)S(1)} %get-tuple-element.25), channel_id=1, source_target_pairs={{0,1},{1,0},{2,3},{3,2},{4,5},{5,4},{6,7},{7,6},{8,9},{9,8},{10,11... | collective-permute-start | bytes 1769480 | tf_op jit(solution)/shard_map/ppermute | solution.py:242
  25.9 7.9 %shard_map.77 = (bf16[2240,256]{1,0:T(8,128)(2,1)S(1)}, f32[8,9,16,256]{3,2,1,0:T(8,128)S(1)}, bf16[8,9,16,256]{3,2,1,0:T(8,128)(2,1)S(1)}) custom-call(s32[1]{0:T(128)} %bitcast.me_ref, bf16[12,160,256]{2,1,0:T(8,128)(2,1)S(1)} %bitcast.27, bf16[4,160,256]{2,1,0:T(8,128)(2,1)S(1)} %collective-permute-done.up, ...), custom_call_target="tpu_custom_call" | custom-call | flops 4529848320 | bytes 8388608 | tf_op jit(solution)/shard_map/pallas_call | solution.py:275
  33.8 0.1 collective-permute-start.2
  33.9 0.0 collective-permute-done.6
  33.9 0.2 convert_add_fusion
  34.1 2.5 %collective-permute-start.7 = (bf16[4,9,16,256]{3,2,1,0:T(8,128)(2,1)S(1)}, bf16[4,9,16,256]{3,2,1,0:T(8,128)(2,1)S(1)}, u32[]{:S(2)}, u32[]{:S(2)}) collective-permute-start(bf16[4,9,16,256]{3,2,1,0:T(8,128)(2,1)S(1)} %slice.82), channel_id=1, source_target_pairs={{0,2},{1,3},{2,0},{3,1},{4,6},{5,7},{6,4},{7,5},{8,10},{9,11},{10,... | collective-permute-start | bytes 884744 | tf_op jit(solution)/shard_map/ppermute | solution.py:242
  36.6 0.0 collective-permute-done.2
  36.6 0.2 convert_add_fusion.1
  36.9 1.6 %collective-permute-start.3 = (bf16[4,9,16,256]{3,2,1,0:T(8,128)(2,1)S(1)}, bf16[4,9,16,256]{3,2,1,0:T(8,128)(2,1)S(1)}, u32[]{:S(2)}, u32[]{:S(2)}) collective-permute-start(bf16[4,9,16,256]{3,2,1,0:T(8,128)(2,1)S(1)} %slice.83), channel_id=1, source_target_pairs={{0,4},{1,5},{2,6},{3,7},{4,0},{5,1},{6,2},{7,3},{8,12},{9,13},{10,... | collective-permute-start | bytes 884744 | tf_op jit(solution)/shard_map/ppermute | solution.py:242
  38.5 7.3 %shard_map.78 = (bf16[12,160,256]{2,1,0:T(8,128)(2,1)}, bf16[12,160,256]{2,1,0:T(8,128)(2,1)}) custom-call(bf16[2240,256]{1,0:T(8,128)(2,1)S(1)} %get-tuple-element.17.hid, bf16[2240,256]{1,0:T(8,128)(2,1)S(1)} %get-tuple-element.19.slope, bf16[12,160,256]{2,1,0:T(8,128)(2,1)S(1)} %bitcast.23, bf16[12,160,256]{2,1,0:T(8,128)(2,1)S(1)} %bitcast.28, ...), custom_call_target="tpu_custom_call" | custom-call | flops 4529848320 | bytes 8585216 | tf_op jit(solution)/shard_map/pallas_call | solution.py:18
  45.8 0.0 collective-permute-done.7
  45.8 0.1 slice_add_fusion
  45.9 0.5 collective-permute-start.8
  46.4 0.1 slice_add_fusion.1
  46.5 1.7 %collective-permute-start.4 = (bf16[2,9,16,256]{3,2,1,0:T(8,128)(2,1)S(1)}, bf16[2,9,16,256]{3,2,1,0:T(8,128)(2,1)S(1)}, u32[]{:S(2)}, u32[]{:S(2)}) collective-permute-start(bf16[2,9,16,256]{3,2,1,0:T(8,128)(2,1)S(1)} %slice.85), channel_id=1, source_target_pairs={{0,2},{1,3},{2,0},{3,1},{4,6},{5,7},{6,4},{7,5},{8,10},{9,11},{10,... | collective-permute-start | bytes 442376 | tf_op jit(solution)/shard_map/ppermute | solution.py:242
  48.3 3.4 %collective-permute-done.8 = bf16[2,9,16,256]{3,2,1,0:T(8,128)(2,1)S(1)} collective-permute-done((bf16[2,9,16,256]{3,2,1,0:T(8,128)(2,1)S(1)}, bf16[2,9,16,256]{3,2,1,0:T(8,128)(2,1)S(1)}, u32[]{:S(2)}, u32[]{:S(2)}) %collective-permute-start.8) | collective-permute-done | bytes 147488 | tf_op jit(solution)/shard_map/ppermute | solution.py:242
  51.7 2.5 %collective-permute-start.9 = (bf16[1,9,16,256]{3,2,1,0:T(8,128)(2,1)S(1)}, bf16[1,9,16,256]{3,2,1,0:T(8,128)(2,1)S(1)}, u32[]{:S(2)}, u32[]{:S(2)}) collective-permute-start(bf16[1,9,16,256]{3,2,1,0:T(8,128)(2,1)S(1)} %slice.86), channel_id=1, source_target_pairs={{0,8},{1,9},{2,10},{3,11},{4,12},{5,13},{6,14},{7,15},{8,0},{9,1},... | collective-permute-start | bytes 221192 | tf_op jit(solution)/shard_map/ppermute | solution.py:242
  54.2 0.0 collective-permute-done.4
  54.3 0.6 collective-permute-start.5
  54.8 5.2 %collective-permute-done.9 = bf16[1,9,16,256]{3,2,1,0:T(8,128)(2,1)S(1)} collective-permute-done((bf16[1,9,16,256]{3,2,1,0:T(8,128)(2,1)S(1)}, bf16[1,9,16,256]{3,2,1,0:T(8,128)(2,1)S(1)}, u32[]{:S(2)}, u32[]{:S(2)}) %collective-permute-start.9) | collective-permute-done | bytes 73760 | tf_op jit(solution)/shard_map/ppermute | solution.py:242
  60.0 0.7 %fusion = f32[16,9,256]{2,0,1:T(8,128)} fusion(f32[2,9,16,256]{3,2,1,0:T(8,128)S(1)} %slice_add_fusion.2, bf16[1,9,16,256]{3,2,1,0:T(8,128)(2,1)S(1)} %collective-permute-done.9), kind=kLoop, calls=%fused_computation.12 | loop fusion | flops 73728 | bytes 368640 | tf_op jit(solution)/shard_map/transpose | solution.py:248
  60.7 0.1 collective-permute-done.5
  60.9 0.7 %fusion.1 = f32[16,9,256]{2,0,1:T(8,128)} fusion(f32[2,9,16,256]{3,2,1,0:T(8,128)S(1)} %slice_add_fusion.3, bf16[1,9,16,256]{3,2,1,0:T(8,128)(2,1)S(1)} %collective-permute-done.5), kind=kLoop, calls=%fused_computation.15 | loop fusion | flops 73728 | bytes 368640 | tf_op jit(solution)/shard_map/transpose | solution.py:248
  (18 shorter events, 0.2 us)
Async XLA Ops:
  0.6 1.2 %copy-start = (bf16[1,12,160,256]{3,2,1,0:T(8,128)(2,1)S(1)}, bf16[1,12,160,256]{3,2,1,0:T(8,128)(2,1)}, u32[]{:S(2)}) copy-start(bf16[1,12,160,256]{3,2,1,0:T(8,128)(2,1)} %param.4) | copy-start | bytes 2949124
  1.8 1.2 %copy-start.2 = (bf16[1,12,160,256]{3,2,1,0:T(8,128)(2,1)S(1)}, bf16[1,12,160,256]{3,2,1,0:T(8,128)(2,1)}, u32[]{:S(2)}) copy-start(bf16[1,12,160,256]{3,2,1,0:T(8,128)(2,1)} %param.5) | copy-start | bytes 2949124
  3.0 9.4 %copy-start.1 = (bf16[1,12,160,256]{3,2,1,0:T(8,128)(2,1)S(1)}, bf16[1,12,160,256]{3,2,1,0:T(8,128)(2,1)}, u32[]{:S(2)}) copy-start(bf16[1,12,160,256]{3,2,1,0:T(8,128)(2,1)} %param.4) | copy-start | bytes 2949124
  3.0 9.4 %copy-start.3 = (bf16[1,12,160,256]{3,2,1,0:T(8,128)(2,1)S(1)}, bf16[1,12,160,256]{3,2,1,0:T(8,128)(2,1)}, u32[]{:S(2)}) copy-start(bf16[1,12,160,256]{3,2,1,0:T(8,128)(2,1)} %param.5) | copy-start | bytes 2949124
  3.0 9.4 %copy-start.4 = (bf16[256,9,256]{2,0,1:T(8,128)(2,1)S(1)}, bf16[256,9,256]{2,0,1:T(8,128)(2,1)}, u32[]{:S(2)}) copy-start(bf16[256,9,256]{2,0,1:T(8,128)(2,1)} %param.6) | copy-start | bytes 3538948
  3.9 4.0 %collective-permute-start = (bf16[4,160,256]{2,1,0:T(8,128)(2,1)}, bf16[4,160,256]{2,1,0:T(8,128)(2,1)S(1)}, u32[]{:S(2)}, u32[]{:S(2)}) collective-permute-start(bf16[4,160,256]{2,1,0:T(8,128)(2,1)} %get-tuple-element.15), channel_id=1, source_target_pairs={{0,1},{1,2},{2,3},{3,4},{4,5},{5,6},{6,7},{7,8},{8,9},{9,10},{10,1... | collective-permute-start | bytes 983048 | tf_op jit(solution)/shard_map/ppermute | solution.py:262
  6.5 6.0 %collective-permute-start.1 = (bf16[4,160,256]{2,1,0:T(8,128)(2,1)}, bf16[4,160,256]{2,1,0:T(8,128)(2,1)}, u32[]{:S(2)}, u32[]{:S(2)}) collective-permute-start(bf16[4,160,256]{2,1,0:T(8,128)(2,1)} %get-tuple-element.16), channel_id=1, source_target_pairs={{1,0},{2,1},{3,2},{4,3},{5,4},{6,5},{7,6},{8,7},{9,8},{10,9},{11,1... | collective-permute-start | bytes 983048 | tf_op jit(solution)/shard_map/ppermute | solution.py:263
  12.4 13.4 %copy-start.5 = (bf16[256,9,256]{2,0,1:T(8,128)(2,1)S(1)}, bf16[256,9,256]{2,0,1:T(8,128)(2,1)}, u32[]{:S(2)}) copy-start(bf16[256,9,256]{2,0,1:T(8,128)(2,1)} %param.7) | copy-start | bytes 3538948
  20.5 13.4 %collective-permute-start.6 = (bf16[8,9,16,256]{3,2,1,0:T(8,128)(2,1)S(1)}, bf16[8,9,16,256]{3,2,1,0:T(8,128)(2,1)S(1)}, u32[]{:S(2)}, u32[]{:S(2)}) collective-permute-start(bf16[8,9,16,256]{3,2,1,0:T(8,128)(2,1)S(1)} %get-tuple-element.25), channel_id=1, source_target_pairs={{0,1},{1,0},{2,3},{3,2},{4,5},{5,4},{6,7},{7,6},{8,9},{9,8},{10,11... | collective-permute-start | bytes 1769480 | tf_op jit(solution)/shard_map/ppermute | solution.py:242
  33.8 2.8 %collective-permute-start.2 = (bf16[8,9,16,256]{3,2,1,0:T(8,128)(2,1)S(1)}, bf16[8,9,16,256]{3,2,1,0:T(8,128)(2,1)S(1)}, u32[]{:S(2)}, u32[]{:S(2)}) collective-permute-start(bf16[8,9,16,256]{3,2,1,0:T(8,128)(2,1)S(1)} %get-tuple-element.23), channel_id=1, source_target_pairs={{0,1},{1,0},{2,3},{3,2},{4,5},{5,4},{6,7},{7,6},{8,9},{9,8},{10,11... | collective-permute-start | bytes 1769480 | tf_op jit(solution)/shard_map/ppermute | solution.py:242
  34.1 11.7 %collective-permute-start.7 = (bf16[4,9,16,256]{3,2,1,0:T(8,128)(2,1)S(1)}, bf16[4,9,16,256]{3,2,1,0:T(8,128)(2,1)S(1)}, u32[]{:S(2)}, u32[]{:S(2)}) collective-permute-start(bf16[4,9,16,256]{3,2,1,0:T(8,128)(2,1)S(1)} %slice.82), channel_id=1, source_target_pairs={{0,2},{1,3},{2,0},{3,1},{4,6},{5,7},{6,4},{7,5},{8,10},{9,11},{10,... | collective-permute-start | bytes 884744 | tf_op jit(solution)/shard_map/ppermute | solution.py:242
  36.9 9.6 %collective-permute-start.3 = (bf16[4,9,16,256]{3,2,1,0:T(8,128)(2,1)S(1)}, bf16[4,9,16,256]{3,2,1,0:T(8,128)(2,1)S(1)}, u32[]{:S(2)}, u32[]{:S(2)}) collective-permute-start(bf16[4,9,16,256]{3,2,1,0:T(8,128)(2,1)S(1)} %slice.83), channel_id=1, source_target_pairs={{0,4},{1,5},{2,6},{3,7},{4,0},{5,1},{6,2},{7,3},{8,12},{9,13},{10,... | collective-permute-start | bytes 884744 | tf_op jit(solution)/shard_map/ppermute | solution.py:242
  45.9 5.7 %collective-permute-start.8 = (bf16[2,9,16,256]{3,2,1,0:T(8,128)(2,1)S(1)}, bf16[2,9,16,256]{3,2,1,0:T(8,128)(2,1)S(1)}, u32[]{:S(2)}, u32[]{:S(2)}) collective-permute-start(bf16[2,9,16,256]{3,2,1,0:T(8,128)(2,1)S(1)} %slice.84), channel_id=1, source_target_pairs={{0,4},{1,5},{2,6},{3,7},{4,0},{5,1},{6,2},{7,3},{8,12},{9,13},{10,... | collective-permute-start | bytes 442376 | tf_op jit(solution)/shard_map/ppermute | solution.py:242
  46.5 7.7 %collective-permute-start.4 = (bf16[2,9,16,256]{3,2,1,0:T(8,128)(2,1)S(1)}, bf16[2,9,16,256]{3,2,1,0:T(8,128)(2,1)S(1)}, u32[]{:S(2)}, u32[]{:S(2)}) collective-permute-start(bf16[2,9,16,256]{3,2,1,0:T(8,128)(2,1)S(1)} %slice.85), channel_id=1, source_target_pairs={{0,2},{1,3},{2,0},{3,1},{4,6},{5,7},{6,4},{7,5},{8,10},{9,11},{10,... | collective-permute-start | bytes 442376 | tf_op jit(solution)/shard_map/ppermute | solution.py:242
  51.7 8.3 %collective-permute-start.9 = (bf16[1,9,16,256]{3,2,1,0:T(8,128)(2,1)S(1)}, bf16[1,9,16,256]{3,2,1,0:T(8,128)(2,1)S(1)}, u32[]{:S(2)}, u32[]{:S(2)}) collective-permute-start(bf16[1,9,16,256]{3,2,1,0:T(8,128)(2,1)S(1)} %slice.86), channel_id=1, source_target_pairs={{0,8},{1,9},{2,10},{3,11},{4,12},{5,13},{6,14},{7,15},{8,0},{9,1},... | collective-permute-start | bytes 221192 | tf_op jit(solution)/shard_map/ppermute | solution.py:242
  54.3 6.6 %collective-permute-start.5 = (bf16[1,9,16,256]{3,2,1,0:T(8,128)(2,1)S(1)}, bf16[1,9,16,256]{3,2,1,0:T(8,128)(2,1)S(1)}, u32[]{:S(2)}, u32[]{:S(2)}) collective-permute-start(bf16[1,9,16,256]{3,2,1,0:T(8,128)(2,1)S(1)} %slice.87), channel_id=1, source_target_pairs={{0,8},{1,9},{2,10},{3,11},{4,12},{5,13},{6,14},{7,15},{8,0},{9,1},... | collective-permute-start | bytes 221192 | tf_op jit(solution)/shard_map/ppermute | solution.py:242

commit v2 on v1

v2 whole, which is shorter than its diff:
```python
import functools

import jax
import jax.numpy as jnp
from jax import lax
from jax.experimental import pallas as pl
from jax.experimental.pallas import tpu as pltpu
from jax.sharding import PartitionSpec as P


F32 = jnp.float32
BF16 = jnp.bfloat16
WHOLE = pl.BlockSpec(memory_space=pltpu.VMEM)
LIMIT = 20 << 20


def struct(shape, dtype):
    return jax.ShapeDtypeStruct(shape, dtype)


def pack_kernel(f, c, first, last, second, before_last, sems):
    rows = f.shape[0]
    copies = []
    for out, row in ((first, 0), (last, rows - 1), (second, 1), (before_last, rows - 2)):
        for k, field in enumerate((f, c)):
            copies.append(pltpu.make_async_copy(field.at[row], out.at[k], sems.at[len(copies)]))
    for copy in copies:
        copy.start()
    for copy in copies:
        copy.wait()


def pack(features, cotangent):
    out = struct((2,) + features.shape[1:], BF16)
    hbm = pl.BlockSpec(memory_space=pltpu.HBM)
    return pl.pallas_call(
        pack_kernel,
        out_shape=(out,) * 4,
        in_specs=[hbm, hbm],
        out_specs=(WHOLE,) * 4,
        scratch_shapes=[pltpu.SemaphoreType.DMA((8,))],
        compiler_params=pltpu.CompilerParams(vmem_limit_bytes=8 << 20),
    )(
        pltpu.with_memory_space_constraint(features, pltpu.HBM),
        pltpu.with_memory_space_constraint(cotangent, pltpu.HBM),
    )


def put_windows(dst, row, value, sign):
    cols, chans = value.shape
    wide = value.astype(F32)
    index = lax.broadcasted_iota(jnp.int32, (cols, chans), 0)
    before = jnp.where(index == 0, 0.0, pltpu.roll(wide, 1, 0)).astype(BF16)
    after = jnp.where(index == cols - 1, 0.0, pltpu.roll(wide, cols - 1, 0)).astype(BF16)
    here = pl.ds(pl.multiple_of(row * cols, cols), cols)
    low, high = (before, after) if sign > 0 else (after, before)
    dst[here, 0:chans] = low
    dst[here, chans : 2 * chans] = value
    dst[here, 2 * chans : 3 * chans] = high


def fill(dst, base, count, source, first, sign):
    def step(k, carry):
        put_windows(dst, base + k, source[first + k], sign)
        return carry

    lax.fori_loop(0, count, step, 0)


def conv_rows(win, weight, start, size, cols):
    left = jnp.concatenate(
        [win[pl.ds(pl.multiple_of(start + a * cols, cols), size), :] for a in range(3)], axis=1
    )
    return jnp.dot(left, weight[...], preferred_element_type=F32)


def conv_t_rows(win, weight, start, size, cols, chans):
    total = None
    for a in range(3):
        left = win[pl.ds(pl.multiple_of(start + (2 - a) * cols, cols), size), :]
        for b in range(3):
            tap = (a * 3 + b) * chans
            part = lax.dot_general(
                left[:, b * chans : (b + 1) * chans],
                weight[tap : tap + chans, :],
                (((1,), (1,)), ((), ())),
                preferred_element_type=F32,
            )
            total = part if total is None else total + part
    return total


def bit_order(order):
    bits = [b for b in order[1:]]
    return bits


def slot_static(j, bits):
    s = 0
    for b in bits:
        s = s * 2 + ((j >> b) & 1)
    return s


def slot_dynamic(me, bits):
    s = jnp.int32(0)
    for b in bits:
        s = s * 2 + ((me >> b) & 1)
    return s


def store_terms(tap, value, keep, send, me, n, order, scale):
    rows = value.shape[0] // n
    value = value * scale
    bits = bit_order(order)
    mine = slot_dynamic(me, bits)
    flip = ((me >> order[0]) & 1) == 1
    for j in range(n):
        if (j >> order[0]) & 1:
            continue
        other = j ^ (1 << order[0])
        low = value[j * rows : (j + 1) * rows]
        high = value[other * rows : (other + 1) * rows]
        slot = slot_static(j, bits) ^ mine
        keep[slot, tap] = jnp.where(flip, high, low)
        send[slot, tap] = jnp.where(flip, low, high).astype(BF16)


def kernel_terms(left, win, keep, send, me, n, order, scale, cols, size):
    chans = left.shape[1]
    for a in range(3):
        right = win[(2 - a) * cols : (2 - a) * cols + size, :]
        out = lax.dot_general(left, right, (((0,), (0,)), ((), ())), preferred_element_type=F32)
        for b in range(3):
            store_terms(
                a * 3 + b, out[:, b * chans : (b + 1) * chans], keep, send, me, n, order, scale
            )


def activation(pre, hid, fac, here):
    sigma = jax.nn.sigmoid(pre)
    hid[here, :] = (pre * sigma).astype(BF16)
    fac[here, :] = sigma * (1.0 + pre * (1.0 - sigma))


def inner_kernel(f, c, w, xs, cs, hid, fac):
    rows, cols, _ = f.shape
    fill(xs, 1, rows, f, 0, 1)
    half = (rows - 2) // 2
    size = half * cols

    def step(k, carry):
        start = (1 + k * half) * cols
        pre = conv_rows(xs, w, start, size, cols)
        activation(pre, hid, fac, pl.ds(pl.multiple_of(start, cols), size))
        return carry

    lax.fori_loop(0, 2, step, 0)
    fill(cs, 1, rows, c, 0, -1)


def edge_kernel(n, order, scale, me_ref, up, down, w, xs_in, cs_in, hid_in, fac_in,
                xs, cs, hid, fac, keep, send):
    cols, _ = up.shape[1:]
    rows = xs.shape[0] // cols - 2
    put_windows(xs, 0, up[0], 1)
    put_windows(xs, rows + 1, down[0], 1)
    put_windows(cs, 0, up[1], -1)
    put_windows(cs, rows + 1, down[1], -1)
    left = jnp.concatenate(
        [
            jnp.concatenate(
                [xs[a * cols : (a + 1) * cols, :], xs[(rows - 1 + a) * cols : (rows + a) * cols, :]],
                axis=0,
            )
            for a in range(3)
        ],
        axis=1,
    )
    pre = jnp.dot(left, w[...], preferred_element_type=F32)
    activation(pre[:cols], hid, fac, pl.ds(0, cols))
    activation(pre[cols:], hid, fac, pl.ds((rows - 1) * cols, cols))
    kernel_terms(hid[...], cs, keep, send, me_ref[0], n, order, scale, cols, rows * cols)


def slope_kernel(cs, fac, w, slope):
    size_all, chans = slope.shape
    cols = (cs.shape[0] - size_all) // 2
    rows = size_all // cols
    half = rows // 2
    size = half * cols

    def step(k, carry):
        start = k * size
        grad = conv_t_rows(cs, w, start, size, cols, chans)
        here = pl.ds(pl.multiple_of(start, cols), size)
        slope[here, :] = (grad * fac[here, :]).astype(BF16)
        return carry

    lax.fori_loop(0, 2, step, 0)


def terms_kernel(n, order, scale, me_ref, xs, slope, keep, send):
    size_all, chans = slope.shape
    cols = (xs.shape[0] - size_all) // 2
    for a in range(3):
        left = xs[a * cols : a * cols + size_all, :]
        out = lax.dot_general(left, slope[...], (((0,), (0,)), ((), ())), preferred_element_type=F32)
        for b in range(3):
            store_terms(
                a * 3 + b, out[b * chans : (b + 1) * chans], keep, send, me_ref[0], n, order, scale
            )


def row_of(ref, k, cols):
    return ref[k * cols : (k + 1) * cols, :]


def edges_kernel(n, me_ref, xs, cs, up, down, w_one, w_two, hid_edge, slope_edge, xe, ce):
    cols, chans = up.shape[1:]
    rows = xs.shape[0] // cols - 2
    put_windows(xe, 0, up[0], 1)
    put_windows(xe, 1, down[0], 1)
    put_windows(ce, 0, up[1], -1)
    put_windows(ce, 1, down[1], -1)

    def pair(one, j, two, k):
        return jnp.concatenate([row_of(one, j, cols), row_of(two, k, cols)], axis=0)

    left = jnp.concatenate(
        [pair(xe, 0, xs, rows), pair(xs, 0, xs, rows + 1), pair(xs, 1, xe, 1)], axis=1
    )
    pre = jnp.dot(left, w_one[...], preferred_element_type=F32)
    total = None
    for a, left in enumerate((pair(cs, 1, ce, 1), pair(cs, 0, cs, rows + 1), pair(ce, 0, cs, rows))):
        for b in range(3):
            tap = (a * 3 + b) * chans
            part = lax.dot_general(
                left[:, b * chans : (b + 1) * chans],
                w_two[tap : tap + chans, :],
                (((1,), (1,)), ((), ())),
                preferred_element_type=F32,
            )
            total = part if total is None else total + part
    sigma = jax.nn.sigmoid(pre)
    hidden = pre * sigma
    slope = total * sigma * (1.0 + pre * (1.0 - sigma))
    for side, outside in ((0, me_ref[0] == 0), (1, me_ref[0] == n - 1)):
        here = slice(side * cols, (side + 1) * cols)
        hid_edge[here, :] = jnp.where(outside, 0.0, hidden[here]).astype(BF16)
        slope_edge[here, :] = jnp.where(outside, 0.0, slope[here]).astype(BF16)


def widen(dst, edge, own, rows, cols, sign):
    put_windows(dst, 0, row_of(edge, 0, cols), sign)
    put_windows(dst, rows + 1, row_of(edge, 1, cols), sign)

    def step(k, carry):
        put_windows(dst, k + 1, own[pl.ds(pl.multiple_of(k * cols, cols), cols), :], sign)
        return carry

    lax.fori_loop(0, rows, step, 0)


def block_kernel(hid_edge, hid, w_two, f, block_out, hs):
    rows, cols, chans = f.shape
    widen(hs, hid_edge, hid, rows, cols, 1)
    half = rows // 2
    size = half * cols

    def step(k, carry):
        here = pl.ds(k * half, half)
        out = conv_rows(hs, w_two, k * size, size, cols)
        block_out[here] = (f[here].astype(F32) + out.reshape(half, cols, chans)).astype(BF16)
        return carry

    lax.fori_loop(0, 2, step, 0)


def input_kernel(slope_edge, slope, w_one, c, input_grad, ss):
    rows, cols, chans = c.shape
    widen(ss, slope_edge, slope, rows, cols, -1)
    half = rows // 2
    size = half * cols

    def step(k, carry):
        here = pl.ds(k * half, half)
        out = conv_t_rows(ss, w_one, k * size, size, cols, chans)
        input_grad[here] = (c[here].astype(F32) + out.reshape(half, cols, chans)).astype(BF16)
        return carry

    lax.fori_loop(0, 2, step, 0)


def halve(keep, send, order, n):
    for bit in order:
        pairs = [(i, i ^ (1 << bit)) for i in range(n)]
        got = lax.ppermute(send, "tile", pairs)
        total = keep + got.astype(F32)
        half = total.shape[0] // 2
        if half:
            keep, send = total[:half], total[half:].astype(BF16)
        else:
            return jnp.swapaxes(total[0], 0, 1)


def layer(features, cotangent, weight_one, weight_two):
    _, rows, cols, chans = features.shape
    n = lax.axis_size("tile")
    scale = float(rows * n * cols) ** (-0.5)
    me = lax.axis_index("tile").astype(jnp.int32).reshape(1)
    f, c = features[0], cotangent[0]
    taps = weight_one.shape[1]
    w_one = jnp.swapaxes(weight_one, 0, 1).reshape(taps * chans, chans)
    w_two = jnp.swapaxes(weight_two, 0, 1).reshape(taps * chans, chans)

    bits = n.bit_length() - 1
    order_two = list(range(bits))
    order_one = [0, 2, 1] + list(range(3, bits)) if bits > 2 else order_two
    size, ext, wide = rows * cols, (rows + 2) * cols, 3 * chans
    flops = 2 * 9 * size * chans * chans
    smem = pl.BlockSpec(memory_space=pltpu.SMEM)

    def call(kernel, args, outs, scratch=(), work=flops, place=False, aliases={}):
        return pl.pallas_call(
            kernel,
            out_shape=outs,
            in_specs=([smem] if place else []) + [WHOLE] * len(args),
            out_specs=tuple(WHOLE for _ in outs),
            scratch_shapes=list(scratch),
            input_output_aliases=aliases,
            compiler_params=pltpu.CompilerParams(vmem_limit_bytes=LIMIT),
            cost_estimate=pl.CostEstimate(flops=work, bytes_accessed=4 << 20, transcendentals=0),
        )(*(((me,) if place else ()) + tuple(args)))

    upward = [(i, i + 1) for i in range(n - 1)]
    downward = [(i + 1, i) for i in range(n - 1)]
    first, last, second, before_last = pack(f, c)
    up = lax.ppermute(last, "tile", upward)
    down = lax.ppermute(first, "tile", downward)

    windows = struct((ext, wide), BF16)
    field, field_wide = struct((size, chans), BF16), struct((size, chans), F32)
    kept = struct((n // 2, taps, chans // n, chans), F32)
    sent = struct((n // 2, taps, chans // n, chans), BF16)
    xs, cs, hid, fac = call(inner_kernel, (f, c, w_one), (windows, windows, field, field_wide))
    xs, cs, hid, fac, keep_two, send_two = call(
        functools.partial(edge_kernel, n, order_two, scale),
        (up, down, w_one, xs, cs, hid, fac),
        (windows, windows, field, field_wide, kept, sent),
        place=True,
        aliases={4: 0, 5: 1, 6: 2, 7: 3},
    )
    up_two = lax.ppermute(before_last, "tile", upward)
    down_two = lax.ppermute(second, "tile", downward)
    (slope,) = call(slope_kernel, (cs, fac, w_two), (field,))
    keep_one, send_one = call(
        functools.partial(terms_kernel, n, order_one, scale), (xs, slope), (kept, sent), place=True
    )
    edge_pair = struct((2 * cols, chans), BF16)
    edge_rows = pltpu.VMEM((2 * cols, wide), BF16)
    all_rows = pltpu.VMEM((ext, wide), BF16)
    hid_edge, slope_edge = call(
        functools.partial(edges_kernel, n),
        (xs, cs, up_two, down_two, w_one, w_two),
        (edge_pair, edge_pair),
        [edge_rows, edge_rows],
        place=True,
    )
    (block_out,) = call(
        block_kernel, (hid_edge, hid, w_two, f), (struct(f.shape, BF16),), [all_rows]
    )
    (input_grad,) = call(
        input_kernel, (slope_edge, slope, w_one, c), (struct(c.shape, BF16),), [all_rows]
    )
    grad_two = halve(keep_two, send_two, order_two, n)
    grad_one = halve(keep_one, send_one, order_one, n)
    return (block_out[None], input_grad[None], grad_one, grad_two)


def solution(mesh):
    in_specs = (P("groups", "tile", None, None), P("groups", "tile", None, None), P(), P())
    out_specs = (
        P("groups", "tile", None, None),
        P("groups", "tile", None, None),
        P("tile", "groups", None),
        P("tile", "groups", None),
    )
    return jax.shard_map(layer, mesh=mesh, in_specs=in_specs, out_specs=out_specs, check_vma=False)
```

time: 61.8 us -> 64.9 us (1.050)
  starting transfers between devices: 18.7 us -> 22.5 us
  Pallas kernels: 24.1 us -> 23 us
  local copies, waits for them, and re-layouts: 2.56 us -> 3.43 us
    ppermute x2 -> x4, waiting for transfers between devices: 4.67 us -> 0.79 us  [the longest x1 0.78 us: layer(): down_two = lax.ppermute(second, 'tile', downward)]
    ppermute x8, waiting for transfers between devices: 8.76 us -> 12.1 us  [halve(): got = lax.ppermute(send, 'tile', pairs)]
    ppermute x2 -> x4, starting transfers between devices: 3.83 us -> 6.92 us  [the longest x1 2.41 us: layer(): up = lax.ppermute(last, 'tile', upward)]
    pallas_call x4 -> x8, Pallas kernels: 24.1 us -> 23 us  [the longest x7 21.7 us: call(): pl.pallas_call(kernel, out_shape=outs, in_specs=([smem] if place else [])...]
    unnamed x12, local copies, waits for them, and re-layouts: 2.41 us -> 3.29 us
    ppermute x8, starting transfers between devices: 14.9 us -> 15.6 us  [halve(): got = lax.ppermute(send, 'tile', pairs)]
  transfers between devices with their start and end apart: 10 -> 12, of which waited for: 5 -> 7; matrix products, arithmetic and copies ran while one was open for 2% -> 2% of each run, Pallas kernels for 25% -> 19%
where the time goes in v2:
time: 64.9 us; the launch traced here: 64.6 us
  Pallas kernels  23 us (35%)
  starting transfers between devices  22.5 us (35%)
  waiting for transfers between devices  12.8 us (20%)
  local copies, waits for them, and re-layouts  3.43 us (5%)
  other arithmetic  1.97 us (3%)
  between operations  0.9 us (1%)
    pallas_call x7, Pallas kernels, call(): pl.pallas_call(kernel, out_shape=outs, in_specs=([smem] if place else [])...  21.7 us
    ppermute x8, starting transfers between devices, halve(): got = lax.ppermute(send, 'tile', pairs)  15.6 us
    ppermute x8, waiting for transfers between devices, halve(): got = lax.ppermute(send, 'tile', pairs)  12.1 us
    unnamed x12, local copies, waits for them, and re-layouts  3.29 us
    ppermute x1, starting transfers between devices, layer(): up = lax.ppermute(last, 'tile', upward)  2.41 us
    ppermute x1, starting transfers between devices, layer(): up_two = lax.ppermute(before_last, 'tile', upward)  1.93 us
    transpose x2, other arithmetic, halve(): return jnp.swapaxes(total[0], 0, 1)  1.36 us
    pallas_call x1, Pallas kernels, pack(): pl.pallas_call(pack_kernel, out_shape=(out,) * 4, in_specs=[hbm, hbm], ou...  1.33 us
  transfers between devices with their start and end apart: 12, of which 7 were waited for; matrix products, arithmetic and copies ran while one was open for 2% of the time, Pallas kernels for 19%

profile of v2, /device:TPU:0, one launch (start us, length us, event | category | flops | bytes accessed | tf_op | source)
XLA Modules:
  0.0 64.6 jit_solution(14817947410785103450)
XLA Ops:
  0.6 1.3 %shard_map.75 = (bf16[2,160,256]{2,1,0:T(8,128)(2,1)S(1)}, bf16[2,160,256]{2,1,0:T(8,128)(2,1)S(1)}, bf16[2,160,256]{2,1,0:T(8,128)(2,1)S(1)}, bf16[2,160,256]{2,1,0:T(8,128)(2,1)S(1)}) custom-call(bf16[12,160,256]{2,1,0:T(8,128)(2,1)} %bitcast.29, bf16[12,160,256]{2,1,0:T(8,128)(2,1)} %bitcast.26), custom_call_target="tpu_custom_call" | custom-call | tf_op jit(solution)/shard_map/pallas_call | solution.py:36
  2.0 2.4 %collective-permute-start = (bf16[2,160,256]{2,1,0:T(8,128)(2,1)S(1)}, bf16[2,160,256]{2,1,0:T(8,128)(2,1)S(1)}, u32[]{:S(2)}, u32[]{:S(2)}) collective-permute-start(bf16[2,160,256]{2,1,0:T(8,128)(2,1)S(1)} %get-tuple-element.22), channel_id=1, source_target_pairs={{0,1},{1,2},{2,3},{3,4},{4,5},{5,6},{6,7},{7,8},{8,9},{9,10},{10,1... | collective-permute-start | bytes 491528 | tf_op jit(solution)/shard_map/ppermute | solution.py:339
  4.4 1.3 %collective-permute-start.1 = (bf16[2,160,256]{2,1,0:T(8,128)(2,1)S(1)}, bf16[2,160,256]{2,1,0:T(8,128)(2,1)S(1)}, u32[]{:S(2)}, u32[]{:S(2)}) collective-permute-start(bf16[2,160,256]{2,1,0:T(8,128)(2,1)S(1)} %get-tuple-element.23), channel_id=1, source_target_pairs={{1,0},{2,1},{3,2},{4,3},{5,4},{6,5},{7,6},{8,7},{9,8},{10,9},{11,1... | collective-permute-start | bytes 491528 | tf_op jit(solution)/shard_map/ppermute | solution.py:340
  5.7 1.2 %copy-done.2 = bf16[1,12,160,256]{3,2,1,0:T(8,128)(2,1)S(1)} copy-done((bf16[1,12,160,256]{3,2,1,0:T(8,128)(2,1)S(1)}, bf16[1,12,160,256]{3,2,1,0:T(8,128)(2,1)}, u32[]{:S(2)}) %copy-start.2) | copy-done | bytes 983064
  6.9 1.2 %copy-done.4 = bf16[1,12,160,256]{3,2,1,0:T(8,128)(2,1)S(1)} copy-done((bf16[1,12,160,256]{3,2,1,0:T(8,128)(2,1)S(1)}, bf16[1,12,160,256]{3,2,1,0:T(8,128)(2,1)}, u32[]{:S(2)}) %copy-start.4) | copy-done | bytes 983064
  8.1 3.3 %shard_map.76 = (bf16[2240,768]{1,0:T(8,128)(2,1)S(1)}, bf16[2240,768]{1,0:T(8,128)(2,1)S(1)}, bf16[1920,256]{1,0:T(8,128)(2,1)S(1)}, f32[1920,256]{1,0:T(8,128)S(1)}) custom-call(bf16[12,160,256]{2,1,0:T(8,128)(2,1)S(1)} %bitcast.30, bf16[12,160,256]{2,1,0:T(8,128)(2,1)S(1)} %bitcast.27, bf16[2304,256]{1,0:T(8,128)(2,1)S(1)} %bitcast.19), custom_call_target="tpu_custom_call" | custom-call | flops 2264924160 | bytes 4194304 | tf_op jit(solution)/shard_map/pallas_call | solution.py:325
  11.4 3.8 %shard_map.77 = (bf16[2240,768]{1,0:T(8,128)(2,1)S(1)}, bf16[2240,768]{1,0:T(8,128)(2,1)S(1)}, bf16[1920,256]{1,0:T(8,128)(2,1)S(1)}, f32[1920,256]{1,0:T(8,128)...) custom-call(s32[1]{0:T(128)} %bitcast.me_ref, ...), custom_call_target="tpu_custom_call", output_to_operand_aliasing={{0}: (4, {}), {1}: (5, {}), {2}: (6, {}), {3}: (7, {})} | custom-call | flops 2264924160 | bytes 4194304 | tf_op jit(solution)/shard_map/pallas_call | solution.py:325
  15.2 2.7 %shard_map.80.slope = bf16[1920,256]{1,0:T(8,128)(2,1)S(1)} custom-call(bf16[2240,768]{1,0:T(8,128)(2,1)S(1)} %get-tuple-element.29.cs, f32[1920,256]{1,0:T(8,128)S(1)} %get-tuple-element.35.fac, bf16[2304,256]{1,0:T(8,128)(2,1)S(1)} %bitcast.23), custom_call_target="tpu_custom_call" | custom-call | flops 2264924160 | bytes 4194304 | tf_op jit(solution)/shard_map/pallas_call | solution.py:325
  17.9 2.7 %shard_map.82 = (f32[8,9,16,256]{3,2,1,0:T(8,128)S(1)}, bf16[8,9,16,256]{3,2,1,0:T(8,128)(2,1)S(1)}) custom-call(s32[1]{0:T(128)} %bitcast.me_ref, bf16[2240,768]{1,0:T(8,128)(2,1)S(1)} %get-tuple-element.28.xs, bf16[1920,256]{1,0:T(8,128)(2,1)S(1)} %shard_map.80.slope), custom_call_target="tpu_custom_call" | custom-call | flops 2264924160 | bytes 4194304 | tf_op jit(solution)/shard_map/pallas_call | solution.py:325
  20.6 3.3 %collective-permute-start.4 = (bf16[8,9,16,256]{3,2,1,0:T(8,128)(2,1)S(1)}, bf16[8,9,16,256]{3,2,1,0:T(8,128)(2,1)S(1)}, u32[]{:S(2)}, u32[]{:S(2)}) collective-permute-start(bf16[8,9,16,256]{3,2,1,0:T(8,128)(2,1)S(1)} %get-tuple-element.37), channel_id=1, source_target_pairs={{0,1},{1,0},{2,3},{3,2},{4,5},{5,4},{6,7},{7,6},{8,9},{9,8},{10,11... | collective-permute-start | bytes 1769480 | tf_op jit(solution)/shard_map/ppermute | solution.py:298
  23.9 1.9 %collective-permute-start.2 = (bf16[2,160,256]{2,1,0:T(8,128)(2,1)S(1)}, bf16[2,160,256]{2,1,0:T(8,128)(2,1)S(1)}, u32[]{:S(2)}, u32[]{:S(2)}) collective-permute-start(bf16[2,160,256]{2,1,0:T(8,128)(2,1)S(1)} %get-tuple-element.30), channel_id=1, source_target_pairs={{0,1},{1,2},{2,3},{3,4},{4,5},{5,6},{6,7},{7,8},{8,9},{9,10},{10,1... | collective-permute-start | bytes 491528 | tf_op jit(solution)/shard_map/ppermute | solution.py:354
  25.8 1.3 %collective-permute-start.3 = (bf16[2,160,256]{2,1,0:T(8,128)(2,1)S(1)}, bf16[2,160,256]{2,1,0:T(8,128)(2,1)S(1)}, u32[]{:S(2)}, u32[]{:S(2)}) collective-permute-start(bf16[2,160,256]{2,1,0:T(8,128)(2,1)S(1)} %get-tuple-element.31), channel_id=1, source_target_pairs={{1,0},{2,1},{3,2},{4,3},{5,4},{6,5},{7,6},{8,7},{9,8},{10,9},{11,1... | collective-permute-start | bytes 491528 | tf_op jit(solution)/shard_map/ppermute | solution.py:355
  27.1 2.4 %collective-permute-start.8 = (bf16[8,9,16,256]{3,2,1,0:T(8,128)(2,1)S(1)}, bf16[8,9,16,256]{3,2,1,0:T(8,128)(2,1)S(1)}, u32[]{:S(2)}, u32[]{:S(2)}) collective-permute-start(bf16[8,9,16,256]{3,2,1,0:T(8,128)(2,1)S(1)} %get-tuple-element.39), channel_id=1, source_target_pairs={{0,1},{1,0},{2,3},{3,2},{4,5},{5,4},{6,7},{7,6},{8,9},{9,8},{10,11... | collective-permute-start | bytes 1769480 | tf_op jit(solution)/shard_map/ppermute | solution.py:298
  29.6 0.8 %collective-permute-done.3.down = bf16[2,160,256]{2,1,0:T(8,128)(2,1)S(1)} collective-permute-done((bf16[2,160,256]{2,1,0:T(8,128)(2,1)S(1)}, bf16[2,160,256]{2,1,0:T(8,128)(2,1)S(1)}, u32[]{:S(2)}, u32[]{:S(2)}) %collective-permute-start.3) | collective-permute-done | bytes 163872 | tf_op jit(solution)/shard_map/ppermute | solution.py:355
  30.3 1.0 %shard_map.78 = (bf16[320,256]{1,0:T(8,128)(2,1)S(1)}, bf16[320,256]{1,0:T(8,128)(2,1)S(1)}) custom-call(s32[1]{0:T(128)} %bitcast.me_ref, bf16[2240,768]{1,0:T(8,128)(2,1)S(1)} %get-tuple-element.28.xs, bf16[2240,768]{1,0:T(8,128)(2,1)S(1)} %get-tuple-element.29.cs, bf16[2,160,256]{2,1,0:T(8,128)(2,1)S(1)} %collective-permute-done.2.up, ...), custom_call_target="tpu_custom_call" | custom-call | flops 2264924160 | bytes 4194304 | tf_op jit(solution)/shard_map/pallas_call | solution.py:325
  31.3 4.2 %shard_map.81 = bf16[12,160,256]{2,1,0:T(8,128)(2,1)} custom-call(bf16[320,256]{1,0:T(8,128)(2,1)S(1)} %get-tuple-element.34.slope_edge, bf16[1920,256]{1,0:T(8,128)(2,1)S(1)} %shard_map.80.slope, bf16[2304,256]{1,0:T(8,128)(2,1)S(1)} %bitcast.22, bf16[12,160,256]{2,1,0:T(8,128)(2,1)S(1)} %bitcast.28), custom_call_target="tpu_custom_call" | custom-call | flops 2264924160 | bytes 4194304 | tf_op jit(solution)/shard_map/pallas_call | solution.py:325
  35.5 0.2 convert_add_fusion.1
  35.8 5.5 %collective-permute-start.5 = (bf16[4,9,16,256]{3,2,1,0:T(8,128)(2,1)S(1)}, bf16[4,9,16,256]{3,2,1,0:T(8,128)(2,1)S(1)}, u32[]{:S(2)}, u32[]{:S(2)}) collective-permute-start(bf16[4,9,16,256]{3,2,1,0:T(8,128)(2,1)S(1)} %slice.83), channel_id=1, source_target_pairs={{0,4},{1,5},{2,6},{3,7},{4,0},{5,1},{6,2},{7,3},{8,12},{9,13},{10,... | collective-permute-start | bytes 884744 | tf_op jit(solution)/shard_map/ppermute | solution.py:298
  41.2 0.2 convert_add_fusion
  41.6 0.9 %copy-done.5 = bf16[1,12,160,256]{3,2,1,0:T(8,128)(2,1)S(1)} copy-done((bf16[1,12,160,256]{3,2,1,0:T(8,128)(2,1)S(1)}, bf16[1,12,160,256]{3,2,1,0:T(8,128)(2,1)}, u32[]{:S(2)}) %copy-start.5) | copy-done | bytes 983064
  42.4 4.1 %shard_map.79 = bf16[12,160,256]{2,1,0:T(8,128)(2,1)} custom-call(bf16[320,256]{1,0:T(8,128)(2,1)S(1)} %get-tuple-element.32.hid_edge, bf16[1920,256]{1,0:T(8,128)(2,1)S(1)} %get-tuple-element.33.hid, bf16[2304,256]{1,0:T(8,128)(2,1)S(1)} %bitcast.25, bf16[12,160,256]{2,1,0:T(8,128)(2,1)S(1)} %bitcast.31), custom_call_target="tpu_custom_call" | custom-call | flops 2264924160 | bytes 4194304 | tf_op jit(solution)/shard_map/pallas_call | solution.py:325
  46.6 2.0 %collective-permute-done.5 = bf16[4,9,16,256]{3,2,1,0:T(8,128)(2,1)S(1)} collective-permute-done((bf16[4,9,16,256]{3,2,1,0:T(8,128)(2,1)S(1)}, bf16[4,9,16,256]{3,2,1,0:T(8,128)(2,1)S(1)}, u32[]{:S(2)}, u32[]{:S(2)}) %collective-permute-start.5) | collective-permute-done | bytes 294944 | tf_op jit(solution)/shard_map/ppermute | solution.py:298
  48.6 0.1 slice_add_fusion.1
  48.8 2.3 %collective-permute-done.9 = bf16[4,9,16,256]{3,2,1,0:T(8,128)(2,1)S(1)} collective-permute-done((bf16[4,9,16,256]{3,2,1,0:T(8,128)(2,1)S(1)}, bf16[4,9,16,256]{3,2,1,0:T(8,128)(2,1)S(1)}, u32[]{:S(2)}, u32[]{:S(2)}) %collective-permute-start.9) | collective-permute-done | bytes 294944 | tf_op jit(solution)/shard_map/ppermute | solution.py:298
  51.3 3.3 %collective-permute-done.6 = bf16[2,9,16,256]{3,2,1,0:T(8,128)(2,1)S(1)} collective-permute-done((bf16[2,9,16,256]{3,2,1,0:T(8,128)(2,1)S(1)}, bf16[2,9,16,256]{3,2,1,0:T(8,128)(2,1)S(1)}, u32[]{:S(2)}, u32[]{:S(2)}) %collective-permute-start.6) | collective-permute-done | bytes 147488 | tf_op jit(solution)/shard_map/ppermute | solution.py:298
  54.7 2.0 %collective-permute-start.7 = (bf16[1,9,16,256]{3,2,1,0:T(8,128)(2,1)S(1)}, bf16[1,9,16,256]{3,2,1,0:T(8,128)(2,1)S(1)}, u32[]{:S(2)}, u32[]{:S(2)}) collective-permute-start(bf16[1,9,16,256]{3,2,1,0:T(8,128)(2,1)S(1)} %slice.87), channel_id=1, source_target_pairs={{0,8},{1,9},{2,10},{3,11},{4,12},{5,13},{6,14},{7,15},{8,0},{9,1},... | collective-permute-start | bytes 221192 | tf_op jit(solution)/shard_map/ppermute | solution.py:298
  56.6 0.6 collective-permute-done.10
  57.3 2.2 %collective-permute-start.11 = (bf16[1,9,16,256]{3,2,1,0:T(8,128)(2,1)S(1)}, bf16[1,9,16,256]{3,2,1,0:T(8,128)(2,1)S(1)}, u32[]{:S(2)}, u32[]{:S(2)}) collective-permute-start(bf16[1,9,16,256]{3,2,1,0:T(8,128)(2,1)S(1)} %slice.86), channel_id=1, source_target_pairs={{0,8},{1,9},{2,10},{3,11},{4,12},{5,13},{6,14},{7,15},{8,0},{9,1},... | collective-permute-start | bytes 221192 | tf_op jit(solution)/shard_map/ppermute | solution.py:298
  59.4 2.5 %collective-permute-done.7 = bf16[1,9,16,256]{3,2,1,0:T(8,128)(2,1)S(1)} collective-permute-done((bf16[1,9,16,256]{3,2,1,0:T(8,128)(2,1)S(1)}, bf16[1,9,16,256]{3,2,1,0:T(8,128)(2,1)S(1)}, u32[]{:S(2)}, u32[]{:S(2)}) %collective-permute-start.7) | collective-permute-done | bytes 73760 | tf_op jit(solution)/shard_map/ppermute | solution.py:298
  61.9 0.7 %fusion.1 = f32[16,9,256]{2,0,1:T(8,128)} fusion(f32[2,9,16,256]{3,2,1,0:T(8,128)S(1)} %slice_add_fusion.3, bf16[1,9,16,256]{3,2,1,0:T(8,128)(2,1)S(1)} %collective-permute-done.7), kind=kLoop, calls=%fused_computation.15 | loop fusion | flops 73728 | bytes 368640 | tf_op jit(solution)/shard_map/transpose | solution.py:304
  62.6 1.3 %collective-permute-done.11 = bf16[1,9,16,256]{3,2,1,0:T(8,128)(2,1)S(1)} collective-permute-done((bf16[1,9,16,256]{3,2,1,0:T(8,128)(2,1)S(1)}, bf16[1,9,16,256]{3,2,1,0:T(8,128)(2,1)S(1)}, u32[]{:S(2)}, u32[]{:S(2)}) %collective-permute-start.11) | collective-permute-done | bytes 73760 | tf_op jit(solution)/shard_map/ppermute | solution.py:298
  63.9 0.7 %fusion = f32[16,9,256]{2,0,1:T(8,128)} fusion(f32[2,9,16,256]{3,2,1,0:T(8,128)S(1)} %slice_add_fusion.2, bf16[1,9,16,256]{3,2,1,0:T(8,128)(2,1)S(1)} %collective-permute-done.11), kind=kLoop, calls=%fused_computation.12 | loop fusion | flops 73728 | bytes 368640 | tf_op jit(solution)/shard_map/transpose | solution.py:304
  (26 shorter events, 0.5 us)
Async XLA Ops:
  0.6 5.1 %copy-start = (bf16[256,9,256]{2,0,1:T(8,128)(2,1)S(1)}, bf16[256,9,256]{2,0,1:T(8,128)(2,1)}, u32[]{:S(2)}) copy-start(bf16[256,9,256]{2,0,1:T(8,128)(2,1)} %param.6) | copy-start | bytes 3538948
  2.0 9.4 %collective-permute-start = (bf16[2,160,256]{2,1,0:T(8,128)(2,1)S(1)}, bf16[2,160,256]{2,1,0:T(8,128)(2,1)S(1)}, u32[]{:S(2)}, u32[]{:S(2)}) collective-permute-start(bf16[2,160,256]{2,1,0:T(8,128)(2,1)S(1)} %get-tuple-element.22), channel_id=1, source_target_pairs={{0,1},{1,2},{2,3},{3,4},{4,5},{5,6},{6,7},{7,8},{8,9},{9,10},{10,1... | collective-permute-start | bytes 491528 | tf_op jit(solution)/shard_map/ppermute | solution.py:339
  4.4 7.0 %collective-permute-start.1 = (bf16[2,160,256]{2,1,0:T(8,128)(2,1)S(1)}, bf16[2,160,256]{2,1,0:T(8,128)(2,1)S(1)}, u32[]{:S(2)}, u32[]{:S(2)}) collective-permute-start(bf16[2,160,256]{2,1,0:T(8,128)(2,1)S(1)} %get-tuple-element.23), channel_id=1, source_target_pairs={{1,0},{2,1},{3,2},{4,3},{5,4},{6,5},{7,6},{8,7},{9,8},{10,9},{11,1... | collective-permute-start | bytes 491528 | tf_op jit(solution)/shard_map/ppermute | solution.py:340
  5.7 1.2 %copy-start.2 = (bf16[1,12,160,256]{3,2,1,0:T(8,128)(2,1)S(1)}, bf16[1,12,160,256]{3,2,1,0:T(8,128)(2,1)}, u32[]{:S(2)}) copy-start(bf16[1,12,160,256]{3,2,1,0:T(8,128)(2,1)} %param.5) | copy-start | bytes 2949124
  6.9 1.2 %copy-start.4 = (bf16[1,12,160,256]{3,2,1,0:T(8,128)(2,1)S(1)}, bf16[1,12,160,256]{3,2,1,0:T(8,128)(2,1)}, u32[]{:S(2)}) copy-start(bf16[1,12,160,256]{3,2,1,0:T(8,128)(2,1)} %param.4) | copy-start | bytes 2949124
  11.4 3.8 %copy-start.1 = (bf16[256,9,256]{2,0,1:T(8,128)(2,1)S(1)}, bf16[256,9,256]{2,0,1:T(8,128)(2,1)}, u32[]{:S(2)}) copy-start(bf16[256,9,256]{2,0,1:T(8,128)(2,1)} %param.7) | copy-start | bytes 3538948
  20.6 15.0 %collective-permute-start.4 = (bf16[8,9,16,256]{3,2,1,0:T(8,128)(2,1)S(1)}, bf16[8,9,16,256]{3,2,1,0:T(8,128)(2,1)S(1)}, u32[]{:S(2)}, u32[]{:S(2)}) collective-permute-start(bf16[8,9,16,256]{3,2,1,0:T(8,128)(2,1)S(1)} %get-tuple-element.37), channel_id=1, source_target_pairs={{0,1},{1,0},{2,3},{3,2},{4,5},{5,4},{6,7},{7,6},{8,9},{9,8},{10,11... | collective-permute-start | bytes 1769480 | tf_op jit(solution)/shard_map/ppermute | solution.py:298
  23.9 5.7 %collective-permute-start.2 = (bf16[2,160,256]{2,1,0:T(8,128)(2,1)S(1)}, bf16[2,160,256]{2,1,0:T(8,128)(2,1)S(1)}, u32[]{:S(2)}, u32[]{:S(2)}) collective-permute-start(bf16[2,160,256]{2,1,0:T(8,128)(2,1)S(1)} %get-tuple-element.30), channel_id=1, source_target_pairs={{0,1},{1,2},{2,3},{3,4},{4,5},{5,6},{6,7},{7,8},{8,9},{9,10},{10,1... | collective-permute-start | bytes 491528 | tf_op jit(solution)/shard_map/ppermute | solution.py:354
  25.8 4.5 %collective-permute-start.3 = (bf16[2,160,256]{2,1,0:T(8,128)(2,1)S(1)}, bf16[2,160,256]{2,1,0:T(8,128)(2,1)S(1)}, u32[]{:S(2)}, u32[]{:S(2)}) collective-permute-start(bf16[2,160,256]{2,1,0:T(8,128)(2,1)S(1)} %get-tuple-element.31), channel_id=1, source_target_pairs={{1,0},{2,1},{3,2},{4,3},{5,4},{6,5},{7,6},{8,7},{9,8},{10,9},{11,1... | collective-permute-start | bytes 491528 | tf_op jit(solution)/shard_map/ppermute | solution.py:355
  27.1 4.2 %copy-start.3 = (bf16[1,12,160,256]{3,2,1,0:T(8,128)(2,1)S(1)}, bf16[1,12,160,256]{3,2,1,0:T(8,128)(2,1)}, u32[]{:S(2)}) copy-start(bf16[1,12,160,256]{3,2,1,0:T(8,128)(2,1)} %param.5) | copy-start | bytes 2949124
  27.1 14.1 %collective-permute-start.8 = (bf16[8,9,16,256]{3,2,1,0:T(8,128)(2,1)S(1)}, bf16[8,9,16,256]{3,2,1,0:T(8,128)(2,1)S(1)}, u32[]{:S(2)}, u32[]{:S(2)}) collective-permute-start(bf16[8,9,16,256]{3,2,1,0:T(8,128)(2,1)S(1)} %get-tuple-element.39), channel_id=1, source_target_pairs={{0,1},{1,0},{2,3},{3,2},{4,5},{5,4},{6,7},{7,6},{8,9},{9,8},{10,11... | collective-permute-start | bytes 1769480 | tf_op jit(solution)/shard_map/ppermute | solution.py:298
  35.8 12.8 %collective-permute-start.5 = (bf16[4,9,16,256]{3,2,1,0:T(8,128)(2,1)S(1)}, bf16[4,9,16,256]{3,2,1,0:T(8,128)(2,1)S(1)}, u32[]{:S(2)}, u32[]{:S(2)}) collective-permute-start(bf16[4,9,16,256]{3,2,1,0:T(8,128)(2,1)S(1)} %slice.83), channel_id=1, source_target_pairs={{0,4},{1,5},{2,6},{3,7},{4,0},{5,1},{6,2},{7,3},{8,12},{9,13},{10,... | collective-permute-start | bytes 884744 | tf_op jit(solution)/shard_map/ppermute | solution.py:298
  41.2 1.2 %copy-start.5 = (bf16[1,12,160,256]{3,2,1,0:T(8,128)(2,1)S(1)}, bf16[1,12,160,256]{3,2,1,0:T(8,128)(2,1)}, u32[]{:S(2)}) copy-start(bf16[1,12,160,256]{3,2,1,0:T(8,128)(2,1)} %param.4) | copy-start | bytes 2949124
  41.5 9.6 %collective-permute-start.9 = (bf16[4,9,16,256]{3,2,1,0:T(8,128)(2,1)S(1)}, bf16[4,9,16,256]{3,2,1,0:T(8,128)(2,1)S(1)}, u32[]{:S(2)}, u32[]{:S(2)}) collective-permute-start(bf16[4,9,16,256]{3,2,1,0:T(8,128)(2,1)S(1)} %slice.82), channel_id=1, source_target_pairs={{0,2},{1,3},{2,0},{3,1},{4,6},{5,7},{6,4},{7,5},{8,10},{9,11},{10,... | collective-permute-start | bytes 884744 | tf_op jit(solution)/shard_map/ppermute | solution.py:298
  48.7 5.9 %collective-permute-start.6 = (bf16[2,9,16,256]{3,2,1,0:T(8,128)(2,1)S(1)}, bf16[2,9,16,256]{3,2,1,0:T(8,128)(2,1)S(1)}, u32[]{:S(2)}, u32[]{:S(2)}) collective-permute-start(bf16[2,9,16,256]{3,2,1,0:T(8,128)(2,1)S(1)} %slice.85), channel_id=1, source_target_pairs={{0,2},{1,3},{2,0},{3,1},{4,6},{5,7},{6,4},{7,5},{8,10},{9,11},{10,... | collective-permute-start | bytes 442376 | tf_op jit(solution)/shard_map/ppermute | solution.py:298
  51.2 6.0 %collective-permute-start.10 = (bf16[2,9,16,256]{3,2,1,0:T(8,128)(2,1)S(1)}, bf16[2,9,16,256]{3,2,1,0:T(8,128)(2,1)S(1)}, u32[]{:S(2)}, u32[]{:S(2)}) collective-permute-start(bf16[2,9,16,256]{3,2,1,0:T(8,128)(2,1)S(1)} %slice.84), channel_id=1, source_target_pairs={{0,4},{1,5},{2,6},{3,7},{4,0},{5,1},{6,2},{7,3},{8,12},{9,13},{10,... | collective-permute-start | bytes 442376 | tf_op jit(solution)/shard_map/ppermute | solution.py:298
  54.7 7.3 %collective-permute-start.7 = (bf16[1,9,16,256]{3,2,1,0:T(8,128)(2,1)S(1)}, bf16[1,9,16,256]{3,2,1,0:T(8,128)(2,1)S(1)}, u32[]{:S(2)}, u32[]{:S(2)}) collective-permute-start(bf16[1,9,16,256]{3,2,1,0:T(8,128)(2,1)S(1)} %slice.87), channel_id=1, source_target_pairs={{0,8},{1,9},{2,10},{3,11},{4,12},{5,13},{6,14},{7,15},{8,0},{9,1},... | collective-permute-start | bytes 221192 | tf_op jit(solution)/shard_map/ppermute | solution.py:298
  57.3 6.7 %collective-permute-start.11 = (bf16[1,9,16,256]{3,2,1,0:T(8,128)(2,1)S(1)}, bf16[1,9,16,256]{3,2,1,0:T(8,128)(2,1)S(1)}, u32[]{:S(2)}, u32[]{:S(2)}) collective-permute-start(bf16[1,9,16,256]{3,2,1,0:T(8,128)(2,1)S(1)} %slice.86), channel_id=1, source_target_pairs={{0,8},{1,9},{2,10},{3,11},{4,12},{5,13},{6,14},{7,15},{8,0},{9,1},... | collective-permute-start | bytes 221192 | tf_op jit(solution)/shard_map/ppermute | solution.py:298

commit v3 on v2

v3 whole, which is shorter than its diff:
```python
import functools

import jax
import jax.numpy as jnp
from jax import lax
from jax.experimental import pallas as pl
from jax.experimental.pallas import tpu as pltpu
from jax.sharding import PartitionSpec as P


F32 = jnp.float32
BF16 = jnp.bfloat16
WHOLE = pl.BlockSpec(memory_space=pltpu.VMEM)
LIMIT = 20 << 20


def struct(shape, dtype):
    return jax.ShapeDtypeStruct(shape, dtype)


def pack_kernel(me_ref, f, c, inside, across, sems):
    rows = f.shape[0]
    odd = (me_ref[0] & 1) == 1
    low, high = jnp.where(odd, 0, rows - 2), jnp.where(odd, rows - 2, 0)
    copies = []
    for out, row in ((across, high), (inside, low)):
        for k, field in enumerate((f, c)):
            copies.append(
                pltpu.make_async_copy(
                    field.at[pl.ds(row, 2)], out.at[pl.ds(2 * k, 2)], sems.at[len(copies)]
                )
            )
    for copy in copies:
        copy.start()
    for copy in copies:
        copy.wait()


def in_hbm(array):
    return pltpu.with_memory_space_constraint(array, pltpu.HBM)


def pack(me, features, cotangent):
    out = struct((4,) + features.shape[1:], BF16)
    hbm = pl.BlockSpec(memory_space=pltpu.HBM)
    return pl.pallas_call(
        pack_kernel,
        out_shape=(out,) * 2,
        in_specs=[pl.BlockSpec(memory_space=pltpu.SMEM), hbm, hbm],
        out_specs=(WHOLE,) * 2,
        scratch_shapes=[pltpu.SemaphoreType.DMA((4,))],
        compiler_params=pltpu.CompilerParams(vmem_limit_bytes=8 << 20),
    )(me, in_hbm(features), in_hbm(cotangent))


def put_windows(dst, row, value, sign):
    cols, chans = value.shape
    wide = value.astype(F32)
    index = lax.broadcasted_iota(jnp.int32, (cols, chans), 0)
    before = jnp.where(index == 0, 0.0, pltpu.roll(wide, 1, 0)).astype(BF16)
    after = jnp.where(index == cols - 1, 0.0, pltpu.roll(wide, cols - 1, 0)).astype(BF16)
    here = pl.ds(pl.multiple_of(row * cols, cols), cols)
    low, high = (before, after) if sign > 0 else (after, before)
    dst[here, 0:chans] = low
    dst[here, chans : 2 * chans] = value
    dst[here, 2 * chans : 3 * chans] = high


def fill(dst, base, count, source, first, sign):
    def step(k, carry):
        put_windows(dst, base + k, source[first + k], sign)
        return carry

    lax.fori_loop(0, count, step, 0)


def conv_rows(win, weight, start, size, cols):
    left = jnp.concatenate(
        [win[pl.ds(pl.multiple_of(start + a * cols, cols), size), :] for a in range(3)], axis=1
    )
    return jnp.dot(left, weight[...], preferred_element_type=F32)


def conv_t_rows(win, weight, start, size, cols, chans):
    total = None
    for a in range(3):
        left = win[pl.ds(pl.multiple_of(start + (2 - a) * cols, cols), size), :]
        for b in range(3):
            tap = (a * 3 + b) * chans
            part = lax.dot_general(
                left[:, b * chans : (b + 1) * chans],
                weight[tap : tap + chans, :],
                (((1,), (1,)), ((), ())),
                preferred_element_type=F32,
            )
            total = part if total is None else total + part
    return total


def bit_order(order):
    bits = [b for b in order[1:]]
    return bits


def slot_static(j, bits):
    s = 0
    for b in bits:
        s = s * 2 + ((j >> b) & 1)
    return s


def slot_dynamic(me, bits):
    s = jnp.int32(0)
    for b in bits:
        s = s * 2 + ((me >> b) & 1)
    return s


def store_terms(tap, value, keep, send, me, n, order, scale):
    rows = value.shape[0] // n
    value = value * scale
    bits = bit_order(order)
    mine = slot_dynamic(me, bits)
    flip = ((me >> order[0]) & 1) == 1
    for j in range(n):
        if (j >> order[0]) & 1:
            continue
        other = j ^ (1 << order[0])
        low = value[j * rows : (j + 1) * rows]
        high = value[other * rows : (other + 1) * rows]
        slot = slot_static(j, bits) ^ mine
        keep[slot, tap] = jnp.where(flip, high, low)
        send[slot, tap] = jnp.where(flip, low, high).astype(BF16)


def transposed_dot(left, right):
    return lax.dot_general(left, right, (((0,), (0,)), ((), ())), preferred_element_type=F32)


def rows_of(ref, first, count, cols):
    return ref[first * cols : (first + count) * cols, :]


def pair(ref, one, two, cols):
    return jnp.concatenate([rows_of(ref, one, 1, cols), rows_of(ref, two, 1, cols)], axis=0)


def pre_of_pair(xs, w, one, two, cols):
    left = [pair(xs, one + 1 + a, two + 1 + a, cols) for a in range(3)]
    return jnp.dot(jnp.concatenate(left, axis=1), w[...], preferred_element_type=F32)


def grad_of_pair(cs, w, one, two, cols):
    total = None
    for a in range(3):
        left = pair(cs, one + 3 - a, two + 3 - a, cols)
        chans = left.shape[1] // 3
        for b in range(3):
            tap = (a * 3 + b) * chans
            part = lax.dot_general(
                left[:, b * chans : (b + 1) * chans],
                w[tap : tap + chans, :],
                (((1,), (1,)), ((), ())),
                preferred_element_type=F32,
            )
            total = part if total is None else total + part
    return total


def derivative(pre, sigma):
    return sigma * (1.0 + pre * (1.0 - sigma))


def inner_kernel(f_hbm, c_hbm, w_hbm, w_one, xs, cs, hid, slope, acc, f, c, w_two, sems):
    rows, cols, chans = f.shape
    copy_f = pltpu.make_async_copy(f_hbm, f, sems.at[0])
    copy_c = pltpu.make_async_copy(c_hbm, c, sems.at[1])
    copy_w = pltpu.make_async_copy(w_hbm, w_two, sems.at[2])
    copy_f.start()
    copy_c.start()
    copy_w.start()
    copy_f.wait()
    fill(xs, 2, rows, f, 0, 1)
    copy_c.wait()
    fill(cs, 2, rows, c, 0, -1)
    copy_w.wait()
    half = (rows - 2) // 2
    size = half * cols

    def step(k, carry):
        start = (2 + k * half) * cols
        here = pl.ds(pl.multiple_of(start, cols), size)
        pre = conv_rows(xs, w_one, start, size, cols)
        sigma = jax.nn.sigmoid(pre)
        hid[here, :] = (pre * sigma).astype(BF16)
        grad = conv_t_rows(cs, w_two, start, size, cols, chans)
        slope[here, :] = (grad * derivative(pre, sigma)).astype(BF16)
        return carry

    lax.fori_loop(0, 2, step, 0)
    left = rows_of(hid, 2, rows - 2, cols)
    for a in range(3):
        acc[a] = transposed_dot(left, rows_of(cs, 4 - a, rows - 2, cols))


def edge_kernel(n, order, scale, me_ref, inside, across, w, xs_in, cs_in, hid_in, acc,
                xs, cs, hid, fac, keep, send):
    cols, chans = inside.shape[1:]
    rows = xs.shape[0] // cols - 4
    me = me_ref[0]
    odd = (me & 1) == 1
    for k in range(2):
        for dst, part, sign in ((xs, k, 1), (cs, 2 + k, -1)):
            one, two = inside[part], across[part]
            put_windows(dst, k, jnp.where(odd, one, two), sign)
            put_windows(dst, rows + 2 + k, jnp.where(odd, two, one), sign)
    pre = pre_of_pair(xs, w, 0, rows - 1, cols)
    sigma = jax.nn.sigmoid(pre)
    hidden = (pre * sigma).astype(BF16)
    hid[cols : 2 * cols, :] = hidden[:cols]
    hid[rows * cols : (rows + 1) * cols, :] = hidden[cols:]
    fac[...] = derivative(pre, sigma)
    left = pair(hid, 1, rows, cols)
    for a in range(3):
        out = acc[a] + transposed_dot(left, pair(cs, 3 - a, rows + 2 - a, cols))
        for b in range(3):
            store_terms(
                a * 3 + b, out[:, b * chans : (b + 1) * chans], keep, send, me, n, order, scale
            )


def terms_kernel(n, order, scale, me_ref, xs, cs, fac, w, slope_in, slope, keep, send):
    chans = slope.shape[1]
    cols = fac.shape[0] // 2
    rows = xs.shape[0] // cols - 4
    value = (grad_of_pair(cs, w, 0, rows - 1, cols) * fac[...]).astype(BF16)
    slope[cols : 2 * cols, :] = value[:cols]
    slope[rows * cols : (rows + 1) * cols, :] = value[cols:]
    right = rows_of(slope, 1, rows, cols)
    for a in range(3):
        out = transposed_dot(rows_of(xs, 1 + a, rows, cols), right)
        for b in range(3):
            store_terms(
                a * 3 + b, out[b * chans : (b + 1) * chans], keep, send, me_ref[0], n, order, scale
            )


def sides_kernel(n, cols, me_ref, xs, cs, w_one, w_two, hid_in, slope_in, hid, slope):
    rows = xs.shape[0] // cols - 4
    pre = pre_of_pair(xs, w_one, -1, rows, cols)
    grad = grad_of_pair(cs, w_two, -1, rows, cols)
    sigma = jax.nn.sigmoid(pre)
    hidden = pre * sigma
    value = grad * derivative(pre, sigma)
    for side, outside in ((0, me_ref[0] == 0), (1, me_ref[0] == n - 1)):
        here = slice(side * cols, (side + 1) * cols)
        there = slice(side * (rows + 1) * cols, (side * (rows + 1) + 1) * cols)
        hid[there, :] = jnp.where(outside, 0.0, hidden[here]).astype(BF16)
        slope[there, :] = jnp.where(outside, 0.0, value[here]).astype(BF16)


def widen(dst, source, count, cols, sign):
    def step(k, carry):
        put_windows(dst, k, source[pl.ds(pl.multiple_of(k * cols, cols), cols), :], sign)
        return carry

    lax.fori_loop(0, count, step, 0)


def block_kernel(hid, w_two, f, block_out, hs):
    rows, cols, chans = f.shape
    widen(hs, hid, rows + 2, cols, 1)
    half = rows // 2
    size = half * cols

    def step(k, carry):
        here = pl.ds(k * half, half)
        out = conv_rows(hs, w_two, k * size, size, cols)
        block_out[here] = (f[here].astype(F32) + out.reshape(half, cols, chans)).astype(BF16)
        return carry

    lax.fori_loop(0, 2, step, 0)


def input_kernel(slope, w_one, c, input_grad, ss):
    rows, cols, chans = c.shape
    widen(ss, slope, rows + 2, cols, -1)
    half = rows // 2
    size = half * cols

    def step(k, carry):
        here = pl.ds(k * half, half)
        out = conv_t_rows(ss, w_one, k * size, size, cols, chans)
        input_grad[here] = (c[here].astype(F32) + out.reshape(half, cols, chans)).astype(BF16)
        return carry

    lax.fori_loop(0, 2, step, 0)


def halve(keep, send, order, n):
    for bit in order:
        pairs = [(i, i ^ (1 << bit)) for i in range(n)]
        got = lax.ppermute(send, "tile", pairs)
        total = keep + got.astype(F32)
        half = total.shape[0] // 2
        if half:
            keep, send = total[:half], total[half:].astype(BF16)
        else:
            return jnp.swapaxes(total[0], 0, 1)


def layer(features, cotangent, weight_one, weight_two):
    _, rows, cols, chans = features.shape
    n = lax.axis_size("tile")
    scale = float(rows * n * cols) ** (-0.5)
    me = lax.axis_index("tile").astype(jnp.int32).reshape(1)
    f, c = features[0], cotangent[0]
    taps = weight_one.shape[1]
    w_one = jnp.swapaxes(weight_one, 0, 1).reshape(taps * chans, chans)
    w_two = jnp.swapaxes(weight_two, 0, 1).reshape(taps * chans, chans)

    bits = n.bit_length() - 1
    order_two = list(range(bits))
    order_one = [0, 2, 1] + list(range(3, bits)) if bits > 2 else order_two
    size, ext, wide = rows * cols, (rows + 2) * cols, 3 * chans
    flops = 2 * 9 * size * chans * chans
    smem = pl.BlockSpec(memory_space=pltpu.SMEM)

    hbm = pl.BlockSpec(memory_space=pltpu.HBM)

    def call(kernel, args, outs, scratch=(), work=flops, place=False, aliases={}, raw=0):
        specs = ([smem] if place else []) + [hbm] * raw + [WHOLE] * (len(args) - raw)
        return pl.pallas_call(
            kernel,
            out_shape=outs,
            in_specs=specs,
            out_specs=tuple(WHOLE for _ in outs),
            scratch_shapes=list(scratch),
            input_output_aliases=aliases,
            compiler_params=pltpu.CompilerParams(vmem_limit_bytes=LIMIT),
            cost_estimate=pl.CostEstimate(flops=work, bytes_accessed=4 << 20, transcendentals=0),
        )(*(((me,) if place else ()) + tuple(args)))

    inside, across = pack(me, f, c)
    pairs = [(i, i + 1) for i in range(1, n - 1, 2)]
    across = lax.ppermute(across, "tile", pairs + [(j, i) for i, j in pairs])
    inside = lax.ppermute(inside, "tile", [(i, i ^ 1) for i in range(n)])

    windows = struct((size + 4 * cols, wide), BF16)
    field = struct((ext, chans), BF16)
    kept = struct((n // 2, taps, chans // n, chans), F32)
    sent = struct((n // 2, taps, chans // n, chans), BF16)
    band = pltpu.VMEM((rows, cols, chans), BF16)
    xs, cs, hid, slope, acc = call(
        inner_kernel,
        (in_hbm(f), in_hbm(c), in_hbm(w_two), w_one),
        (windows, windows, field, field, struct((3, chans, wide), F32)),
        [band, band, pltpu.VMEM(w_two.shape, BF16), pltpu.SemaphoreType.DMA((3,))],
        work=3 * flops,
        raw=3,
    )
    xs, cs, hid, fac, keep_two, send_two = call(
        functools.partial(edge_kernel, n, order_two, scale),
        (inside, across, w_one, xs, cs, hid, acc),
        (windows, windows, field, struct((2 * cols, chans), F32), kept, sent),
        place=True,
        aliases={4: 0, 5: 1, 6: 2},
    )
    slope, keep_one, send_one = call(
        functools.partial(terms_kernel, n, order_one, scale),
        (xs, cs, fac, w_two, slope),
        (field, kept, sent),
        place=True,
        aliases={5: 0},
    )
    all_rows = pltpu.VMEM((ext, wide), BF16)
    hid, slope = call(
        functools.partial(sides_kernel, n, cols),
        (xs, cs, w_one, w_two, hid, slope),
        (field, field),
        place=True,
        aliases={5: 0, 6: 1},
    )
    (block_out,) = call(block_kernel, (hid, w_two, f), (struct(f.shape, BF16),), [all_rows])
    (input_grad,) = call(input_kernel, (slope, w_one, c), (struct(c.shape, BF16),), [all_rows])
    grad_two = halve(keep_two, send_two, order_two, n)
    grad_one = halve(keep_one, send_one, order_one, n)
    return (block_out[None], input_grad[None], grad_one, grad_two)


def solution(mesh):
    in_specs = (P("groups", "tile", None, None), P("groups", "tile", None, None), P(), P())
    out_specs = (
        P("groups", "tile", None, None),
        P("groups", "tile", None, None),
        P("tile", "groups", None),
        P("tile", "groups", None),
    )
    return jax.shard_map(layer, mesh=mesh, in_specs=in_specs, out_specs=out_specs, check_vma=False)
```

time: 64.9 us -> 50.7 us (0.78)
  starting transfers between devices: 22.5 us -> 15.9 us
  waiting for transfers between devices: 12.8 us -> 6.87 us
  local copies, waits for them, and re-layouts: 3.43 us -> 0.38 us
  Pallas kernels: 23 us -> 24.6 us
    ppermute x4 -> x2, starting transfers between devices: 6.92 us -> 1.23 us  [the longest x1 0.67 us: layer(): across = lax.ppermute(across, 'tile', pairs + [(j, i) for i, j in pairs])]
    ppermute x8, waiting for transfers between devices: 12.1 us -> 6.87 us  [halve(): got = lax.ppermute(send, 'tile', pairs)]
    unnamed x12 -> x8, local copies, waits for them, and re-layouts: 3.29 us -> 0.24 us
    pallas_call x8 -> x7, Pallas kernels: 23 us -> 24.6 us  [the longest x6 23.3 us: call(): pl.pallas_call(kernel, out_shape=outs, in_specs=specs, out_specs=tuple((W...]
    ppermute x8, starting transfers between devices: 15.6 us -> 14.7 us  [halve(): got = lax.ppermute(send, 'tile', pairs)]
    ppermute x4 -> x2, waiting for transfers between devices: 0.79 us -> 0.01 us  [the longest x1 0.01 us: layer(): across = lax.ppermute(across, 'tile', pairs + [(j, i) for i, j in pairs])]
  transfers between devices with their start and end apart: 12 -> 10, of which waited for: 7 -> 4; matrix products, arithmetic and copies ran while one was open for 2% -> 3% of each run, Pallas kernels for 19% -> 42%
where the time goes in v3:
time: 50.7 us; the launch traced here: 50.5 us
  Pallas kernels  24.6 us (49%)
  starting transfers between devices  15.9 us (31%)
  waiting for transfers between devices  6.87 us (14%)
  other arithmetic  1.98 us (4%)
  between operations  0.82 us (2%)
    pallas_call x6, Pallas kernels, call(): pl.pallas_call(kernel, out_shape=outs, in_specs=specs, out_specs=tuple((W...  23.3 us
    ppermute x8, starting transfers between devices, halve(): got = lax.ppermute(send, 'tile', pairs)  14.7 us
    ppermute x8, waiting for transfers between devices, halve(): got = lax.ppermute(send, 'tile', pairs)  6.87 us
    transpose x2, other arithmetic, halve(): return jnp.swapaxes(total[0], 0, 1)  1.35 us
    pallas_call x1, Pallas kernels, pack(): pl.pallas_call(pack_kernel, out_shape=(out,) * 2, in_specs=[pl.BlockSpec(...  1.28 us
  transfers between devices with their start and end apart: 10, of which 4 were waited for; matrix products, arithmetic and copies ran while one was open for 3% of the time, Pallas kernels for 42%

profile of v3, /device:TPU:0, one launch (start us, length us, event | category | flops | bytes accessed | tf_op | source)
XLA Modules:
  0.0 50.5 jit_solution(4280591353225498581)
XLA Ops:
  0.6 1.3 %shard_map.75 = (bf16[4,160,256]{2,1,0:T(8,128)(2,1)S(1)}, bf16[4,160,256]{2,1,0:T(8,128)(2,1)S(1)}) custom-call(s32[1]{0:T(128)} %bitcast.me_ref, bf16[12,160,256]{2,1,0:T(8,128)(2,1)} %bitcast.27, bf16[12,160,256]{2,1,0:T(8,128)(2,1)} %bitcast.30), custom_call_target="tpu_custom_call" | custom-call | tf_op jit(solution)/shard_map/pallas_call | solution.py:46
  1.9 0.6 %collective-permute-start = (bf16[4,160,256]{2,1,0:T(8,128)(2,1)S(1)}, bf16[4,160,256]{2,1,0:T(8,128)(2,1)S(1)}, u32[]{:S(2)}, u32[]{:S(2)}) collective-permute-start(bf16[4,160,256]{2,1,0:T(8,128)(2,1)S(1)} %get-tuple-element.22), channel_id=1, source_target_pairs={{0,1},{1,0},{2,3},{3,2},{4,5},{5,4},{6,7},{7,6},{8,9},{9,8},{10,11... | collective-permute-start | bytes 983048 | tf_op jit(solution)/shard_map/ppermute | solution.py:347
  2.5 0.7 %collective-permute-start.1 = (bf16[4,160,256]{2,1,0:T(8,128)(2,1)S(1)}, bf16[4,160,256]{2,1,0:T(8,128)(2,1)S(1)}, u32[]{:S(2)}, u32[]{:S(2)}) collective-permute-start(bf16[4,160,256]{2,1,0:T(8,128)(2,1)S(1)} %get-tuple-element.23), channel_id=1, source_target_pairs={{1,2},{3,4},{5,6},{7,8},{9,10},{11,12},{13,14},{2,1},{4,3},{6,5},{... | collective-permute-start | bytes 983048 | tf_op jit(solution)/shard_map/ppermute | solution.py:346
  3.2 8.8 %shard_map.76 = (bf16[2560,768]{1,0:T(8,128)(2,1)S(1)}, bf16[2560,768]{1,0:T(8,128)(2,1)S(1)}, bf16[2240,256]{1,0:T(8,128)(2,1)S(1)}, bf16[2240,256]{1,0:T(8,128)(2,1)S(1)}, f32[3,256,768]{2,1,0:T(8,128)S(1)}) custom-call(bf16[12,160,256]{2,1,0:T(8,128)(2,1)} %bitcast.28, bf16[12,160,256]{2,1,0:T(8,128)(2,1)} %bitcast.31, bf16[2304,256]{1,0:T(8,128)(2,1)} %bitcast.23, ...), custom_call_target="tpu_custom_call" | custom-call | flops 6794772480 | bytes 4194304 | tf_op jit(solution)/shard_map/pallas_call | solution.py:333
  11.9 0.0 collective-permute-done.1.across
  12.0 0.0 copy-start.1
  12.0 2.1 %shard_map.77 = (bf16[2560,768]{1,0:T(8,128)(2,1)S(1)}, bf16[2560,768]{1,0:T(8,128)(2,1)S(1)}, bf16[2240,256]{1,0:T(8,128)(2,1)S(1)}, f32[320,256]{1,0:T(8,128)S...) custom-call(s32[1]{0:T(128)} %bitcast.me_ref, ...), custom_call_target="tpu_custom_call", output_to_operand_aliasing={{0}: (4, {}), {1}: (5, {}), {2}: (6, {})} | custom-call | flops 2264924160 | bytes 4194304 | tf_op jit(solution)/shard_map/pallas_call | solution.py:333
  14.1 3.9 %collective-permute-start.6 = (bf16[8,9,16,256]{3,2,1,0:T(8,128)(2,1)S(1)}, bf16[8,9,16,256]{3,2,1,0:T(8,128)(2,1)S(1)}, u32[]{:S(2)}, u32[]{:S(2)}) collective-permute-start(bf16[8,9,16,256]{3,2,1,0:T(8,128)(2,1)S(1)} %get-tuple-element.39), channel_id=1, source_target_pairs={{0,1},{1,0},{2,3},{3,2},{4,5},{5,4},{6,7},{7,6},{8,9},{9,8},{10,11... | collective-permute-start | bytes 1769480 | tf_op jit(solution)/shard_map/ppermute | solution.py:303
  18.0 3.2 %shard_map.78 = (bf16[2240,256]{1,0:T(8,128)(2,1)S(1)}, f32[8,9,16,256]{3,2,1,0:T(8,128)S(1)}, bf16[8,9,16,256]{3,2,1,0:T(8,128)(2,1)S(1)}) custom-call(s32[1]{0:T(128)} %bitcast.me_ref, bf16[2560,768]{1,0:T(8,128)(2,1)S(1)} %get-tuple-element.28.xs, bf16[2560,768]{1,0:T(8,128)(2,1)S(1)} %get-tuple-element.29.cs, ...), custom_call_target="tpu_custom_call", output_to_operand_aliasing={{0}: (5, {})} | custom-call | flops 2264924160 | bytes 4194304 | tf_op jit(solution)/shard_map/pallas_call | solution.py:333
  21.2 0.1 collective-permute-start.2
  21.3 1.0 %shard_map.79 = (bf16[2240,256]{1,0:T(8,128)(2,1)S(1)}, bf16[2240,256]{1,0:T(8,128)(2,1)S(1)}) custom-call(s32[1]{0:T(128)} %bitcast.me_ref, bf16[2560,768]{1,0:T(8,128)(2,1)S(1)} %get-tuple-element.28.xs, bf16[2560,768]{1,0:T(8,128)(2,1)S(1)} %get-tuple-element.29.cs, bf16[2304,256]{1,0:T(8,128)(2,1)S(1)} %bitcast.21, ...), custom_call_target="tpu_custom_call", output_to_operand_aliasing={{0}: (5, {}), {1}: (6, {})} | custom-call | flops 2264924160 | bytes 4194304 | tf_op jit(solution)/shard_map/pallas_call | solution.py:333
  22.3 0.2 copy-done.2
  22.5 4.1 %shard_map.80 = bf16[12,160,256]{2,1,0:T(8,128)(2,1)} custom-call(bf16[2240,256]{1,0:T(8,128)(2,1)S(1)} %get-tuple-element.34.hid, bf16[2304,256]{1,0:T(8,128)(2,1)S(1)} %bitcast.26, bf16[12,160,256]{2,1,0:T(8,128)(2,1)S(1)} %bitcast.29), custom_call_target="tpu_custom_call" | custom-call | flops 2264924160 | bytes 4194304 | tf_op jit(solution)/shard_map/pallas_call | solution.py:333
  26.6 0.2 convert_add_fusion
  26.9 1.6 %collective-permute-start.7 = (bf16[4,9,16,256]{3,2,1,0:T(8,128)(2,1)S(1)}, bf16[4,9,16,256]{3,2,1,0:T(8,128)(2,1)S(1)}, u32[]{:S(2)}, u32[]{:S(2)}) collective-permute-start(bf16[4,9,16,256]{3,2,1,0:T(8,128)(2,1)S(1)} %slice.82), channel_id=1, source_target_pairs={{0,2},{1,3},{2,0},{3,1},{4,6},{5,7},{6,4},{7,5},{8,10},{9,11},{10,... | collective-permute-start | bytes 884744 | tf_op jit(solution)/shard_map/ppermute | solution.py:303
  28.5 0.0 collective-permute-done.2
  28.5 0.2 convert_add_fusion.1
  28.8 1.6 %collective-permute-start.3 = (bf16[4,9,16,256]{3,2,1,0:T(8,128)(2,1)S(1)}, bf16[4,9,16,256]{3,2,1,0:T(8,128)(2,1)S(1)}, u32[]{:S(2)}, u32[]{:S(2)}) collective-permute-start(bf16[4,9,16,256]{3,2,1,0:T(8,128)(2,1)S(1)} %slice.83), channel_id=1, source_target_pairs={{0,4},{1,5},{2,6},{3,7},{4,0},{5,1},{6,2},{7,3},{8,12},{9,13},{10,... | collective-permute-start | bytes 884744 | tf_op jit(solution)/shard_map/ppermute | solution.py:303
  30.4 4.2 %shard_map.81 = bf16[12,160,256]{2,1,0:T(8,128)(2,1)} custom-call(bf16[2240,256]{1,0:T(8,128)(2,1)S(1)} %get-tuple-element.35.slope, bf16[2304,256]{1,0:T(8,128)(2,1)S(1)} %bitcast.22, bf16[12,160,256]{2,1,0:T(8,128)(2,1)S(1)} %bitcast.32), custom_call_target="tpu_custom_call" | custom-call | flops 2264924160 | bytes 4194304 | tf_op jit(solution)/shard_map/pallas_call | solution.py:333
  34.6 1.8 %collective-permute-done.7 = bf16[4,9,16,256]{3,2,1,0:T(8,128)(2,1)S(1)} collective-permute-done((bf16[4,9,16,256]{3,2,1,0:T(8,128)(2,1)S(1)}, bf16[4,9,16,256]{3,2,1,0:T(8,128)(2,1)S(1)}, u32[]{:S(2)}, u32[]{:S(2)}) %collective-permute-start.7) | collective-permute-done | bytes 294944 | tf_op jit(solution)/shard_map/ppermute | solution.py:303
  36.3 0.1 slice_add_fusion
  36.5 1.7 %collective-permute-start.8 = (bf16[2,9,16,256]{3,2,1,0:T(8,128)(2,1)S(1)}, bf16[2,9,16,256]{3,2,1,0:T(8,128)(2,1)S(1)}, u32[]{:S(2)}, u32[]{:S(2)}) collective-permute-start(bf16[2,9,16,256]{3,2,1,0:T(8,128)(2,1)S(1)} %slice.84), channel_id=1, source_target_pairs={{0,4},{1,5},{2,6},{3,7},{4,0},{5,1},{6,2},{7,3},{8,12},{9,13},{10,... | collective-permute-start | bytes 442376 | tf_op jit(solution)/shard_map/ppermute | solution.py:303
  38.1 0.0 collective-permute-done.3
  38.1 0.1 slice_add_fusion.1
  38.3 1.5 %collective-permute-start.4 = (bf16[2,9,16,256]{3,2,1,0:T(8,128)(2,1)S(1)}, bf16[2,9,16,256]{3,2,1,0:T(8,128)(2,1)S(1)}, u32[]{:S(2)}, u32[]{:S(2)}) collective-permute-start(bf16[2,9,16,256]{3,2,1,0:T(8,128)(2,1)S(1)} %slice.85), channel_id=1, source_target_pairs={{0,2},{1,3},{2,0},{3,1},{4,6},{5,7},{6,4},{7,5},{8,10},{9,11},{10,... | collective-permute-start | bytes 442376 | tf_op jit(solution)/shard_map/ppermute | solution.py:303
  39.8 2.1 %collective-permute-done.8 = bf16[2,9,16,256]{3,2,1,0:T(8,128)(2,1)S(1)} collective-permute-done((bf16[2,9,16,256]{3,2,1,0:T(8,128)(2,1)S(1)}, bf16[2,9,16,256]{3,2,1,0:T(8,128)(2,1)S(1)}, u32[]{:S(2)}, u32[]{:S(2)}) %collective-permute-start.8) | collective-permute-done | bytes 147488 | tf_op jit(solution)/shard_map/ppermute | solution.py:303
  42.0 2.5 %collective-permute-start.9 = (bf16[1,9,16,256]{3,2,1,0:T(8,128)(2,1)S(1)}, bf16[1,9,16,256]{3,2,1,0:T(8,128)(2,1)S(1)}, u32[]{:S(2)}, u32[]{:S(2)}) collective-permute-start(bf16[1,9,16,256]{3,2,1,0:T(8,128)(2,1)S(1)} %slice.86), channel_id=1, source_target_pairs={{0,8},{1,9},{2,10},{3,11},{4,12},{5,13},{6,14},{7,15},{8,0},{9,1},... | collective-permute-start | bytes 221192 | tf_op jit(solution)/shard_map/ppermute | solution.py:303
  44.5 1.7 %collective-permute-start.5 = (bf16[1,9,16,256]{3,2,1,0:T(8,128)(2,1)S(1)}, bf16[1,9,16,256]{3,2,1,0:T(8,128)(2,1)S(1)}, u32[]{:S(2)}, u32[]{:S(2)}) collective-permute-start(bf16[1,9,16,256]{3,2,1,0:T(8,128)(2,1)S(1)} %slice.87), channel_id=1, source_target_pairs={{0,8},{1,9},{2,10},{3,11},{4,12},{5,13},{6,14},{7,15},{8,0},{9,1},... | collective-permute-start | bytes 221192 | tf_op jit(solution)/shard_map/ppermute | solution.py:303
  46.2 2.9 %collective-permute-done.9 = bf16[1,9,16,256]{3,2,1,0:T(8,128)(2,1)S(1)} collective-permute-done((bf16[1,9,16,256]{3,2,1,0:T(8,128)(2,1)S(1)}, bf16[1,9,16,256]{3,2,1,0:T(8,128)(2,1)S(1)}, u32[]{:S(2)}, u32[]{:S(2)}) %collective-permute-start.9) | collective-permute-done | bytes 73760 | tf_op jit(solution)/shard_map/ppermute | solution.py:303
  49.1 0.7 %fusion = f32[16,9,256]{2,0,1:T(8,128)} fusion(f32[2,9,16,256]{3,2,1,0:T(8,128)S(1)} %slice_add_fusion.2, bf16[1,9,16,256]{3,2,1,0:T(8,128)(2,1)S(1)} %collective-permute-done.9), kind=kLoop, calls=%fused_computation.12 | loop fusion | flops 73728 | bytes 368640 | tf_op jit(solution)/shard_map/transpose | solution.py:309
  49.8 0.1 collective-permute-done.5
  49.9 0.7 %fusion.1 = f32[16,9,256]{2,0,1:T(8,128)} fusion(f32[2,9,16,256]{3,2,1,0:T(8,128)S(1)} %slice_add_fusion.3, bf16[1,9,16,256]{3,2,1,0:T(8,128)(2,1)S(1)} %collective-permute-done.5), kind=kLoop, calls=%fused_computation.15 | loop fusion | flops 73728 | bytes 368640 | tf_op jit(solution)/shard_map/transpose | solution.py:309
  (17 shorter events, 0.2 us)
Async XLA Ops:
  0.6 2.5 %copy-start = (bf16[256,9,256]{2,0,1:T(8,128)(2,1)S(1)}, bf16[256,9,256]{2,0,1:T(8,128)(2,1)}, u32[]{:S(2)}) copy-start(bf16[256,9,256]{2,0,1:T(8,128)(2,1)} %param.6) | copy-start | bytes 3538948
  1.9 10.0 %collective-permute-start = (bf16[4,160,256]{2,1,0:T(8,128)(2,1)S(1)}, bf16[4,160,256]{2,1,0:T(8,128)(2,1)S(1)}, u32[]{:S(2)}, u32[]{:S(2)}) collective-permute-start(bf16[4,160,256]{2,1,0:T(8,128)(2,1)S(1)} %get-tuple-element.22), channel_id=1, source_target_pairs={{0,1},{1,0},{2,3},{3,2},{4,5},{5,4},{6,7},{7,6},{8,9},{9,8},{10,11... | collective-permute-start | bytes 983048 | tf_op jit(solution)/shard_map/ppermute | solution.py:347
  2.5 9.5 %collective-permute-start.1 = (bf16[4,160,256]{2,1,0:T(8,128)(2,1)S(1)}, bf16[4,160,256]{2,1,0:T(8,128)(2,1)S(1)}, u32[]{:S(2)}, u32[]{:S(2)}) collective-permute-start(bf16[4,160,256]{2,1,0:T(8,128)(2,1)S(1)} %get-tuple-element.23), channel_id=1, source_target_pairs={{1,2},{3,4},{5,6},{7,8},{9,10},{11,12},{13,14},{2,1},{4,3},{6,5},{... | collective-permute-start | bytes 983048 | tf_op jit(solution)/shard_map/ppermute | solution.py:346
  12.0 6.1 %copy-start.1 = (bf16[256,9,256]{2,0,1:T(8,128)(2,1)S(1)}, bf16[256,9,256]{2,0,1:T(8,128)(2,1)}, u32[]{:S(2)}) copy-start(bf16[256,9,256]{2,0,1:T(8,128)(2,1)} %param.7) | copy-start | bytes 3538948
  14.1 12.6 %collective-permute-start.6 = (bf16[8,9,16,256]{3,2,1,0:T(8,128)(2,1)S(1)}, bf16[8,9,16,256]{3,2,1,0:T(8,128)(2,1)S(1)}, u32[]{:S(2)}, u32[]{:S(2)}) collective-permute-start(bf16[8,9,16,256]{3,2,1,0:T(8,128)(2,1)S(1)} %get-tuple-element.39), channel_id=1, source_target_pairs={{0,1},{1,0},{2,3},{3,2},{4,5},{5,4},{6,7},{7,6},{8,9},{9,8},{10,11... | collective-permute-start | bytes 1769480 | tf_op jit(solution)/shard_map/ppermute | solution.py:303
  21.2 7.3 %collective-permute-start.2 = (bf16[8,9,16,256]{3,2,1,0:T(8,128)(2,1)S(1)}, bf16[8,9,16,256]{3,2,1,0:T(8,128)(2,1)S(1)}, u32[]{:S(2)}, u32[]{:S(2)}) collective-permute-start(bf16[8,9,16,256]{3,2,1,0:T(8,128)(2,1)S(1)} %get-tuple-element.37), channel_id=1, source_target_pairs={{0,1},{1,0},{2,3},{3,2},{4,5},{5,4},{6,7},{7,6},{8,9},{9,8},{10,11... | collective-permute-start | bytes 1769480 | tf_op jit(solution)/shard_map/ppermute | solution.py:303
  21.3 1.2 %copy-start.2 = (bf16[1,12,160,256]{3,2,1,0:T(8,128)(2,1)S(1)}, bf16[1,12,160,256]{3,2,1,0:T(8,128)(2,1)}, u32[]{:S(2)}) copy-start(bf16[1,12,160,256]{3,2,1,0:T(8,128)(2,1)} %param.4) | copy-start | bytes 2949124
  26.9 9.5 %collective-permute-start.7 = (bf16[4,9,16,256]{3,2,1,0:T(8,128)(2,1)S(1)}, bf16[4,9,16,256]{3,2,1,0:T(8,128)(2,1)S(1)}, u32[]{:S(2)}, u32[]{:S(2)}) collective-permute-start(bf16[4,9,16,256]{3,2,1,0:T(8,128)(2,1)S(1)} %slice.82), channel_id=1, source_target_pairs={{0,2},{1,3},{2,0},{3,1},{4,6},{5,7},{6,4},{7,5},{8,10},{9,11},{10,... | collective-permute-start | bytes 884744 | tf_op jit(solution)/shard_map/ppermute | solution.py:303
  28.5 1.9 %copy-start.3 = (bf16[1,12,160,256]{3,2,1,0:T(8,128)(2,1)S(1)}, bf16[1,12,160,256]{3,2,1,0:T(8,128)(2,1)}, u32[]{:S(2)}) copy-start(bf16[1,12,160,256]{3,2,1,0:T(8,128)(2,1)} %param.5) | copy-start | bytes 2949124
  28.8 9.4 %collective-permute-start.3 = (bf16[4,9,16,256]{3,2,1,0:T(8,128)(2,1)S(1)}, bf16[4,9,16,256]{3,2,1,0:T(8,128)(2,1)S(1)}, u32[]{:S(2)}, u32[]{:S(2)}) collective-permute-start(bf16[4,9,16,256]{3,2,1,0:T(8,128)(2,1)S(1)} %slice.83), channel_id=1, source_target_pairs={{0,4},{1,5},{2,6},{3,7},{4,0},{5,1},{6,2},{7,3},{8,12},{9,13},{10,... | collective-permute-start | bytes 884744 | tf_op jit(solution)/shard_map/ppermute | solution.py:303
  36.5 5.4 %collective-permute-start.8 = (bf16[2,9,16,256]{3,2,1,0:T(8,128)(2,1)S(1)}, bf16[2,9,16,256]{3,2,1,0:T(8,128)(2,1)S(1)}, u32[]{:S(2)}, u32[]{:S(2)}) collective-permute-start(bf16[2,9,16,256]{3,2,1,0:T(8,128)(2,1)S(1)} %slice.84), channel_id=1, source_target_pairs={{0,4},{1,5},{2,6},{3,7},{4,0},{5,1},{6,2},{7,3},{8,12},{9,13},{10,... | collective-permute-start | bytes 442376 | tf_op jit(solution)/shard_map/ppermute | solution.py:303
  38.3 6.2 %collective-permute-start.4 = (bf16[2,9,16,256]{3,2,1,0:T(8,128)(2,1)S(1)}, bf16[2,9,16,256]{3,2,1,0:T(8,128)(2,1)S(1)}, u32[]{:S(2)}, u32[]{:S(2)}) collective-permute-start(bf16[2,9,16,256]{3,2,1,0:T(8,128)(2,1)S(1)} %slice.85), channel_id=1, source_target_pairs={{0,2},{1,3},{2,0},{3,1},{4,6},{5,7},{6,4},{7,5},{8,10},{9,11},{10,... | collective-permute-start | bytes 442376 | tf_op jit(solution)/shard_map/ppermute | solution.py:303
  42.0 7.1 %collective-permute-start.9 = (bf16[1,9,16,256]{3,2,1,0:T(8,128)(2,1)S(1)}, bf16[1,9,16,256]{3,2,1,0:T(8,128)(2,1)S(1)}, u32[]{:S(2)}, u32[]{:S(2)}) collective-permute-start(bf16[1,9,16,256]{3,2,1,0:T(8,128)(2,1)S(1)} %slice.86), channel_id=1, source_target_pairs={{0,8},{1,9},{2,10},{3,11},{4,12},{5,13},{6,14},{7,15},{8,0},{9,1},... | collective-permute-start | bytes 221192 | tf_op jit(solution)/shard_map/ppermute | solution.py:303
  44.5 5.4 %collective-permute-start.5 = (bf16[1,9,16,256]{3,2,1,0:T(8,128)(2,1)S(1)}, bf16[1,9,16,256]{3,2,1,0:T(8,128)(2,1)S(1)}, u32[]{:S(2)}, u32[]{:S(2)}) collective-permute-start(bf16[1,9,16,256]{3,2,1,0:T(8,128)(2,1)S(1)} %slice.87), channel_id=1, source_target_pairs={{0,8},{1,9},{2,10},{3,11},{4,12},{5,13},{6,14},{7,15},{8,0},{9,1},... | collective-permute-start | bytes 221192 | tf_op jit(solution)/shard_map/ppermute | solution.py:303

commit v4 on v3

--- a/solution.py
+++ b/solution.py
@@ -12,6 +12,7 @@
 BF16 = jnp.bfloat16
 WHOLE = pl.BlockSpec(memory_space=pltpu.VMEM)
 LIMIT = 20 << 20
+OUTPUT_PARTS = 3
 
 
 def struct(shape, dtype):
@@ -187,7 +188,7 @@
     half = (rows - 2) // 2
     size = half * cols
 
-    def step(k, carry):
+    for k in range(2):
         start = (2 + k * half) * cols
         here = pl.ds(pl.multiple_of(start, cols), size)
         pre = conv_rows(xs, w_one, start, size, cols)
@@ -195,9 +196,6 @@
         hid[here, :] = (pre * sigma).astype(BF16)
         grad = conv_t_rows(cs, w_two, start, size, cols, chans)
         slope[here, :] = (grad * derivative(pre, sigma)).astype(BF16)
-        return carry
-
-    lax.fori_loop(0, 2, step, 0)
     left = rows_of(hid, 2, rows - 2, cols)
     for a in range(3):
         acc[a] = transposed_dot(left, rows_of(cs, 4 - a, rows - 2, cols))
@@ -212,8 +210,9 @@
     for k in range(2):
         for dst, part, sign in ((xs, k, 1), (cs, 2 + k, -1)):
             one, two = inside[part], across[part]
-            put_windows(dst, k, jnp.where(odd, one, two), sign)
-            put_windows(dst, rows + 2 + k, jnp.where(odd, two, one), sign)
+            above, below = jnp.where(odd, one, two), jnp.where(odd, two, one)
+            put_windows(dst, k, jnp.where(me == 0, 0.0, above).astype(BF16), sign)
+            put_windows(dst, rows + 2 + k, jnp.where(me == n - 1, 0.0, below).astype(BF16), sign)
     pre = pre_of_pair(xs, w, 0, rows - 1, cols)
     sigma = jax.nn.sigmoid(pre)
     hidden = (pre * sigma).astype(BF16)
@@ -221,12 +220,19 @@
     hid[rows * cols : (rows + 1) * cols, :] = hidden[cols:]
     fac[...] = derivative(pre, sigma)
     left = pair(hid, 1, rows, cols)
-    for a in range(3):
-        out = acc[a] + transposed_dot(left, pair(cs, 3 - a, rows + 2 - a, cols))
+
+    def part(a, carry):
+        two = [
+            cs[pl.ds(pl.multiple_of((first - a) * cols, cols), cols), :] for first in (3, rows + 2)
+        ]
+        out = acc[a] + transposed_dot(left, jnp.concatenate(two, axis=0))
         for b in range(3):
             store_terms(
                 a * 3 + b, out[:, b * chans : (b + 1) * chans], keep, send, me, n, order, scale
             )
+        return carry
+
+    lax.fori_loop(0, 3, part, 0)
 
 
 def terms_kernel(n, order, scale, me_ref, xs, cs, fac, w, slope_in, slope, keep, send):
@@ -259,42 +265,31 @@
         slope[there, :] = jnp.where(outside, 0.0, value[here]).astype(BF16)
 
 
-def widen(dst, source, count, cols, sign):
+def outputs_kernel(first, hid, slope, xs, cs, w_two, w_one, *refs):
+    block_out, input_grad, hs, ss, f_done, c_done, sems = refs[-7:]
+    count, cols, chans = f_done.shape
+    here = pl.ds(first, count)
+
     def step(k, carry):
-        put_windows(dst, k, source[pl.ds(pl.multiple_of(k * cols, cols), cols), :], sign)
+        row = pl.ds(pl.multiple_of((first + k) * cols, cols), cols)
+        put_windows(hs, k, hid[row, :], 1)
+        put_windows(ss, k, slope[row, :], -1)
         return carry
 
-    lax.fori_loop(0, count, step, 0)
-
-
-def block_kernel(hid, w_two, f, block_out, hs):
-    rows, cols, chans = f.shape
-    widen(hs, hid, rows + 2, cols, 1)
-    half = rows // 2
-    size = half * cols
-
-    def step(k, carry):
-        here = pl.ds(k * half, half)
-        out = conv_rows(hs, w_two, k * size, size, cols)
-        block_out[here] = (f[here].astype(F32) + out.reshape(half, cols, chans)).astype(BF16)
-        return carry
-
-    lax.fori_loop(0, 2, step, 0)
-
-
-def input_kernel(slope, w_one, c, input_grad, ss):
-    rows, cols, chans = c.shape
-    widen(ss, slope, rows + 2, cols, -1)
-    half = rows // 2
-    size = half * cols
-
-    def step(k, carry):
-        here = pl.ds(k * half, half)
-        out = conv_t_rows(ss, w_one, k * size, size, cols, chans)
-        input_grad[here] = (c[here].astype(F32) + out.reshape(half, cols, chans)).astype(BF16)
-        return carry
-
-    lax.fori_loop(0, 2, step, 0)
+    lax.fori_loop(0, count + 2, step, 0)
+    own = slice((first + 2) * cols, (first + 2 + count) * cols)
+    shape = (count, cols, chans)
+    total = xs[own, chans : 2 * chans].astype(F32) + conv_rows(hs, w_two, 0, count * cols, cols)
+    f_done[...] = total.astype(BF16).reshape(shape)
+    store_f = pltpu.make_async_copy(f_done, block_out.at[here], sems.at[0])
+    store_f.start()
+    grad = conv_t_rows(ss, w_one, 0, count * cols, cols, chans)
+    total = cs[own, chans : 2 * chans].astype(F32) + grad
+    c_done[...] = total.astype(BF16).reshape(shape)
+    store_c = pltpu.make_async_copy(c_done, input_grad.at[here], sems.at[1])
+    store_c.start()
+    store_f.wait()
+    store_c.wait()
 
 
 def halve(keep, send, order, n):
@@ -342,7 +337,7 @@
         )(*(((me,) if place else ()) + tuple(args)))
 
     inside, across = pack(me, f, c)
-    pairs = [(i, i + 1) for i in range(1, n - 1, 2)]
+    pairs = [(i, (i + 1) % n) for i in range(1, n, 2)]
     across = lax.ppermute(across, "tile", pairs + [(j, i) for i, j in pairs])
     inside = lax.ppermute(inside, "tile", [(i, i ^ 1) for i in range(n)])
 
@@ -373,7 +368,6 @@
         place=True,
         aliases={5: 0},
     )
-    all_rows = pltpu.VMEM((ext, wide), BF16)
     hid, slope = call(
         functools.partial(sides_kernel, n, cols),
         (xs, cs, w_one, w_two, hid, slope),
@@ -381,8 +375,25 @@
         place=True,
         aliases={5: 0, 6: 1},
     )
-    (block_out,) = call(block_kernel, (hid, w_two, f), (struct(f.shape, BF16),), [all_rows])
-    (input_grad,) = call(input_kernel, (slope, w_one, c), (struct(c.shape, BF16),), [all_rows])
+    parts = OUTPUT_PARTS if rows % OUTPUT_PARTS == 0 else 1
+    count = rows // parts
+    outs = ()
+    for part in range(parts):
+        outs = pl.pallas_call(
+            functools.partial(outputs_kernel, part * count),
+            out_shape=(struct(f.shape, BF16), struct(c.shape, BF16)),
+            in_specs=[WHOLE] * 6 + [hbm] * len(outs),
+            out_specs=(hbm, hbm),
+            scratch_shapes=[pltpu.VMEM(((count + 2) * cols, wide), BF16)] * 2
+            + [pltpu.VMEM((count, cols, chans), BF16)] * 2
+            + [pltpu.SemaphoreType.DMA((2,))],
+            input_output_aliases={6: 0, 7: 1} if outs else {},
+            compiler_params=pltpu.CompilerParams(vmem_limit_bytes=LIMIT),
+            cost_estimate=pl.CostEstimate(
+                flops=2 * flops // parts, bytes_accessed=4 << 20, transcendentals=0
+            ),
+        )(hid, slope, xs, cs, w_two, w_one, *outs)
+    block_out, input_grad = outs
     grad_two = halve(keep_two, send_two, order_two, n)
     grad_one = halve(keep_one, send_one, order_one, n)
     return (block_out[None], input_grad[None], grad_one, grad_two)

time: 50.7 us -> 52.8 us (1.041)
  waiting for transfers between devices: 6.87 us -> 12.8 us
  starting transfers between devices: 15.9 us -> 11.9 us
    pallas_call x0 -> x3, Pallas kernels: none -> 9.03 us  [layer(): pl.pallas_call(functools.partial(outputs_kernel, part * count), out_shape...]
    ppermute x8, starting transfers between devices: 14.7 us -> 5.73 us  [halve(): got = lax.ppermute(send, 'tile', pairs)]
    pallas_call x6 -> x4, Pallas kernels: 23.3 us -> 14.6 us  [call(): pl.pallas_call(kernel, out_shape=outs, in_specs=specs, out_specs=tuple((W...]
    ppermute x8, waiting for transfers between devices: 6.87 us -> 12.8 us  [halve(): got = lax.ppermute(send, 'tile', pairs)]
    ppermute x1, starting transfers between devices: 0.67 us -> 5.66 us  [layer(): across = lax.ppermute(across, 'tile', pairs + [(j, i) for i, j in pairs])]
  transfers between devices with their start and end apart: 10 -> 10, of which waited for: 4 -> 5; matrix products, arithmetic and copies ran while one was open for 3% -> 3% of each run, Pallas kernels for 42% -> 41%
where the time goes in v4:
time: 52.8 us; the launch traced here: 52.7 us
  Pallas kernels  24.9 us (47%)
  waiting for transfers between devices  12.8 us (24%)
  starting transfers between devices  11.9 us (23%)
  other arithmetic  1.98 us (4%)
  between operations  0.87 us (2%)
    pallas_call x4, Pallas kernels, call(): pl.pallas_call(kernel, out_shape=outs, in_specs=specs, out_specs=tuple((W...  14.6 us
    ppermute x8, waiting for transfers between devices, halve(): got = lax.ppermute(send, 'tile', pairs)  12.8 us
    pallas_call x3, Pallas kernels, layer(): pl.pallas_call(functools.partial(outputs_kernel, part * count), out_shape...  9.03 us
    ppermute x8, starting transfers between devices, halve(): got = lax.ppermute(send, 'tile', pairs)  5.73 us
    ppermute x1, starting transfers between devices, layer(): across = lax.ppermute(across, 'tile', pairs + [(j, i) for i, j in pairs])  5.66 us
    transpose x2, other arithmetic, halve(): return jnp.swapaxes(total[0], 0, 1)  1.36 us
    pallas_call x1, Pallas kernels, pack(): pl.pallas_call(pack_kernel, out_shape=(out,) * 2, in_specs=[pl.BlockSpec(...  1.28 us
  transfers between devices with their start and end apart: 10, of which 5 were waited for; matrix products, arithmetic and copies ran while one was open for 3% of the time, Pallas kernels for 41%

profile of v4, /device:TPU:0, one launch (start us, length us, event | category | flops | bytes accessed | tf_op | source)
XLA Modules:
  0.0 52.7 jit_solution(6729323268982153643)
XLA Ops:
  0.6 1.3 %shard_map.75 = (bf16[4,160,256]{2,1,0:T(8,128)(2,1)S(1)}, bf16[4,160,256]{2,1,0:T(8,128)(2,1)S(1)}) custom-call(s32[1]{0:T(128)} %bitcast.me_ref, bf16[12,160,256]{2,1,0:T(8,128)(2,1)} %bitcast.33, bf16[12,160,256]{2,1,0:T(8,128)(2,1)} %bitcast.35), custom_call_target="tpu_custom_call" | custom-call | tf_op jit(solution)/shard_map/pallas_call | solution.py:47
  1.9 0.6 %collective-permute-start = (bf16[4,160,256]{2,1,0:T(8,128)(2,1)S(1)}, bf16[4,160,256]{2,1,0:T(8,128)(2,1)S(1)}, u32[]{:S(2)}, u32[]{:S(2)}) collective-permute-start(bf16[4,160,256]{2,1,0:T(8,128)(2,1)S(1)} %get-tuple-element.28), channel_id=1, source_target_pairs={{0,1},{1,0},{2,3},{3,2},{4,5},{5,4},{6,7},{7,6},{8,9},{9,8},{10,11... | collective-permute-start | bytes 983048 | tf_op jit(solution)/shard_map/ppermute | solution.py:342
  2.5 5.7 %collective-permute-start.1 = (bf16[4,160,256]{2,1,0:T(8,128)(2,1)S(1)}, bf16[4,160,256]{2,1,0:T(8,128)(2,1)S(1)}, u32[]{:S(2)}, u32[]{:S(2)}) collective-permute-start(bf16[4,160,256]{2,1,0:T(8,128)(2,1)S(1)} %get-tuple-element.29), channel_id=1, source_target_pairs={{1,2},{3,4},{5,6},{7,8},{9,10},{11,12},{13,14},{15,0},{2,1},{4,3},... | collective-permute-start | bytes 983048 | tf_op jit(solution)/shard_map/ppermute | solution.py:341
  8.2 8.4 %shard_map.76 = (bf16[2560,768]{1,0:T(8,128)(2,1)S(1)}, bf16[2560,768]{1,0:T(8,128)(2,1)S(1)}, bf16[2240,256]{1,0:T(8,128)(2,1)S(1)}, bf16[2240,256]{1,0:T(8,128)(2,1)S(1)}, f32[3,256,768]{2,1,0:T(8,128)S(1)}) custom-call(bf16[12,160,256]{2,1,0:T(8,128)(2,1)} %bitcast.34, bf16[12,160,256]{2,1,0:T(8,128)(2,1)} %bitcast.36, bf16[2304,256]{1,0:T(8,128)(2,1)} %bitcast.25, ...), custom_call_target="tpu_custom_call" | custom-call | flops 6794772480 | bytes 4194304 | tf_op jit(solution)/shard_map/pallas_call | solution.py:328
  16.5 0.0 collective-permute-done.inside
  16.6 0.0 collective-permute-done.1.across
  16.6 0.0 copy-start.1
  16.6 2.0 %shard_map.77 = (bf16[2560,768]{1,0:T(8,128)(2,1)S(1)}, bf16[2560,768]{1,0:T(8,128)(2,1)S(1)}, bf16[2240,256]{1,0:T(8,128)(2,1)S(1)}, f32[320,256]{1,0:T(8,128)S...) custom-call(s32[1]{0:T(128)} %bitcast.me_ref, ...), custom_call_target="tpu_custom_call", output_to_operand_aliasing={{0}: (4, {}), {1}: (5, {}), {2}: (6, {})} | custom-call | flops 2264924160 | bytes 4194304 | tf_op jit(solution)/shard_map/pallas_call | solution.py:328
  18.6 0.1 collective-permute-start.6
  18.7 3.2 %shard_map.78 = (bf16[2240,256]{1,0:T(8,128)(2,1)S(1)}, f32[8,9,16,256]{3,2,1,0:T(8,128)S(1)}, bf16[8,9,16,256]{3,2,1,0:T(8,128)(2,1)S(1)}) custom-call(s32[1]{0:T(128)} %bitcast.me_ref, bf16[2560,768]{1,0:T(8,128)(2,1)S(1)} %get-tuple-element.34.xs, bf16[2560,768]{1,0:T(8,128)(2,1)S(1)} %get-tuple-element.35.cs, ...), custom_call_target="tpu_custom_call", output_to_operand_aliasing={{0}: (5, {})} | custom-call | flops 2264924160 | bytes 4194304 | tf_op jit(solution)/shard_map/pallas_call | solution.py:328
  21.9 0.5 %collective-permute-start.2 = (bf16[8,9,16,256]{3,2,1,0:T(8,128)(2,1)S(1)}, bf16[8,9,16,256]{3,2,1,0:T(8,128)(2,1)S(1)}, u32[]{:S(2)}, u32[]{:S(2)}) collective-permute-start(bf16[8,9,16,256]{3,2,1,0:T(8,128)(2,1)S(1)} %get-tuple-element.49), channel_id=1, source_target_pairs={{0,1},{1,0},{2,3},{3,2},{4,5},{5,4},{6,7},{7,6},{8,9},{9,8},{10,11... | collective-permute-start | bytes 1769480 | tf_op jit(solution)/shard_map/ppermute | solution.py:298
  22.4 1.0 %shard_map.79 = (bf16[2240,256]{1,0:T(8,128)(2,1)S(1)}, bf16[2240,256]{1,0:T(8,128)(2,1)S(1)}) custom-call(s32[1]{0:T(128)} %bitcast.me_ref, bf16[2560,768]{1,0:T(8,128)(2,1)S(1)} %get-tuple-element.34.xs, bf16[2560,768]{1,0:T(8,128)(2,1)S(1)} %get-tuple-element.35.cs, bf16[2304,256]{1,0:T(8,128)(2,1)S(1)} %bitcast.21, ...), custom_call_target="tpu_custom_call", output_to_operand_aliasing={{0}: (5, {}), {1}: (6, {})} | custom-call | flops 2264924160 | bytes 4194304 | tf_op jit(solution)/shard_map/pallas_call | solution.py:328
  23.4 3.0 %shard_map.80 = (bf16[12,160,256]{2,1,0:T(8,128)(2,1)}, bf16[12,160,256]{2,1,0:T(8,128)(2,1)}) custom-call(bf16[2240,256]{1,0:T(8,128)(2,1)S(1)} %get-tuple-element.40.hid, bf16[2240,256]{1,0:T(8,128)(2,1)S(1)} %get-tuple-element.41.slope, bf16[2560,768]{1,0:T(8,128)(2,1)S(1)} %get-tuple-element.34.xs, bf16[2560,768]{1,0:T(8,128)(2,1)S(1)} %get-tuple-element.35.cs, ...), custom_call_target="tpu_custom_call" | custom-call | flops 1509949440 | bytes 4194304 | tf_op jit(solution)/shard_map/pallas_call | solution.py:382
  26.4 3.0 %shard_map.81 = (bf16[12,160,256]{2,1,0:T(8,128)(2,1)}, bf16[12,160,256]{2,1,0:T(8,128)(2,1)}) custom-call(bf16[2240,256]{1,0:T(8,128)(2,1)S(1)} %get-tuple-element.40.hid, bf16[2240,256]{1,0:T(8,128)(2,1)S(1)} %get-tuple-element.41.slope, bf16[2560,768]{1,0:T(8,128)(2,1)S(1)} %get-tuple-element.34.xs, ...), custom_call_target="tpu_custom_call", output_to_operand_aliasing={{0}: (6, {}), {1}: (7, {})} | custom-call | flops 1509949440 | bytes 4194304 | tf_op jit(solution)/shard_map/pallas_call | solution.py:382
  29.5 0.2 convert_add_fusion
  29.7 0.1 collective-permute-start.7
  29.8 0.2 convert_add_fusion.1
  30.0 0.1 collective-permute-start.3
  30.2 3.0 %shard_map.82 = (bf16[12,160,256]{2,1,0:T(8,128)(2,1)}, bf16[12,160,256]{2,1,0:T(8,128)(2,1)}) custom-call(bf16[2240,256]{1,0:T(8,128)(2,1)S(1)} %get-tuple-element.40.hid, bf16[2240,256]{1,0:T(8,128)(2,1)S(1)} %get-tuple-element.41.slope, bf16[2560,768]{1,0:T(8,128)(2,1)S(1)} %get-tuple-element.34.xs, ...), custom_call_target="tpu_custom_call", output_to_operand_aliasing={{0}: (6, {}), {1}: (7, {})} | custom-call | flops 1509949440 | bytes 4194304 | tf_op jit(solution)/shard_map/pallas_call | solution.py:382
  33.2 5.5 %collective-permute-done.7 = bf16[4,9,16,256]{3,2,1,0:T(8,128)(2,1)S(1)} collective-permute-done((bf16[4,9,16,256]{3,2,1,0:T(8,128)(2,1)S(1)}, bf16[4,9,16,256]{3,2,1,0:T(8,128)(2,1)S(1)}, u32[]{:S(2)}, u32[]{:S(2)}) %collective-permute-start.7) | collective-permute-done | bytes 294944 | tf_op jit(solution)/shard_map/ppermute | solution.py:298
  38.7 0.1 slice_add_fusion
  38.8 0.1 collective-permute-start.8
  38.9 0.1 collective-permute-done.3
  39.0 0.1 slice_add_fusion.1
  39.2 1.8 %collective-permute-start.4 = (bf16[2,9,16,256]{3,2,1,0:T(8,128)(2,1)S(1)}, bf16[2,9,16,256]{3,2,1,0:T(8,128)(2,1)S(1)}, u32[]{:S(2)}, u32[]{:S(2)}) collective-permute-start(bf16[2,9,16,256]{3,2,1,0:T(8,128)(2,1)S(1)} %slice.85), channel_id=1, source_target_pairs={{0,2},{1,3},{2,0},{3,1},{4,6},{5,7},{6,4},{7,5},{8,10},{9,11},{10,... | collective-permute-start | bytes 442376 | tf_op jit(solution)/shard_map/ppermute | solution.py:298
  41.0 3.1 %collective-permute-done.8 = bf16[2,9,16,256]{3,2,1,0:T(8,128)(2,1)S(1)} collective-permute-done((bf16[2,9,16,256]{3,2,1,0:T(8,128)(2,1)S(1)}, bf16[2,9,16,256]{3,2,1,0:T(8,128)(2,1)S(1)}, u32[]{:S(2)}, u32[]{:S(2)}) %collective-permute-start.8) | collective-permute-done | bytes 147488 | tf_op jit(solution)/shard_map/ppermute | solution.py:298
  44.1 0.3 collective-permute-start.9
  44.4 2.8 %collective-permute-start.5 = (bf16[1,9,16,256]{3,2,1,0:T(8,128)(2,1)S(1)}, bf16[1,9,16,256]{3,2,1,0:T(8,128)(2,1)S(1)}, u32[]{:S(2)}, u32[]{:S(2)}) collective-permute-start(bf16[1,9,16,256]{3,2,1,0:T(8,128)(2,1)S(1)} %slice.87), channel_id=1, source_target_pairs={{0,8},{1,9},{2,10},{3,11},{4,12},{5,13},{6,14},{7,15},{8,0},{9,1},... | collective-permute-start | bytes 221192 | tf_op jit(solution)/shard_map/ppermute | solution.py:298
  47.2 4.0 %collective-permute-done.9 = bf16[1,9,16,256]{3,2,1,0:T(8,128)(2,1)S(1)} collective-permute-done((bf16[1,9,16,256]{3,2,1,0:T(8,128)(2,1)S(1)}, bf16[1,9,16,256]{3,2,1,0:T(8,128)(2,1)S(1)}, u32[]{:S(2)}, u32[]{:S(2)}) %collective-permute-start.9) | collective-permute-done | bytes 73760 | tf_op jit(solution)/shard_map/ppermute | solution.py:298
  51.2 0.7 %fusion = f32[16,9,256]{2,0,1:T(8,128)} fusion(f32[2,9,16,256]{3,2,1,0:T(8,128)S(1)} %slice_add_fusion.2, bf16[1,9,16,256]{3,2,1,0:T(8,128)(2,1)S(1)} %collective-permute-done.9), kind=kLoop, calls=%fused_computation.12 | loop fusion | flops 73728 | bytes 368640 | tf_op jit(solution)/shard_map/transpose | solution.py:304
  51.9 0.1 collective-permute-done.5
  52.0 0.7 %fusion.1 = f32[16,9,256]{2,0,1:T(8,128)} fusion(f32[2,9,16,256]{3,2,1,0:T(8,128)S(1)} %slice_add_fusion.3, bf16[1,9,16,256]{3,2,1,0:T(8,128)(2,1)S(1)} %collective-permute-done.5), kind=kLoop, calls=%fused_computation.15 | loop fusion | flops 73728 | bytes 368640 | tf_op jit(solution)/shard_map/transpose | solution.py:304
  (14 shorter events, 0.2 us)
Async XLA Ops:
  0.6 7.5 %copy-start = (bf16[256,9,256]{2,0,1:T(8,128)(2,1)S(1)}, bf16[256,9,256]{2,0,1:T(8,128)(2,1)}, u32[]{:S(2)}) copy-start(bf16[256,9,256]{2,0,1:T(8,128)(2,1)} %param.6) | copy-start | bytes 3538948
  1.9 14.6 %collective-permute-start = (bf16[4,160,256]{2,1,0:T(8,128)(2,1)S(1)}, bf16[4,160,256]{2,1,0:T(8,128)(2,1)S(1)}, u32[]{:S(2)}, u32[]{:S(2)}) collective-permute-start(bf16[4,160,256]{2,1,0:T(8,128)(2,1)S(1)} %get-tuple-element.28), channel_id=1, source_target_pairs={{0,1},{1,0},{2,3},{3,2},{4,5},{5,4},{6,7},{7,6},{8,9},{9,8},{10,11... | collective-permute-start | bytes 983048 | tf_op jit(solution)/shard_map/ppermute | solution.py:342
  2.5 14.1 %collective-permute-start.1 = (bf16[4,160,256]{2,1,0:T(8,128)(2,1)S(1)}, bf16[4,160,256]{2,1,0:T(8,128)(2,1)S(1)}, u32[]{:S(2)}, u32[]{:S(2)}) collective-permute-start(bf16[4,160,256]{2,1,0:T(8,128)(2,1)S(1)} %get-tuple-element.29), channel_id=1, source_target_pairs={{1,2},{3,4},{5,6},{7,8},{9,10},{11,12},{13,14},{15,0},{2,1},{4,3},... | collective-permute-start | bytes 983048 | tf_op jit(solution)/shard_map/ppermute | solution.py:341
  16.6 2.1 %copy-start.1 = (bf16[256,9,256]{2,0,1:T(8,128)(2,1)S(1)}, bf16[256,9,256]{2,0,1:T(8,128)(2,1)}, u32[]{:S(2)}) copy-start(bf16[256,9,256]{2,0,1:T(8,128)(2,1)} %param.7) | copy-start | bytes 3538948
  18.6 10.8 %collective-permute-start.6 = (bf16[8,9,16,256]{3,2,1,0:T(8,128)(2,1)S(1)}, bf16[8,9,16,256]{3,2,1,0:T(8,128)(2,1)S(1)}, u32[]{:S(2)}, u32[]{:S(2)}) collective-permute-start(bf16[8,9,16,256]{3,2,1,0:T(8,128)(2,1)S(1)} %get-tuple-element.51), channel_id=1, source_target_pairs={{0,1},{1,0},{2,3},{3,2},{4,5},{5,4},{6,7},{7,6},{8,9},{9,8},{10,11... | collective-permute-start | bytes 1769480 | tf_op jit(solution)/shard_map/ppermute | solution.py:298
  21.9 7.9 %collective-permute-start.2 = (bf16[8,9,16,256]{3,2,1,0:T(8,128)(2,1)S(1)}, bf16[8,9,16,256]{3,2,1,0:T(8,128)(2,1)S(1)}, u32[]{:S(2)}, u32[]{:S(2)}) collective-permute-start(bf16[8,9,16,256]{3,2,1,0:T(8,128)(2,1)S(1)} %get-tuple-element.49), channel_id=1, source_target_pairs={{0,1},{1,0},{2,3},{3,2},{4,5},{5,4},{6,7},{7,6},{8,9},{9,8},{10,11... | collective-permute-start | bytes 1769480 | tf_op jit(solution)/shard_map/ppermute | solution.py:298
  29.7 9.0 %collective-permute-start.7 = (bf16[4,9,16,256]{3,2,1,0:T(8,128)(2,1)S(1)}, bf16[4,9,16,256]{3,2,1,0:T(8,128)(2,1)S(1)}, u32[]{:S(2)}, u32[]{:S(2)}) collective-permute-start(bf16[4,9,16,256]{3,2,1,0:T(8,128)(2,1)S(1)} %slice.82), channel_id=1, source_target_pairs={{0,2},{1,3},{2,0},{3,1},{4,6},{5,7},{6,4},{7,5},{8,10},{9,11},{10,... | collective-permute-start | bytes 884744 | tf_op jit(solution)/shard_map/ppermute | solution.py:298
  30.0 9.0 %collective-permute-start.3 = (bf16[4,9,16,256]{3,2,1,0:T(8,128)(2,1)S(1)}, bf16[4,9,16,256]{3,2,1,0:T(8,128)(2,1)S(1)}, u32[]{:S(2)}, u32[]{:S(2)}) collective-permute-start(bf16[4,9,16,256]{3,2,1,0:T(8,128)(2,1)S(1)} %slice.83), channel_id=1, source_target_pairs={{0,4},{1,5},{2,6},{3,7},{4,0},{5,1},{6,2},{7,3},{8,12},{9,13},{10,... | collective-permute-start | bytes 884744 | tf_op jit(solution)/shard_map/ppermute | solution.py:298
  38.8 5.2 %collective-permute-start.8 = (bf16[2,9,16,256]{3,2,1,0:T(8,128)(2,1)S(1)}, bf16[2,9,16,256]{3,2,1,0:T(8,128)(2,1)S(1)}, u32[]{:S(2)}, u32[]{:S(2)}) collective-permute-start(bf16[2,9,16,256]{3,2,1,0:T(8,128)(2,1)S(1)} %slice.84), channel_id=1, source_target_pairs={{0,4},{1,5},{2,6},{3,7},{4,0},{5,1},{6,2},{7,3},{8,12},{9,13},{10,... | collective-permute-start | bytes 442376 | tf_op jit(solution)/shard_map/ppermute | solution.py:298
  39.2 5.2 %collective-permute-start.4 = (bf16[2,9,16,256]{3,2,1,0:T(8,128)(2,1)S(1)}, bf16[2,9,16,256]{3,2,1,0:T(8,128)(2,1)S(1)}, u32[]{:S(2)}, u32[]{:S(2)}) collective-permute-start(bf16[2,9,16,256]{3,2,1,0:T(8,128)(2,1)S(1)} %slice.85), channel_id=1, source_target_pairs={{0,2},{1,3},{2,0},{3,1},{4,6},{5,7},{6,4},{7,5},{8,10},{9,11},{10,... | collective-permute-start | bytes 442376 | tf_op jit(solution)/shard_map/ppermute | solution.py:298
  44.1 7.1 %collective-permute-start.9 = (bf16[1,9,16,256]{3,2,1,0:T(8,128)(2,1)S(1)}, bf16[1,9,16,256]{3,2,1,0:T(8,128)(2,1)S(1)}, u32[]{:S(2)}, u32[]{:S(2)}) collective-permute-start(bf16[1,9,16,256]{3,2,1,0:T(8,128)(2,1)S(1)} %slice.86), channel_id=1, source_target_pairs={{0,8},{1,9},{2,10},{3,11},{4,12},{5,13},{6,14},{7,15},{8,0},{9,1},... | collective-permute-start | bytes 221192 | tf_op jit(solution)/shard_map/ppermute | solution.py:298
  44.4 7.5 %collective-permute-start.5 = (bf16[1,9,16,256]{3,2,1,0:T(8,128)(2,1)S(1)}, bf16[1,9,16,256]{3,2,1,0:T(8,128)(2,1)S(1)}, u32[]{:S(2)}, u32[]{:S(2)}) collective-permute-start(bf16[1,9,16,256]{3,2,1,0:T(8,128)(2,1)S(1)} %slice.87), channel_id=1, source_target_pairs={{0,8},{1,9},{2,10},{3,11},{4,12},{5,13},{6,14},{7,15},{8,0},{9,1},... | collective-permute-start | bytes 221192 | tf_op jit(solution)/shard_map/ppermute | solution.py:298

commit v5 on v4

--- a/solution.py
+++ b/solution.py
@@ -12,7 +12,7 @@
 BF16 = jnp.bfloat16
 WHOLE = pl.BlockSpec(memory_space=pltpu.VMEM)
 LIMIT = 20 << 20
-OUTPUT_PARTS = 3
+OUTPUT_PARTS = 4
 
 
 def struct(shape, dtype):
@@ -35,6 +35,17 @@
         copy.start()
     for copy in copies:
         copy.wait()
+
+
+def across_pairs(groups, n):
+    pairs = []
+    for group in range(groups):
+        base = group * n
+        pairs += [(base + i, base + i + 1) for i in range(1, n - 1, 2)]
+        pairs += [(base + i + 1, base + i) for i in range(1, n - 1, 2)]
+        twin = (group ^ 1) * n if groups % 2 == 0 else base
+        pairs += [(base, twin), (base + n - 1, twin + n - 1)]
+    return pairs
 
 
 def in_hbm(array):
@@ -337,8 +348,7 @@
         )(*(((me,) if place else ()) + tuple(args)))
 
     inside, across = pack(me, f, c)
-    pairs = [(i, (i + 1) % n) for i in range(1, n, 2)]
-    across = lax.ppermute(across, "tile", pairs + [(j, i) for i, j in pairs])
+    across = lax.ppermute(across, ("groups", "tile"), across_pairs(lax.axis_size("groups"), n))
     inside = lax.ppermute(inside, "tile", [(i, i ^ 1) for i in range(n)])
 
     windows = struct((size + 4 * cols, wide), BF16)

time: 52.8 us -> 52.5 us (level)
  waiting for transfers between devices: 12.8 us -> 8.87 us
  starting transfers between devices: 11.9 us -> 14.6 us
  Pallas kernels: 24.9 us -> 26 us
    ppermute x8, starting transfers between devices: 5.73 us -> 11.5 us  [halve(): got = lax.ppermute(send, 'tile', pairs)]
    ppermute x8, waiting for transfers between devices: 12.8 us -> 8.87 us  [halve(): got = lax.ppermute(send, 'tile', pairs)]
    ppermute x1, starting transfers between devices: 5.66 us -> 2.55 us  [layer(): lax.ppermute(across, ('groups', 'tile'), across_pairs(lax.axis_size('grou...]
    pallas_call x3 -> x4, Pallas kernels: 9.03 us -> 10.1 us  [layer(): pl.pallas_call(functools.partial(outputs_kernel, part * count), out_shape...]
  transfers between devices with their start and end apart: 10 -> 10, of which waited for: 5 -> 4; matrix products, arithmetic and copies ran while one was open for 3% -> 3% of each run, Pallas kernels for 41% -> 43%
where the time goes in v5:
time: 52.5 us; the launch traced here: 52.4 us
  Pallas kernels  26 us (50%)
  starting transfers between devices  14.6 us (28%)
  waiting for transfers between devices  8.87 us (17%)
  other arithmetic  1.98 us (4%)
  between operations  0.84 us (2%)
    pallas_call x4, Pallas kernels, call(): pl.pallas_call(kernel, out_shape=outs, in_specs=specs, out_specs=tuple((W...  14.6 us
    ppermute x8, starting transfers between devices, halve(): got = lax.ppermute(send, 'tile', pairs)  11.5 us
    pallas_call x4, Pallas kernels, layer(): pl.pallas_call(functools.partial(outputs_kernel, part * count), out_shape...  10.1 us
    ppermute x8, waiting for transfers between devices, halve(): got = lax.ppermute(send, 'tile', pairs)  8.87 us
    ppermute x1, starting transfers between devices, layer(): lax.ppermute(across, ('groups', 'tile'), across_pairs(lax.axis_size('grou...  2.55 us
    transpose x2, other arithmetic, halve(): return jnp.swapaxes(total[0], 0, 1)  1.36 us
    pallas_call x1, Pallas kernels, pack(): pl.pallas_call(pack_kernel, out_shape=(out,) * 2, in_specs=[pl.BlockSpec(...  1.28 us
  transfers between devices with their start and end apart: 10, of which 4 were waited for; matrix products, arithmetic and copies ran while one was open for 3% of the time, Pallas kernels for 43%

profile of v5, /device:TPU:0, one launch (start us, length us, event | category | flops | bytes accessed | tf_op | source)
XLA Modules:
  0.0 52.4 jit_solution(11246308354724139942)
XLA Ops:
  0.6 1.3 %shard_map.75 = (bf16[4,160,256]{2,1,0:T(8,128)(2,1)S(1)}, bf16[4,160,256]{2,1,0:T(8,128)(2,1)S(1)}) custom-call(s32[1]{0:T(128)} %bitcast.me_ref, bf16[12,160,256]{2,1,0:T(8,128)(2,1)} %bitcast.35, bf16[12,160,256]{2,1,0:T(8,128)(2,1)} %bitcast.37), custom_call_target="tpu_custom_call" | custom-call | tf_op jit(solution)/shard_map/pallas_call | solution.py:58
  1.9 0.6 %collective-permute-start = (bf16[4,160,256]{2,1,0:T(8,128)(2,1)S(1)}, bf16[4,160,256]{2,1,0:T(8,128)(2,1)S(1)}, u32[]{:S(2)}, u32[]{:S(2)}) collective-permute-start(bf16[4,160,256]{2,1,0:T(8,128)(2,1)S(1)} %get-tuple-element.30), channel_id=1, source_target_pairs={{0,1},{1,0},{2,3},{3,2},{4,5},{5,4},{6,7},{7,6},{8,9},{9,8},{10,11... | collective-permute-start | bytes 983048 | tf_op jit(solution)/shard_map/ppermute | solution.py:352
  2.5 2.6 %collective-permute-start.1 = (bf16[4,160,256]{2,1,0:T(8,128)(2,1)S(1)}, bf16[4,160,256]{2,1,0:T(8,128)(2,1)S(1)}, u32[]{:S(2)}, u32[]{:S(2)}) collective-permute-start(bf16[4,160,256]{2,1,0:T(8,128)(2,1)S(1)} %get-tuple-element.31), channel_id=1, source_target_pairs={{1,2},{3,4},{5,6},{7,8},{9,10},{11,12},{13,14},{2,1},{4,3},{6,5},{... | collective-permute-start | bytes 983048 | tf_op jit(solution)/shard_map/ppermute | solution.py:351
  5.0 8.4 %shard_map.76 = (bf16[2560,768]{1,0:T(8,128)(2,1)S(1)}, bf16[2560,768]{1,0:T(8,128)(2,1)S(1)}, bf16[2240,256]{1,0:T(8,128)(2,1)S(1)}, bf16[2240,256]{1,0:T(8,128)(2,1)S(1)}, f32[3,256,768]{2,1,0:T(8,128)S(1)}) custom-call(bf16[12,160,256]{2,1,0:T(8,128)(2,1)} %bitcast.36, bf16[12,160,256]{2,1,0:T(8,128)(2,1)} %bitcast.38, bf16[2304,256]{1,0:T(8,128)(2,1)} %bitcast.26, ...), custom_call_target="tpu_custom_call" | custom-call | flops 6794772480 | bytes 4194304 | tf_op jit(solution)/shard_map/pallas_call | solution.py:339
  13.4 0.0 collective-permute-done.inside
  13.5 0.0 collective-permute-done.1.across
  13.5 0.0 copy-start.1
  13.5 2.0 %shard_map.77 = (bf16[2560,768]{1,0:T(8,128)(2,1)S(1)}, bf16[2560,768]{1,0:T(8,128)(2,1)S(1)}, bf16[2240,256]{1,0:T(8,128)(2,1)S(1)}, f32[320,256]{1,0:T(8,128)S...) custom-call(s32[1]{0:T(128)} %bitcast.me_ref, ...), custom_call_target="tpu_custom_call", output_to_operand_aliasing={{0}: (4, {}), {1}: (5, {}), {2}: (6, {})} | custom-call | flops 2264924160 | bytes 4194304 | tf_op jit(solution)/shard_map/pallas_call | solution.py:339
  15.5 0.2 collective-permute-start.6
  15.7 3.2 %shard_map.78 = (bf16[2240,256]{1,0:T(8,128)(2,1)S(1)}, f32[8,9,16,256]{3,2,1,0:T(8,128)S(1)}, bf16[8,9,16,256]{3,2,1,0:T(8,128)(2,1)S(1)}) custom-call(s32[1]{0:T(128)} %bitcast.me_ref, bf16[2560,768]{1,0:T(8,128)(2,1)S(1)} %get-tuple-element.36.xs, bf16[2560,768]{1,0:T(8,128)(2,1)S(1)} %get-tuple-element.37.cs, ...), custom_call_target="tpu_custom_call", output_to_operand_aliasing={{0}: (5, {})} | custom-call | flops 2264924160 | bytes 4194304 | tf_op jit(solution)/shard_map/pallas_call | solution.py:339
  18.9 0.4 collective-permute-start.2
  19.3 1.0 %shard_map.79 = (bf16[2240,256]{1,0:T(8,128)(2,1)S(1)}, bf16[2240,256]{1,0:T(8,128)(2,1)S(1)}) custom-call(s32[1]{0:T(128)} %bitcast.me_ref, bf16[2560,768]{1,0:T(8,128)(2,1)S(1)} %get-tuple-element.36.xs, bf16[2560,768]{1,0:T(8,128)(2,1)S(1)} %get-tuple-element.37.cs, bf16[2304,256]{1,0:T(8,128)(2,1)S(1)} %bitcast.21, ...), custom_call_target="tpu_custom_call", output_to_operand_aliasing={{0}: (5, {}), {1}: (6, {})} | custom-call | flops 2264924160 | bytes 4194304 | tf_op jit(solution)/shard_map/pallas_call | solution.py:339
  20.3 2.5 %shard_map.80 = (bf16[12,160,256]{2,1,0:T(8,128)(2,1)}, bf16[12,160,256]{2,1,0:T(8,128)(2,1)}) custom-call(bf16[2240,256]{1,0:T(8,128)(2,1)S(1)} %get-tuple-element.42.hid, bf16[2240,256]{1,0:T(8,128)(2,1)S(1)} %get-tuple-element.43.slope, bf16[2560,768]{1,0:T(8,128)(2,1)S(1)} %get-tuple-element.36.xs, bf16[2560,768]{1,0:T(8,128)(2,1)S(1)} %get-tuple-element.37.cs, ...), custom_call_target="tpu_custom_call" | custom-call | flops 1132462080 | bytes 4194304 | tf_op jit(solution)/shard_map/pallas_call | solution.py:392
  22.8 2.5 %shard_map.81 = (bf16[12,160,256]{2,1,0:T(8,128)(2,1)}, bf16[12,160,256]{2,1,0:T(8,128)(2,1)}) custom-call(bf16[2240,256]{1,0:T(8,128)(2,1)S(1)} %get-tuple-element.42.hid, bf16[2240,256]{1,0:T(8,128)(2,1)S(1)} %get-tuple-element.43.slope, bf16[2560,768]{1,0:T(8,128)(2,1)S(1)} %get-tuple-element.36.xs, ...), custom_call_target="tpu_custom_call", output_to_operand_aliasing={{0}: (6, {}), {1}: (7, {})} | custom-call | flops 1132462080 | bytes 4194304 | tf_op jit(solution)/shard_map/pallas_call | solution.py:392
  25.3 2.7 %shard_map.82 = (bf16[12,160,256]{2,1,0:T(8,128)(2,1)}, bf16[12,160,256]{2,1,0:T(8,128)(2,1)}) custom-call(bf16[2240,256]{1,0:T(8,128)(2,1)S(1)} %get-tuple-element.42.hid, bf16[2240,256]{1,0:T(8,128)(2,1)S(1)} %get-tuple-element.43.slope, bf16[2560,768]{1,0:T(8,128)(2,1)S(1)} %get-tuple-element.36.xs, ...), custom_call_target="tpu_custom_call", output_to_operand_aliasing={{0}: (6, {}), {1}: (7, {})} | custom-call | flops 1132462080 | bytes 4194304 | tf_op jit(solution)/shard_map/pallas_call | solution.py:392
  28.0 0.2 convert_add_fusion
  28.2 1.7 %collective-permute-start.7 = (bf16[4,9,16,256]{3,2,1,0:T(8,128)(2,1)S(1)}, bf16[4,9,16,256]{3,2,1,0:T(8,128)(2,1)S(1)}, u32[]{:S(2)}, u32[]{:S(2)}) collective-permute-start(bf16[4,9,16,256]{3,2,1,0:T(8,128)(2,1)S(1)} %slice.82), channel_id=1, source_target_pairs={{0,2},{1,3},{2,0},{3,1},{4,6},{5,7},{6,4},{7,5},{8,10},{9,11},{10,... | collective-permute-start | bytes 884744 | tf_op jit(solution)/shard_map/ppermute | solution.py:309
  29.9 0.2 convert_add_fusion.1
  30.2 1.6 %collective-permute-start.3 = (bf16[4,9,16,256]{3,2,1,0:T(8,128)(2,1)S(1)}, bf16[4,9,16,256]{3,2,1,0:T(8,128)(2,1)S(1)}, u32[]{:S(2)}, u32[]{:S(2)}) collective-permute-start(bf16[4,9,16,256]{3,2,1,0:T(8,128)(2,1)S(1)} %slice.83), channel_id=1, source_target_pairs={{0,4},{1,5},{2,6},{3,7},{4,0},{5,1},{6,2},{7,3},{8,12},{9,13},{10,... | collective-permute-start | bytes 884744 | tf_op jit(solution)/shard_map/ppermute | solution.py:309
  31.8 2.5 %shard_map.83 = (bf16[12,160,256]{2,1,0:T(8,128)(2,1)}, bf16[12,160,256]{2,1,0:T(8,128)(2,1)}) custom-call(bf16[2240,256]{1,0:T(8,128)(2,1)S(1)} %get-tuple-element.42.hid, bf16[2240,256]{1,0:T(8,128)(2,1)S(1)} %get-tuple-element.43.slope, bf16[2560,768]{1,0:T(8,128)(2,1)S(1)} %get-tuple-element.36.xs, ...), custom_call_target="tpu_custom_call", output_to_operand_aliasing={{0}: (6, {}), {1}: (7, {})} | custom-call | flops 1132462080 | bytes 4194304 | tf_op jit(solution)/shard_map/pallas_call | solution.py:392
  34.3 3.1 %collective-permute-done.7 = bf16[4,9,16,256]{3,2,1,0:T(8,128)(2,1)S(1)} collective-permute-done((bf16[4,9,16,256]{3,2,1,0:T(8,128)(2,1)S(1)}, bf16[4,9,16,256]{3,2,1,0:T(8,128)(2,1)S(1)}, u32[]{:S(2)}, u32[]{:S(2)}) %collective-permute-start.7) | collective-permute-done | bytes 294944 | tf_op jit(solution)/shard_map/ppermute | solution.py:309
  37.4 0.1 slice_add_fusion
  37.5 2.0 %collective-permute-start.8 = (bf16[2,9,16,256]{3,2,1,0:T(8,128)(2,1)S(1)}, bf16[2,9,16,256]{3,2,1,0:T(8,128)(2,1)S(1)}, u32[]{:S(2)}, u32[]{:S(2)}) collective-permute-start(bf16[2,9,16,256]{3,2,1,0:T(8,128)(2,1)S(1)} %slice.84), channel_id=1, source_target_pairs={{0,4},{1,5},{2,6},{3,7},{4,0},{5,1},{6,2},{7,3},{8,12},{9,13},{10,... | collective-permute-start | bytes 442376 | tf_op jit(solution)/shard_map/ppermute | solution.py:309
  39.5 0.1 slice_add_fusion.1
  39.6 1.2 %collective-permute-start.4 = (bf16[2,9,16,256]{3,2,1,0:T(8,128)(2,1)S(1)}, bf16[2,9,16,256]{3,2,1,0:T(8,128)(2,1)S(1)}, u32[]{:S(2)}, u32[]{:S(2)}) collective-permute-start(bf16[2,9,16,256]{3,2,1,0:T(8,128)(2,1)S(1)} %slice.85), channel_id=1, source_target_pairs={{0,2},{1,3},{2,0},{3,1},{4,6},{5,7},{6,4},{7,5},{8,10},{9,11},{10,... | collective-permute-start | bytes 442376 | tf_op jit(solution)/shard_map/ppermute | solution.py:309
  40.8 2.3 %collective-permute-done.8 = bf16[2,9,16,256]{3,2,1,0:T(8,128)(2,1)S(1)} collective-permute-done((bf16[2,9,16,256]{3,2,1,0:T(8,128)(2,1)S(1)}, bf16[2,9,16,256]{3,2,1,0:T(8,128)(2,1)S(1)}, u32[]{:S(2)}, u32[]{:S(2)}) %collective-permute-start.8) | collective-permute-done | bytes 147488 | tf_op jit(solution)/shard_map/ppermute | solution.py:309
  43.2 2.8 %collective-permute-start.9 = (bf16[1,9,16,256]{3,2,1,0:T(8,128)(2,1)S(1)}, bf16[1,9,16,256]{3,2,1,0:T(8,128)(2,1)S(1)}, u32[]{:S(2)}, u32[]{:S(2)}) collective-permute-start(bf16[1,9,16,256]{3,2,1,0:T(8,128)(2,1)S(1)} %slice.86), channel_id=1, source_target_pairs={{0,8},{1,9},{2,10},{3,11},{4,12},{5,13},{6,14},{7,15},{8,0},{9,1},... | collective-permute-start | bytes 221192 | tf_op jit(solution)/shard_map/ppermute | solution.py:309
  46.1 1.5 %collective-permute-start.5 = (bf16[1,9,16,256]{3,2,1,0:T(8,128)(2,1)S(1)}, bf16[1,9,16,256]{3,2,1,0:T(8,128)(2,1)S(1)}, u32[]{:S(2)}, u32[]{:S(2)}) collective-permute-start(bf16[1,9,16,256]{3,2,1,0:T(8,128)(2,1)S(1)} %slice.87), channel_id=1, source_target_pairs={{0,8},{1,9},{2,10},{3,11},{4,12},{5,13},{6,14},{7,15},{8,0},{9,1},... | collective-permute-start | bytes 221192 | tf_op jit(solution)/shard_map/ppermute | solution.py:309
  47.6 1.4 %collective-permute-done.9 = bf16[1,9,16,256]{3,2,1,0:T(8,128)(2,1)S(1)} collective-permute-done((bf16[1,9,16,256]{3,2,1,0:T(8,128)(2,1)S(1)}, bf16[1,9,16,256]{3,2,1,0:T(8,128)(2,1)S(1)}, u32[]{:S(2)}, u32[]{:S(2)}) %collective-permute-start.9) | collective-permute-done | bytes 73760 | tf_op jit(solution)/shard_map/ppermute | solution.py:309
  48.9 0.7 %fusion = f32[16,9,256]{2,0,1:T(8,128)} fusion(f32[2,9,16,256]{3,2,1,0:T(8,128)S(1)} %slice_add_fusion.2, bf16[1,9,16,256]{3,2,1,0:T(8,128)(2,1)S(1)} %collective-permute-done.9), kind=kLoop, calls=%fused_computation.12 | loop fusion | flops 73728 | bytes 368640 | tf_op jit(solution)/shard_map/transpose | solution.py:315
  49.6 2.1 %collective-permute-done.5 = bf16[1,9,16,256]{3,2,1,0:T(8,128)(2,1)S(1)} collective-permute-done((bf16[1,9,16,256]{3,2,1,0:T(8,128)(2,1)S(1)}, bf16[1,9,16,256]{3,2,1,0:T(8,128)(2,1)S(1)}, u32[]{:S(2)}, u32[]{:S(2)}) %collective-permute-start.5) | collective-permute-done | bytes 73760 | tf_op jit(solution)/shard_map/ppermute | solution.py:309
  51.7 0.7 %fusion.1 = f32[16,9,256]{2,0,1:T(8,128)} fusion(f32[2,9,16,256]{3,2,1,0:T(8,128)S(1)} %slice_add_fusion.3, bf16[1,9,16,256]{3,2,1,0:T(8,128)(2,1)S(1)} %collective-permute-done.5), kind=kLoop, calls=%fused_computation.15 | loop fusion | flops 73728 | bytes 368640 | tf_op jit(solution)/shard_map/transpose | solution.py:315
  (15 shorter events, 0.2 us)
Async XLA Ops:
  0.6 4.4 %copy-start = (bf16[256,9,256]{2,0,1:T(8,128)(2,1)S(1)}, bf16[256,9,256]{2,0,1:T(8,128)(2,1)}, u32[]{:S(2)}) copy-start(bf16[256,9,256]{2,0,1:T(8,128)(2,1)} %param.6) | copy-start | bytes 3538948
  1.9 11.5 %collective-permute-start = (bf16[4,160,256]{2,1,0:T(8,128)(2,1)S(1)}, bf16[4,160,256]{2,1,0:T(8,128)(2,1)S(1)}, u32[]{:S(2)}, u32[]{:S(2)}) collective-permute-start(bf16[4,160,256]{2,1,0:T(8,128)(2,1)S(1)} %get-tuple-element.30), channel_id=1, source_target_pairs={{0,1},{1,0},{2,3},{3,2},{4,5},{5,4},{6,7},{7,6},{8,9},{9,8},{10,11... | collective-permute-start | bytes 983048 | tf_op jit(solution)/shard_map/ppermute | solution.py:352
  2.5 11.0 %collective-permute-start.1 = (bf16[4,160,256]{2,1,0:T(8,128)(2,1)S(1)}, bf16[4,160,256]{2,1,0:T(8,128)(2,1)S(1)}, u32[]{:S(2)}, u32[]{:S(2)}) collective-permute-start(bf16[4,160,256]{2,1,0:T(8,128)(2,1)S(1)} %get-tuple-element.31), channel_id=1, source_target_pairs={{1,2},{3,4},{5,6},{7,8},{9,10},{11,12},{13,14},{2,1},{4,3},{6,5},{... | collective-permute-start | bytes 983048 | tf_op jit(solution)/shard_map/ppermute | solution.py:351
  13.5 2.3 %copy-start.1 = (bf16[256,9,256]{2,0,1:T(8,128)(2,1)S(1)}, bf16[256,9,256]{2,0,1:T(8,128)(2,1)}, u32[]{:S(2)}) copy-start(bf16[256,9,256]{2,0,1:T(8,128)(2,1)} %param.7) | copy-start | bytes 3538948
  15.5 12.5 %collective-permute-start.6 = (bf16[8,9,16,256]{3,2,1,0:T(8,128)(2,1)S(1)}, bf16[8,9,16,256]{3,2,1,0:T(8,128)(2,1)S(1)}, u32[]{:S(2)}, u32[]{:S(2)}) collective-permute-start(bf16[8,9,16,256]{3,2,1,0:T(8,128)(2,1)S(1)} %get-tuple-element.55), channel_id=1, source_target_pairs={{0,1},{1,0},{2,3},{3,2},{4,5},{5,4},{6,7},{7,6},{8,9},{9,8},{10,11... | collective-permute-start | bytes 1769480 | tf_op jit(solution)/shard_map/ppermute | solution.py:309
  18.9 11.0 %collective-permute-start.2 = (bf16[8,9,16,256]{3,2,1,0:T(8,128)(2,1)S(1)}, bf16[8,9,16,256]{3,2,1,0:T(8,128)(2,1)S(1)}, u32[]{:S(2)}, u32[]{:S(2)}) collective-permute-start(bf16[8,9,16,256]{3,2,1,0:T(8,128)(2,1)S(1)} %get-tuple-element.53), channel_id=1, source_target_pairs={{0,1},{1,0},{2,3},{3,2},{4,5},{5,4},{6,7},{7,6},{8,9},{9,8},{10,11... | collective-permute-start | bytes 1769480 | tf_op jit(solution)/shard_map/ppermute | solution.py:309
  28.2 9.1 %collective-permute-start.7 = (bf16[4,9,16,256]{3,2,1,0:T(8,128)(2,1)S(1)}, bf16[4,9,16,256]{3,2,1,0:T(8,128)(2,1)S(1)}, u32[]{:S(2)}, u32[]{:S(2)}) collective-permute-start(bf16[4,9,16,256]{3,2,1,0:T(8,128)(2,1)S(1)} %slice.82), channel_id=1, source_target_pairs={{0,2},{1,3},{2,0},{3,1},{4,6},{5,7},{6,4},{7,5},{8,10},{9,11},{10,... | collective-permute-start | bytes 884744 | tf_op jit(solution)/shard_map/ppermute | solution.py:309
  30.2 9.3 %collective-permute-start.3 = (bf16[4,9,16,256]{3,2,1,0:T(8,128)(2,1)S(1)}, bf16[4,9,16,256]{3,2,1,0:T(8,128)(2,1)S(1)}, u32[]{:S(2)}, u32[]{:S(2)}) collective-permute-start(bf16[4,9,16,256]{3,2,1,0:T(8,128)(2,1)S(1)} %slice.83), channel_id=1, source_target_pairs={{0,4},{1,5},{2,6},{3,7},{4,0},{5,1},{6,2},{7,3},{8,12},{9,13},{10,... | collective-permute-start | bytes 884744 | tf_op jit(solution)/shard_map/ppermute | solution.py:309
  37.5 5.7 %collective-permute-start.8 = (bf16[2,9,16,256]{3,2,1,0:T(8,128)(2,1)S(1)}, bf16[2,9,16,256]{3,2,1,0:T(8,128)(2,1)S(1)}, u32[]{:S(2)}, u32[]{:S(2)}) collective-permute-start(bf16[2,9,16,256]{3,2,1,0:T(8,128)(2,1)S(1)} %slice.84), channel_id=1, source_target_pairs={{0,4},{1,5},{2,6},{3,7},{4,0},{5,1},{6,2},{7,3},{8,12},{9,13},{10,... | collective-permute-start | bytes 442376 | tf_op jit(solution)/shard_map/ppermute | solution.py:309
  39.6 6.4 %collective-permute-start.4 = (bf16[2,9,16,256]{3,2,1,0:T(8,128)(2,1)S(1)}, bf16[2,9,16,256]{3,2,1,0:T(8,128)(2,1)S(1)}, u32[]{:S(2)}, u32[]{:S(2)}) collective-permute-start(bf16[2,9,16,256]{3,2,1,0:T(8,128)(2,1)S(1)} %slice.85), channel_id=1, source_target_pairs={{0,2},{1,3},{2,0},{3,1},{4,6},{5,7},{6,4},{7,5},{8,10},{9,11},{10,... | collective-permute-start | bytes 442376 | tf_op jit(solution)/shard_map/ppermute | solution.py:309
  43.2 5.7 %collective-permute-start.9 = (bf16[1,9,16,256]{3,2,1,0:T(8,128)(2,1)S(1)}, bf16[1,9,16,256]{3,2,1,0:T(8,128)(2,1)S(1)}, u32[]{:S(2)}, u32[]{:S(2)}) collective-permute-start(bf16[1,9,16,256]{3,2,1,0:T(8,128)(2,1)S(1)} %slice.86), channel_id=1, source_target_pairs={{0,8},{1,9},{2,10},{3,11},{4,12},{5,13},{6,14},{7,15},{8,0},{9,1},... | collective-permute-start | bytes 221192 | tf_op jit(solution)/shard_map/ppermute | solution.py:309
  46.1 5.6 %collective-permute-start.5 = (bf16[1,9,16,256]{3,2,1,0:T(8,128)(2,1)S(1)}, bf16[1,9,16,256]{3,2,1,0:T(8,128)(2,1)S(1)}, u32[]{:S(2)}, u32[]{:S(2)}) collective-permute-start(bf16[1,9,16,256]{3,2,1,0:T(8,128)(2,1)S(1)} %slice.87), channel_id=1, source_target_pairs={{0,8},{1,9},{2,10},{3,11},{4,12},{5,13},{6,14},{7,15},{8,0},{9,1},... | collective-permute-start | bytes 221192 | tf_op jit(solution)/shard_map/ppermute | solution.py:309

commit v6 on v5

--- a/solution.py
+++ b/solution.py
@@ -12,7 +12,8 @@
 BF16 = jnp.bfloat16
 WHOLE = pl.BlockSpec(memory_space=pltpu.VMEM)
 LIMIT = 20 << 20
-OUTPUT_PARTS = 4
+SHARES = (6, 6)
+PIECES = 4
 
 
 def struct(shape, dtype):
@@ -67,10 +68,9 @@
 
 def put_windows(dst, row, value, sign):
     cols, chans = value.shape
-    wide = value.astype(F32)
-    index = lax.broadcasted_iota(jnp.int32, (cols, chans), 0)
-    before = jnp.where(index == 0, 0.0, pltpu.roll(wide, 1, 0)).astype(BF16)
-    after = jnp.where(index == cols - 1, 0.0, pltpu.roll(wide, cols - 1, 0)).astype(BF16)
+    zero = jnp.zeros((1, chans), value.dtype)
+    before = jnp.concatenate([zero, value[: cols - 1]], axis=0)
+    after = jnp.concatenate([value[1:], zero], axis=0)
     here = pl.ds(pl.multiple_of(row * cols, cols), cols)
     low, high = (before, after) if sign > 0 else (after, before)
     dst[here, 0:chans] = low
@@ -185,17 +185,27 @@
 
 def inner_kernel(f_hbm, c_hbm, w_hbm, w_one, xs, cs, hid, slope, acc, f, c, w_two, sems):
     rows, cols, chans = f.shape
-    copy_f = pltpu.make_async_copy(f_hbm, f, sems.at[0])
-    copy_c = pltpu.make_async_copy(c_hbm, c, sems.at[1])
-    copy_w = pltpu.make_async_copy(w_hbm, w_two, sems.at[2])
-    copy_f.start()
-    copy_c.start()
-    copy_w.start()
-    copy_f.wait()
-    fill(xs, 2, rows, f, 0, 1)
-    copy_c.wait()
-    fill(cs, 2, rows, c, 0, -1)
-    copy_w.wait()
+    loads = []
+    for slot, (source, target) in enumerate(((f_hbm, f), (c_hbm, c), (w_hbm, w_two))):
+        piece = target.shape[0] // PIECES
+        loads.append([
+            pltpu.make_async_copy(
+                source.at[pl.ds(j * piece, piece)],
+                target.at[pl.ds(j * piece, piece)],
+                sems.at[slot * PIECES + j],
+            )
+            for j in range(PIECES)
+        ])
+    for group in loads:
+        for load in group:
+            load.start()
+    for dst, field, group, sign in ((xs, f, loads[0], 1), (cs, c, loads[1], -1)):
+        piece = rows // PIECES
+        for j, load in enumerate(group):
+            load.wait()
+            fill(dst, 2 + j * piece, piece, field, j * piece, sign)
+    for load in loads[2]:
+        load.wait()
     half = (rows - 2) // 2
     size = half * cols
 
@@ -360,7 +370,7 @@
         inner_kernel,
         (in_hbm(f), in_hbm(c), in_hbm(w_two), w_one),
         (windows, windows, field, field, struct((3, chans, wide), F32)),
-        [band, band, pltpu.VMEM(w_two.shape, BF16), pltpu.SemaphoreType.DMA((3,))],
+        [band, band, pltpu.VMEM(w_two.shape, BF16), pltpu.SemaphoreType.DMA((3 * PIECES,))],
         work=3 * flops,
         raw=3,
     )
@@ -385,12 +395,12 @@
         place=True,
         aliases={5: 0, 6: 1},
     )
-    parts = OUTPUT_PARTS if rows % OUTPUT_PARTS == 0 else 1
-    count = rows // parts
-    outs = ()
-    for part in range(parts):
+    shares = [rows * share // sum(SHARES) for share in SHARES]
+    shares[-1] = rows - sum(shares[:-1])
+    outs, first = (), 0
+    for count in shares:
         outs = pl.pallas_call(
-            functools.partial(outputs_kernel, part * count),
+            functools.partial(outputs_kernel, first),
             out_shape=(struct(f.shape, BF16), struct(c.shape, BF16)),
             in_specs=[WHOLE] * 6 + [hbm] * len(outs),
             out_specs=(hbm, hbm),
@@ -400,9 +410,10 @@
             input_output_aliases={6: 0, 7: 1} if outs else {},
             compiler_params=pltpu.CompilerParams(vmem_limit_bytes=LIMIT),
             cost_estimate=pl.CostEstimate(
-                flops=2 * flops // parts, bytes_accessed=4 << 20, transcendentals=0
+                flops=2 * flops * count // rows, bytes_accessed=4 << 20, transcendentals=0
             ),
         )(hid, slope, xs, cs, w_two, w_one, *outs)
+        first += count
     block_out, input_grad = outs
     grad_two = halve(keep_two, send_two, order_two, n)
     grad_one = halve(keep_one, send_one, order_one, n)

time: 52.5 us -> 48.8 us (0.930)
  Pallas kernels: 26 us -> 23.7 us
  waiting for transfers between devices: 8.87 us -> 7.32 us
    pallas_call x4 -> x2, Pallas kernels: 10.1 us -> 7.95 us  [layer(): pl.pallas_call(functools.partial(outputs_kernel, first), out_shape=(struc...]
    ppermute x8, waiting for transfers between devices: 8.87 us -> 7.31 us  [halve(): got = lax.ppermute(send, 'tile', pairs)]
  transfers between devices with their start and end apart: 10 -> 10, of which waited for: 4 -> 4; matrix products, arithmetic and copies ran while one was open for 3% -> 3% of each run, Pallas kernels for 43% -> 42%
where the time goes in v6:
time: 48.8 us; the launch traced here: 48.7 us
  Pallas kernels  23.7 us (49%)
  starting transfers between devices  14.7 us (30%)
  waiting for transfers between devices  7.32 us (15%)
  other arithmetic  1.98 us (4%)
  between operations  0.83 us (2%)
    pallas_call x4, Pallas kernels, call(): pl.pallas_call(kernel, out_shape=outs, in_specs=specs, out_specs=tuple((W...  14.4 us
    ppermute x8, starting transfers between devices, halve(): got = lax.ppermute(send, 'tile', pairs)  11.6 us
    pallas_call x2, Pallas kernels, layer(): pl.pallas_call(functools.partial(outputs_kernel, first), out_shape=(struc...  7.95 us
    ppermute x8, waiting for transfers between devices, halve(): got = lax.ppermute(send, 'tile', pairs)  7.31 us
    ppermute x1, starting transfers between devices, layer(): lax.ppermute(across, ('groups', 'tile'), across_pairs(lax.axis_size('grou...  2.55 us
    transpose x2, other arithmetic, halve(): return jnp.swapaxes(total[0], 0, 1)  1.36 us
    pallas_call x1, Pallas kernels, pack(): pl.pallas_call(pack_kernel, out_shape=(out,) * 2, in_specs=[pl.BlockSpec(...  1.28 us
  transfers between devices with their start and end apart: 10, of which 4 were waited for; matrix products, arithmetic and copies ran while one was open for 3% of the time, Pallas kernels for 42%

profile of v6, /device:TPU:0, one launch (start us, length us, event | category | flops | bytes accessed | tf_op | source)
XLA Modules:
  0.0 48.7 jit_solution(15667563426475042162)
XLA Ops:
  0.6 1.3 %shard_map.75 = (bf16[4,160,256]{2,1,0:T(8,128)(2,1)S(1)}, bf16[4,160,256]{2,1,0:T(8,128)(2,1)S(1)}) custom-call(s32[1]{0:T(128)} %bitcast.me_ref, bf16[12,160,256]{2,1,0:T(8,128)(2,1)} %bitcast.29, bf16[12,160,256]{2,1,0:T(8,128)(2,1)} %bitcast.31), custom_call_target="tpu_custom_call" | custom-call | tf_op jit(solution)/shard_map/pallas_call | solution.py:59
  1.9 0.6 %collective-permute-start = (bf16[4,160,256]{2,1,0:T(8,128)(2,1)S(1)}, bf16[4,160,256]{2,1,0:T(8,128)(2,1)S(1)}, u32[]{:S(2)}, u32[]{:S(2)}) collective-permute-start(bf16[4,160,256]{2,1,0:T(8,128)(2,1)S(1)} %get-tuple-element.26), channel_id=1, source_target_pairs={{0,1},{1,0},{2,3},{3,2},{4,5},{5,4},{6,7},{7,6},{8,9},{9,8},{10,11... | collective-permute-start | bytes 983048 | tf_op jit(solution)/shard_map/ppermute | solution.py:362
  2.5 2.6 %collective-permute-start.1 = (bf16[4,160,256]{2,1,0:T(8,128)(2,1)S(1)}, bf16[4,160,256]{2,1,0:T(8,128)(2,1)S(1)}, u32[]{:S(2)}, u32[]{:S(2)}) collective-permute-start(bf16[4,160,256]{2,1,0:T(8,128)(2,1)S(1)} %get-tuple-element.27), channel_id=1, source_target_pairs={{1,2},{3,4},{5,6},{7,8},{9,10},{11,12},{13,14},{2,1},{4,3},{6,5},{... | collective-permute-start | bytes 983048 | tf_op jit(solution)/shard_map/ppermute | solution.py:361
  5.0 8.3 %shard_map.76 = (bf16[2560,768]{1,0:T(8,128)(2,1)S(1)}, bf16[2560,768]{1,0:T(8,128)(2,1)S(1)}, bf16[2240,256]{1,0:T(8,128)(2,1)S(1)}, bf16[2240,256]{1,0:T(8,128)(2,1)S(1)}, f32[3,256,768]{2,1,0:T(8,128)S(1)}) custom-call(bf16[12,160,256]{2,1,0:T(8,128)(2,1)} %bitcast.30, bf16[12,160,256]{2,1,0:T(8,128)(2,1)} %bitcast.32, bf16[2304,256]{1,0:T(8,128)(2,1)} %bitcast.24, ...), custom_call_target="tpu_custom_call" | custom-call | flops 6794772480 | bytes 4194304 | tf_op jit(solution)/shard_map/pallas_call | solution.py:349
  13.4 0.0 collective-permute-done.inside
  13.4 0.0 collective-permute-done.1.across
  13.4 0.0 copy-start.1
  13.4 2.0 %shard_map.77 = (bf16[2560,768]{1,0:T(8,128)(2,1)S(1)}, bf16[2560,768]{1,0:T(8,128)(2,1)S(1)}, bf16[2240,256]{1,0:T(8,128)(2,1)S(1)}, f32[320,256]{1,0:T(8,128)S...) custom-call(s32[1]{0:T(128)} %bitcast.me_ref, ...), custom_call_target="tpu_custom_call", output_to_operand_aliasing={{0}: (4, {}), {1}: (5, {}), {2}: (6, {})} | custom-call | flops 2264924160 | bytes 4194304 | tf_op jit(solution)/shard_map/pallas_call | solution.py:349
  15.4 0.2 collective-permute-start.6
  15.6 3.2 %shard_map.78 = (bf16[2240,256]{1,0:T(8,128)(2,1)S(1)}, f32[8,9,16,256]{3,2,1,0:T(8,128)S(1)}, bf16[8,9,16,256]{3,2,1,0:T(8,128)(2,1)S(1)}) custom-call(s32[1]{0:T(128)} %bitcast.me_ref, bf16[2560,768]{1,0:T(8,128)(2,1)S(1)} %get-tuple-element.32.xs, bf16[2560,768]{1,0:T(8,128)(2,1)S(1)} %get-tuple-element.33.cs, ...), custom_call_target="tpu_custom_call", output_to_operand_aliasing={{0}: (5, {})} | custom-call | flops 2264924160 | bytes 4194304 | tf_op jit(solution)/shard_map/pallas_call | solution.py:349
  18.8 0.4 collective-permute-start.2
  19.2 1.0 %shard_map.79 = (bf16[2240,256]{1,0:T(8,128)(2,1)S(1)}, bf16[2240,256]{1,0:T(8,128)(2,1)S(1)}) custom-call(s32[1]{0:T(128)} %bitcast.me_ref, bf16[2560,768]{1,0:T(8,128)(2,1)S(1)} %get-tuple-element.32.xs, bf16[2560,768]{1,0:T(8,128)(2,1)S(1)} %get-tuple-element.33.cs, bf16[2304,256]{1,0:T(8,128)(2,1)S(1)} %bitcast.21, ...), custom_call_target="tpu_custom_call", output_to_operand_aliasing={{0}: (5, {}), {1}: (6, {})} | custom-call | flops 2264924160 | bytes 4194304 | tf_op jit(solution)/shard_map/pallas_call | solution.py:349
  20.2 4.0 %shard_map.80 = (bf16[12,160,256]{2,1,0:T(8,128)(2,1)}, bf16[12,160,256]{2,1,0:T(8,128)(2,1)}) custom-call(bf16[2240,256]{1,0:T(8,128)(2,1)S(1)} %get-tuple-element.38.hid, bf16[2240,256]{1,0:T(8,128)(2,1)S(1)} %get-tuple-element.39.slope, bf16[2560,768]{1,0:T(8,128)(2,1)S(1)} %get-tuple-element.32.xs, bf16[2560,768]{1,0:T(8,128)(2,1)S(1)} %get-tuple-element.33.cs, ...), custom_call_target="tpu_custom_call" | custom-call | flops 2264924160 | bytes 4194304 | tf_op jit(solution)/shard_map/pallas_call | solution.py:402
  24.2 0.0 collective-permute-done.6
  24.2 0.2 convert_add_fusion
  24.4 1.8 %collective-permute-start.7 = (bf16[4,9,16,256]{3,2,1,0:T(8,128)(2,1)S(1)}, bf16[4,9,16,256]{3,2,1,0:T(8,128)(2,1)S(1)}, u32[]{:S(2)}, u32[]{:S(2)}) collective-permute-start(bf16[4,9,16,256]{3,2,1,0:T(8,128)(2,1)S(1)} %slice.82), channel_id=1, source_target_pairs={{0,2},{1,3},{2,0},{3,1},{4,6},{5,7},{6,4},{7,5},{8,10},{9,11},{10,... | collective-permute-start | bytes 884744 | tf_op jit(solution)/shard_map/ppermute | solution.py:319
  26.2 0.0 collective-permute-done.2
  26.2 0.2 convert_add_fusion.1
  26.4 1.6 %collective-permute-start.3 = (bf16[4,9,16,256]{3,2,1,0:T(8,128)(2,1)S(1)}, bf16[4,9,16,256]{3,2,1,0:T(8,128)(2,1)S(1)}, u32[]{:S(2)}, u32[]{:S(2)}) collective-permute-start(bf16[4,9,16,256]{3,2,1,0:T(8,128)(2,1)S(1)} %slice.83), channel_id=1, source_target_pairs={{0,4},{1,5},{2,6},{3,7},{4,0},{5,1},{6,2},{7,3},{8,12},{9,13},{10,... | collective-permute-start | bytes 884744 | tf_op jit(solution)/shard_map/ppermute | solution.py:319
  28.1 4.0 %shard_map.81 = (bf16[12,160,256]{2,1,0:T(8,128)(2,1)}, bf16[12,160,256]{2,1,0:T(8,128)(2,1)}) custom-call(bf16[2240,256]{1,0:T(8,128)(2,1)S(1)} %get-tuple-element.38.hid, bf16[2240,256]{1,0:T(8,128)(2,1)S(1)} %get-tuple-element.39.slope, bf16[2560,768]{1,0:T(8,128)(2,1)S(1)} %get-tuple-element.32.xs, ...), custom_call_target="tpu_custom_call", output_to_operand_aliasing={{0}: (6, {}), {1}: (7, {})} | custom-call | flops 2264924160 | bytes 4194304 | tf_op jit(solution)/shard_map/pallas_call | solution.py:402
  32.1 1.5 %collective-permute-done.7 = bf16[4,9,16,256]{3,2,1,0:T(8,128)(2,1)S(1)} collective-permute-done((bf16[4,9,16,256]{3,2,1,0:T(8,128)(2,1)S(1)}, bf16[4,9,16,256]{3,2,1,0:T(8,128)(2,1)S(1)}, u32[]{:S(2)}, u32[]{:S(2)}) %collective-permute-start.7) | collective-permute-done | bytes 294944 | tf_op jit(solution)/shard_map/ppermute | solution.py:319
  33.5 0.1 slice_add_fusion
  33.7 2.1 %collective-permute-start.8 = (bf16[2,9,16,256]{3,2,1,0:T(8,128)(2,1)S(1)}, bf16[2,9,16,256]{3,2,1,0:T(8,128)(2,1)S(1)}, u32[]{:S(2)}, u32[]{:S(2)}) collective-permute-start(bf16[2,9,16,256]{3,2,1,0:T(8,128)(2,1)S(1)} %slice.84), channel_id=1, source_target_pairs={{0,4},{1,5},{2,6},{3,7},{4,0},{5,1},{6,2},{7,3},{8,12},{9,13},{10,... | collective-permute-start | bytes 442376 | tf_op jit(solution)/shard_map/ppermute | solution.py:319
  35.8 0.1 slice_add_fusion.1
  35.9 1.2 %collective-permute-start.4 = (bf16[2,9,16,256]{3,2,1,0:T(8,128)(2,1)S(1)}, bf16[2,9,16,256]{3,2,1,0:T(8,128)(2,1)S(1)}, u32[]{:S(2)}, u32[]{:S(2)}) collective-permute-start(bf16[2,9,16,256]{3,2,1,0:T(8,128)(2,1)S(1)} %slice.85), channel_id=1, source_target_pairs={{0,2},{1,3},{2,0},{3,1},{4,6},{5,7},{6,4},{7,5},{8,10},{9,11},{10,... | collective-permute-start | bytes 442376 | tf_op jit(solution)/shard_map/ppermute | solution.py:319
  37.1 2.4 %collective-permute-done.8 = bf16[2,9,16,256]{3,2,1,0:T(8,128)(2,1)S(1)} collective-permute-done((bf16[2,9,16,256]{3,2,1,0:T(8,128)(2,1)S(1)}, bf16[2,9,16,256]{3,2,1,0:T(8,128)(2,1)S(1)}, u32[]{:S(2)}, u32[]{:S(2)}) %collective-permute-start.8) | collective-permute-done | bytes 147488 | tf_op jit(solution)/shard_map/ppermute | solution.py:319
  39.5 2.8 %collective-permute-start.9 = (bf16[1,9,16,256]{3,2,1,0:T(8,128)(2,1)S(1)}, bf16[1,9,16,256]{3,2,1,0:T(8,128)(2,1)S(1)}, u32[]{:S(2)}, u32[]{:S(2)}) collective-permute-start(bf16[1,9,16,256]{3,2,1,0:T(8,128)(2,1)S(1)} %slice.86), channel_id=1, source_target_pairs={{0,8},{1,9},{2,10},{3,11},{4,12},{5,13},{6,14},{7,15},{8,0},{9,1},... | collective-permute-start | bytes 221192 | tf_op jit(solution)/shard_map/ppermute | solution.py:319
  42.4 1.5 %collective-permute-start.5 = (bf16[1,9,16,256]{3,2,1,0:T(8,128)(2,1)S(1)}, bf16[1,9,16,256]{3,2,1,0:T(8,128)(2,1)S(1)}, u32[]{:S(2)}, u32[]{:S(2)}) collective-permute-start(bf16[1,9,16,256]{3,2,1,0:T(8,128)(2,1)S(1)} %slice.87), channel_id=1, source_target_pairs={{0,8},{1,9},{2,10},{3,11},{4,12},{5,13},{6,14},{7,15},{8,0},{9,1},... | collective-permute-start | bytes 221192 | tf_op jit(solution)/shard_map/ppermute | solution.py:319
  43.8 1.4 %collective-permute-done.9 = bf16[1,9,16,256]{3,2,1,0:T(8,128)(2,1)S(1)} collective-permute-done((bf16[1,9,16,256]{3,2,1,0:T(8,128)(2,1)S(1)}, bf16[1,9,16,256]{3,2,1,0:T(8,128)(2,1)S(1)}, u32[]{:S(2)}, u32[]{:S(2)}) %collective-permute-start.9) | collective-permute-done | bytes 73760 | tf_op jit(solution)/shard_map/ppermute | solution.py:319
  45.2 0.7 %fusion = f32[16,9,256]{2,0,1:T(8,128)} fusion(f32[2,9,16,256]{3,2,1,0:T(8,128)S(1)} %slice_add_fusion.2, bf16[1,9,16,256]{3,2,1,0:T(8,128)(2,1)S(1)} %collective-permute-done.9), kind=kLoop, calls=%fused_computation.12 | loop fusion | flops 73728 | bytes 368640 | tf_op jit(solution)/shard_map/transpose | solution.py:325
  45.9 2.1 %collective-permute-done.5 = bf16[1,9,16,256]{3,2,1,0:T(8,128)(2,1)S(1)} collective-permute-done((bf16[1,9,16,256]{3,2,1,0:T(8,128)(2,1)S(1)}, bf16[1,9,16,256]{3,2,1,0:T(8,128)(2,1)S(1)}, u32[]{:S(2)}, u32[]{:S(2)}) %collective-permute-start.5) | collective-permute-done | bytes 73760 | tf_op jit(solution)/shard_map/ppermute | solution.py:319
  48.0 0.7 %fusion.1 = f32[16,9,256]{2,0,1:T(8,128)} fusion(f32[2,9,16,256]{3,2,1,0:T(8,128)S(1)} %slice_add_fusion.3, bf16[1,9,16,256]{3,2,1,0:T(8,128)(2,1)S(1)} %collective-permute-done.5), kind=kLoop, calls=%fused_computation.15 | loop fusion | flops 73728 | bytes 368640 | tf_op jit(solution)/shard_map/transpose | solution.py:325
  (13 shorter events, 0.2 us)
Async XLA Ops:
  0.6 4.4 %copy-start = (bf16[256,9,256]{2,0,1:T(8,128)(2,1)S(1)}, bf16[256,9,256]{2,0,1:T(8,128)(2,1)}, u32[]{:S(2)}) copy-start(bf16[256,9,256]{2,0,1:T(8,128)(2,1)} %param.6) | copy-start | bytes 3538948
  1.9 11.4 %collective-permute-start = (bf16[4,160,256]{2,1,0:T(8,128)(2,1)S(1)}, bf16[4,160,256]{2,1,0:T(8,128)(2,1)S(1)}, u32[]{:S(2)}, u32[]{:S(2)}) collective-permute-start(bf16[4,160,256]{2,1,0:T(8,128)(2,1)S(1)} %get-tuple-element.26), channel_id=1, source_target_pairs={{0,1},{1,0},{2,3},{3,2},{4,5},{5,4},{6,7},{7,6},{8,9},{9,8},{10,11... | collective-permute-start | bytes 983048 | tf_op jit(solution)/shard_map/ppermute | solution.py:362
  2.5 10.9 %collective-permute-start.1 = (bf16[4,160,256]{2,1,0:T(8,128)(2,1)S(1)}, bf16[4,160,256]{2,1,0:T(8,128)(2,1)S(1)}, u32[]{:S(2)}, u32[]{:S(2)}) collective-permute-start(bf16[4,160,256]{2,1,0:T(8,128)(2,1)S(1)} %get-tuple-element.27), channel_id=1, source_target_pairs={{1,2},{3,4},{5,6},{7,8},{9,10},{11,12},{13,14},{2,1},{4,3},{6,5},{... | collective-permute-start | bytes 983048 | tf_op jit(solution)/shard_map/ppermute | solution.py:361
  13.4 2.2 %copy-start.1 = (bf16[256,9,256]{2,0,1:T(8,128)(2,1)S(1)}, bf16[256,9,256]{2,0,1:T(8,128)(2,1)}, u32[]{:S(2)}) copy-start(bf16[256,9,256]{2,0,1:T(8,128)(2,1)} %param.7) | copy-start | bytes 3538948
  15.4 8.8 %collective-permute-start.6 = (bf16[8,9,16,256]{3,2,1,0:T(8,128)(2,1)S(1)}, bf16[8,9,16,256]{3,2,1,0:T(8,128)(2,1)S(1)}, u32[]{:S(2)}, u32[]{:S(2)}) collective-permute-start(bf16[8,9,16,256]{3,2,1,0:T(8,128)(2,1)S(1)} %get-tuple-element.47), channel_id=1, source_target_pairs={{0,1},{1,0},{2,3},{3,2},{4,5},{5,4},{6,7},{7,6},{8,9},{9,8},{10,11... | collective-permute-start | bytes 1769480 | tf_op jit(solution)/shard_map/ppermute | solution.py:319
  18.8 7.4 %collective-permute-start.2 = (bf16[8,9,16,256]{3,2,1,0:T(8,128)(2,1)S(1)}, bf16[8,9,16,256]{3,2,1,0:T(8,128)(2,1)S(1)}, u32[]{:S(2)}, u32[]{:S(2)}) collective-permute-start(bf16[8,9,16,256]{3,2,1,0:T(8,128)(2,1)S(1)} %get-tuple-element.45), channel_id=1, source_target_pairs={{0,1},{1,0},{2,3},{3,2},{4,5},{5,4},{6,7},{7,6},{8,9},{9,8},{10,11... | collective-permute-start | bytes 1769480 | tf_op jit(solution)/shard_map/ppermute | solution.py:319
  24.4 9.1 %collective-permute-start.7 = (bf16[4,9,16,256]{3,2,1,0:T(8,128)(2,1)S(1)}, bf16[4,9,16,256]{3,2,1,0:T(8,128)(2,1)S(1)}, u32[]{:S(2)}, u32[]{:S(2)}) collective-permute-start(bf16[4,9,16,256]{3,2,1,0:T(8,128)(2,1)S(1)} %slice.82), channel_id=1, source_target_pairs={{0,2},{1,3},{2,0},{3,1},{4,6},{5,7},{6,4},{7,5},{8,10},{9,11},{10,... | collective-permute-start | bytes 884744 | tf_op jit(solution)/shard_map/ppermute | solution.py:319
  26.4 9.3 %collective-permute-start.3 = (bf16[4,9,16,256]{3,2,1,0:T(8,128)(2,1)S(1)}, bf16[4,9,16,256]{3,2,1,0:T(8,128)(2,1)S(1)}, u32[]{:S(2)}, u32[]{:S(2)}) collective-permute-start(bf16[4,9,16,256]{3,2,1,0:T(8,128)(2,1)S(1)} %slice.83), channel_id=1, source_target_pairs={{0,4},{1,5},{2,6},{3,7},{4,0},{5,1},{6,2},{7,3},{8,12},{9,13},{10,... | collective-permute-start | bytes 884744 | tf_op jit(solution)/shard_map/ppermute | solution.py:319
  33.7 5.8 %collective-permute-start.8 = (bf16[2,9,16,256]{3,2,1,0:T(8,128)(2,1)S(1)}, bf16[2,9,16,256]{3,2,1,0:T(8,128)(2,1)S(1)}, u32[]{:S(2)}, u32[]{:S(2)}) collective-permute-start(bf16[2,9,16,256]{3,2,1,0:T(8,128)(2,1)S(1)} %slice.84), channel_id=1, source_target_pairs={{0,4},{1,5},{2,6},{3,7},{4,0},{5,1},{6,2},{7,3},{8,12},{9,13},{10,... | collective-permute-start | bytes 442376 | tf_op jit(solution)/shard_map/ppermute | solution.py:319
  35.9 6.4 %collective-permute-start.4 = (bf16[2,9,16,256]{3,2,1,0:T(8,128)(2,1)S(1)}, bf16[2,9,16,256]{3,2,1,0:T(8,128)(2,1)S(1)}, u32[]{:S(2)}, u32[]{:S(2)}) collective-permute-start(bf16[2,9,16,256]{3,2,1,0:T(8,128)(2,1)S(1)} %slice.85), channel_id=1, source_target_pairs={{0,2},{1,3},{2,0},{3,1},{4,6},{5,7},{6,4},{7,5},{8,10},{9,11},{10,... | collective-permute-start | bytes 442376 | tf_op jit(solution)/shard_map/ppermute | solution.py:319
  39.5 5.7 %collective-permute-start.9 = (bf16[1,9,16,256]{3,2,1,0:T(8,128)(2,1)S(1)}, bf16[1,9,16,256]{3,2,1,0:T(8,128)(2,1)S(1)}, u32[]{:S(2)}, u32[]{:S(2)}) collective-permute-start(bf16[1,9,16,256]{3,2,1,0:T(8,128)(2,1)S(1)} %slice.86), channel_id=1, source_target_pairs={{0,8},{1,9},{2,10},{3,11},{4,12},{5,13},{6,14},{7,15},{8,0},{9,1},... | collective-permute-start | bytes 221192 | tf_op jit(solution)/shard_map/ppermute | solution.py:319
  42.4 5.6 %collective-permute-start.5 = (bf16[1,9,16,256]{3,2,1,0:T(8,128)(2,1)S(1)}, bf16[1,9,16,256]{3,2,1,0:T(8,128)(2,1)S(1)}, u32[]{:S(2)}, u32[]{:S(2)}) collective-permute-start(bf16[1,9,16,256]{3,2,1,0:T(8,128)(2,1)S(1)} %slice.87), channel_id=1, source_target_pairs={{0,8},{1,9},{2,10},{3,11},{4,12},{5,13},{6,14},{7,15},{8,0},{9,1},... | collective-permute-start | bytes 221192 | tf_op jit(solution)/shard_map/ppermute | solution.py:319

commit v7 on v6

--- a/solution.py
+++ b/solution.py
@@ -286,18 +286,31 @@
         slope[there, :] = jnp.where(outside, 0.0, value[here]).astype(BF16)
 
 
-def outputs_kernel(first, hid, slope, xs, cs, w_two, w_one, *refs):
-    block_out, input_grad, hs, ss, f_done, c_done, sems = refs[-7:]
-    count, cols, chans = f_done.shape
-    here = pl.ds(first, count)
-
+def widen_rows(hs, ss, hid, slope, first, count, cols):
     def step(k, carry):
         row = pl.ds(pl.multiple_of((first + k) * cols, cols), cols)
         put_windows(hs, k, hid[row, :], 1)
         put_windows(ss, k, slope[row, :], -1)
         return carry
 
-    lax.fori_loop(0, count + 2, step, 0)
+    lax.fori_loop(0, count, step, 0)
+
+
+def ready_kernel(first, cols, hid, slope, hs, ss):
+    widen_rows(hs, ss, hid, slope, first, hs.shape[0] // cols, cols)
+
+
+def outputs_kernel(first, ready, *refs):
+    if ready:
+        hs, ss, xs, cs, w_two, w_one = refs[:6]
+        block_out, input_grad, f_done, c_done, sems = refs[-5:]
+        count, cols, chans = f_done.shape
+    else:
+        hid, slope, xs, cs, w_two, w_one = refs[:6]
+        block_out, input_grad, hs, ss, f_done, c_done, sems = refs[-7:]
+        count, cols, chans = f_done.shape
+        widen_rows(hs, ss, hid, slope, first, count + 2, cols)
+    here = pl.ds(first, count)
     own = slice((first + 2) * cols, (first + 2 + count) * cols)
     shape = (count, cols, chans)
     total = xs[own, chans : 2 * chans].astype(F32) + conv_rows(hs, w_two, 0, count * cols, cols)
@@ -398,13 +411,23 @@
     shares = [rows * share // sum(SHARES) for share in SHARES]
     shares[-1] = rows - sum(shares[:-1])
     outs, first = (), 0
-    for count in shares:
+    for part, count in enumerate(shares):
+        ready = part > 0
+        sources, scratch = (hid, slope), [pltpu.VMEM(((count + 2) * cols, wide), BF16)] * 2
+        if ready:
+            whole = struct(((count + 2) * cols, wide), BF16)
+            sources, scratch = call(
+                functools.partial(ready_kernel, first, cols),
+                (hid, slope),
+                (whole, whole),
+                work=1 << 20,
+            ), []
         outs = pl.pallas_call(
-            functools.partial(outputs_kernel, first),
+            functools.partial(outputs_kernel, first, ready),
             out_shape=(struct(f.shape, BF16), struct(c.shape, BF16)),
             in_specs=[WHOLE] * 6 + [hbm] * len(outs),
             out_specs=(hbm, hbm),
-            scratch_shapes=[pltpu.VMEM(((count + 2) * cols, wide), BF16)] * 2
+            scratch_shapes=scratch
             + [pltpu.VMEM((count, cols, chans), BF16)] * 2
             + [pltpu.SemaphoreType.DMA((2,))],
             input_output_aliases={6: 0, 7: 1} if outs else {},
@@ -412,7 +435,7 @@
             cost_estimate=pl.CostEstimate(
                 flops=2 * flops * count // rows, bytes_accessed=4 << 20, transcendentals=0
             ),
-        )(hid, slope, xs, cs, w_two, w_one, *outs)
+        )(*sources, xs, cs, w_two, w_one, *outs)
         first += count
     block_out, input_grad = outs
     grad_two = halve(keep_two, send_two, order_two, n)

time: 48.8 us -> 49.6 us (1.016)
  waiting for transfers between devices: 7.32 us -> 7.9 us
    pallas_call x4 -> x5, Pallas kernels: 14.4 us -> 15 us  [call(): pl.pallas_call(kernel, out_shape=outs, in_specs=specs, out_specs=tuple((W...]
    ppermute x8, waiting for transfers between devices: 7.31 us -> 7.89 us  [halve(): got = lax.ppermute(send, 'tile', pairs)]
where the time goes in v7:
time: 49.6 us; the launch traced here: 49.4 us
  Pallas kernels  23.8 us (48%)
  starting transfers between devices  14.7 us (30%)
  waiting for transfers between devices  7.9 us (16%)
  other arithmetic  1.97 us (4%)
  between operations  0.84 us (2%)
    pallas_call x5, Pallas kernels, call(): pl.pallas_call(kernel, out_shape=outs, in_specs=specs, out_specs=tuple((W...  15 us
    ppermute x8, starting transfers between devices, halve(): got = lax.ppermute(send, 'tile', pairs)  11.6 us
    ppermute x8, waiting for transfers between devices, halve(): got = lax.ppermute(send, 'tile', pairs)  7.89 us
    pallas_call x2, Pallas kernels, layer(): pl.pallas_call(functools.partial(outputs_kernel, first, ready), out_shape...  7.54 us
    ppermute x1, starting transfers between devices, layer(): lax.ppermute(across, ('groups', 'tile'), across_pairs(lax.axis_size('grou...  2.55 us
    transpose x2, other arithmetic, halve(): return jnp.swapaxes(total[0], 0, 1)  1.36 us
    pallas_call x1, Pallas kernels, pack(): pl.pallas_call(pack_kernel, out_shape=(out,) * 2, in_specs=[pl.BlockSpec(...  1.28 us
  transfers between devices with their start and end apart: 10, of which 4 were waited for; matrix products, arithmetic and copies ran while one was open for 3% of the time, Pallas kernels for 42%

profile of v7, /device:TPU:0, one launch (start us, length us, event | category | flops | bytes accessed | tf_op | source)
XLA Modules:
  0.0 49.4 jit_solution(6386231839750392888)
XLA Ops:
  0.6 1.3 %shard_map.75 = (bf16[4,160,256]{2,1,0:T(8,128)(2,1)S(1)}, bf16[4,160,256]{2,1,0:T(8,128)(2,1)S(1)}) custom-call(s32[1]{0:T(128)} %bitcast.me_ref, bf16[12,160,256]{2,1,0:T(8,128)(2,1)} %bitcast.29, bf16[12,160,256]{2,1,0:T(8,128)(2,1)} %bitcast.31), custom_call_target="tpu_custom_call" | custom-call | tf_op jit(solution)/shard_map/pallas_call | solution.py:59
  1.9 0.6 %collective-permute-start = (bf16[4,160,256]{2,1,0:T(8,128)(2,1)S(1)}, bf16[4,160,256]{2,1,0:T(8,128)(2,1)S(1)}, u32[]{:S(2)}, u32[]{:S(2)}) collective-permute-start(bf16[4,160,256]{2,1,0:T(8,128)(2,1)S(1)} %get-tuple-element.28), channel_id=1, source_target_pairs={{0,1},{1,0},{2,3},{3,2},{4,5},{5,4},{6,7},{7,6},{8,9},{9,8},{10,11... | collective-permute-start | bytes 983048 | tf_op jit(solution)/shard_map/ppermute | solution.py:375
  2.5 2.6 %collective-permute-start.1 = (bf16[4,160,256]{2,1,0:T(8,128)(2,1)S(1)}, bf16[4,160,256]{2,1,0:T(8,128)(2,1)S(1)}, u32[]{:S(2)}, u32[]{:S(2)}) collective-permute-start(bf16[4,160,256]{2,1,0:T(8,128)(2,1)S(1)} %get-tuple-element.29), channel_id=1, source_target_pairs={{1,2},{3,4},{5,6},{7,8},{9,10},{11,12},{13,14},{2,1},{4,3},{6,5},{... | collective-permute-start | bytes 983048 | tf_op jit(solution)/shard_map/ppermute | solution.py:374
  5.0 8.3 %shard_map.76 = (bf16[2560,768]{1,0:T(8,128)(2,1)S(1)}, bf16[2560,768]{1,0:T(8,128)(2,1)S(1)}, bf16[2240,256]{1,0:T(8,128)(2,1)S(1)}, bf16[2240,256]{1,0:T(8,128)(2,1)S(1)}, f32[3,256,768]{2,1,0:T(8,128)S(1)}) custom-call(bf16[12,160,256]{2,1,0:T(8,128)(2,1)} %bitcast.30, bf16[12,160,256]{2,1,0:T(8,128)(2,1)} %bitcast.32, bf16[2304,256]{1,0:T(8,128)(2,1)} %bitcast.24, ...), custom_call_target="tpu_custom_call" | custom-call | flops 6794772480 | bytes 4194304 | tf_op jit(solution)/shard_map/pallas_call | solution.py:362
  13.4 0.0 collective-permute-done.inside
  13.4 0.0 copy-start.1
  13.4 2.0 %shard_map.77 = (bf16[2560,768]{1,0:T(8,128)(2,1)S(1)}, bf16[2560,768]{1,0:T(8,128)(2,1)S(1)}, bf16[2240,256]{1,0:T(8,128)(2,1)S(1)}, f32[320,256]{1,0:T(8,128)S...) custom-call(s32[1]{0:T(128)} %bitcast.me_ref, ...), custom_call_target="tpu_custom_call", output_to_operand_aliasing={{0}: (4, {}), {1}: (5, {}), {2}: (6, {})} | custom-call | flops 2264924160 | bytes 4194304 | tf_op jit(solution)/shard_map/pallas_call | solution.py:362
  15.4 0.2 collective-permute-start.6
  15.6 3.2 %shard_map.78 = (bf16[2240,256]{1,0:T(8,128)(2,1)S(1)}, f32[8,9,16,256]{3,2,1,0:T(8,128)S(1)}, bf16[8,9,16,256]{3,2,1,0:T(8,128)(2,1)S(1)}) custom-call(s32[1]{0:T(128)} %bitcast.me_ref, bf16[2560,768]{1,0:T(8,128)(2,1)S(1)} %get-tuple-element.34.xs.refs_2_, bf16[2560,768]{1,0:T(8,128)(2,1)S(1)} %get-tuple-element.35.cs.refs_3_, ...), custom_call_target="tpu_custom_call", output_to_operand_aliasing={{0}: (5, {})} | custom-call | flops 2264924160 | bytes 4194304 | tf_op jit(solution)/shard_map/pallas_call | solution.py:362
  18.8 0.4 collective-permute-start.2
  19.2 1.0 %shard_map.79 = (bf16[2240,256]{1,0:T(8,128)(2,1)S(1)}, bf16[2240,256]{1,0:T(8,128)(2,1)S(1)}) custom-call(s32[1]{0:T(128)} %bitcast.me_ref, bf16[2560,768]{1,0:T(8,128)(2,1)S(1)} %get-tuple-element.34.xs.refs_2_, bf16[2560,768]{1,0:T(8,128)(2,1)S(1)} %get-tuple-element.35.cs.refs_3_, ...), custom_call_target="tpu_custom_call", output_to_operand_aliasing={{0}: (5, {}), {1}: (6, {})} | custom-call | flops 2264924160 | bytes 4194304 | tf_op jit(solution)/shard_map/pallas_call | solution.py:362
  20.2 0.6 %shard_map.80 = (bf16[1280,768]{1,0:T(8,128)(2,1)S(1)}, bf16[1280,768]{1,0:T(8,128)(2,1)S(1)}) custom-call(bf16[2240,256]{1,0:T(8,128)(2,1)S(1)} %get-tuple-element.40.hid.refs_0_, bf16[2240,256]{1,0:T(8,128)(2,1)S(1)} %get-tuple-element.41.slope.refs_1_), custom_call_target="tpu_custom_call" | custom-call | flops 1048576 | bytes 4194304 | tf_op jit(solution)/shard_map/pallas_call | solution.py:362
  20.8 4.2 %shard_map.81 = (bf16[12,160,256]{2,1,0:T(8,128)(2,1)}, bf16[12,160,256]{2,1,0:T(8,128)(2,1)}) custom-call(bf16[2240,256]{1,0:T(8,128)(2,1)S(1)} %get-tuple-element.40.hid.refs_0_, bf16[2240,256]{1,0:T(8,128)(2,1)S(1)} %get-tuple-element.41.slope.refs_1_, bf16[2560,768]{1,0:T(8,128)(2,1)S(1)} %get-tuple-element.34.xs.refs_2_, ...), custom_call_target="tpu_custom_call" | custom-call | flops 2264924160 | bytes 4194304 | tf_op jit(solution)/shard_map/pallas_call | solution.py:425
  24.9 0.0 collective-permute-done.6
  25.0 0.2 convert_add_fusion
  25.2 1.8 %collective-permute-start.7 = (bf16[4,9,16,256]{3,2,1,0:T(8,128)(2,1)S(1)}, bf16[4,9,16,256]{3,2,1,0:T(8,128)(2,1)S(1)}, u32[]{:S(2)}, u32[]{:S(2)}) collective-permute-start(bf16[4,9,16,256]{3,2,1,0:T(8,128)(2,1)S(1)} %slice.82), channel_id=1, source_target_pairs={{0,2},{1,3},{2,0},{3,1},{4,6},{5,7},{6,4},{7,5},{8,10},{9,11},{10,... | collective-permute-start | bytes 884744 | tf_op jit(solution)/shard_map/ppermute | solution.py:332
  27.0 0.2 convert_add_fusion.1
  27.2 1.6 %collective-permute-start.3 = (bf16[4,9,16,256]{3,2,1,0:T(8,128)(2,1)S(1)}, bf16[4,9,16,256]{3,2,1,0:T(8,128)(2,1)S(1)}, u32[]{:S(2)}, u32[]{:S(2)}) collective-permute-start(bf16[4,9,16,256]{3,2,1,0:T(8,128)(2,1)S(1)} %slice.83), channel_id=1, source_target_pairs={{0,4},{1,5},{2,6},{3,7},{4,0},{5,1},{6,2},{7,3},{8,12},{9,13},{10,... | collective-permute-start | bytes 884744 | tf_op jit(solution)/shard_map/ppermute | solution.py:332
  28.9 3.4 %shard_map.82 = (bf16[12,160,256]{2,1,0:T(8,128)(2,1)}, bf16[12,160,256]{2,1,0:T(8,128)(2,1)}) custom-call(bf16[1280,768]{1,0:T(8,128)(2,1)S(1)} %get-tuple-element.42.refs_0_, bf16[1280,768]{1,0:T(8,128)(2,1)S(1)} %get-tuple-element.43.refs_1_, bf16[2560,768]{1,0:T(8,128)(2,1)S(1)} %get-tuple-element.34.xs.refs_2_, ...), custom_call_target="tpu_custom_call", output_to_operand_aliasing={{0}: (6, {}), {1}: (7, {})} | custom-call | flops 2264924160 | bytes 4194304 | tf_op jit(solution)/shard_map/pallas_call | solution.py:425
  32.3 2.1 %collective-permute-done.7 = bf16[4,9,16,256]{3,2,1,0:T(8,128)(2,1)S(1)} collective-permute-done((bf16[4,9,16,256]{3,2,1,0:T(8,128)(2,1)S(1)}, bf16[4,9,16,256]{3,2,1,0:T(8,128)(2,1)S(1)}, u32[]{:S(2)}, u32[]{:S(2)}) %collective-permute-start.7) | collective-permute-done | bytes 294944 | tf_op jit(solution)/shard_map/ppermute | solution.py:332
  34.3 0.1 slice_add_fusion
  34.4 2.1 %collective-permute-start.8 = (bf16[2,9,16,256]{3,2,1,0:T(8,128)(2,1)S(1)}, bf16[2,9,16,256]{3,2,1,0:T(8,128)(2,1)S(1)}, u32[]{:S(2)}, u32[]{:S(2)}) collective-permute-start(bf16[2,9,16,256]{3,2,1,0:T(8,128)(2,1)S(1)} %slice.84), channel_id=1, source_target_pairs={{0,4},{1,5},{2,6},{3,7},{4,0},{5,1},{6,2},{7,3},{8,12},{9,13},{10,... | collective-permute-start | bytes 442376 | tf_op jit(solution)/shard_map/ppermute | solution.py:332
  36.5 0.0 collective-permute-done.3
  36.5 0.1 slice_add_fusion.1
  36.7 1.2 %collective-permute-start.4 = (bf16[2,9,16,256]{3,2,1,0:T(8,128)(2,1)S(1)}, bf16[2,9,16,256]{3,2,1,0:T(8,128)(2,1)S(1)}, u32[]{:S(2)}, u32[]{:S(2)}) collective-permute-start(bf16[2,9,16,256]{3,2,1,0:T(8,128)(2,1)S(1)} %slice.85), channel_id=1, source_target_pairs={{0,2},{1,3},{2,0},{3,1},{4,6},{5,7},{6,4},{7,5},{8,10},{9,11},{10,... | collective-permute-start | bytes 442376 | tf_op jit(solution)/shard_map/ppermute | solution.py:332
  37.8 2.3 %collective-permute-done.8 = bf16[2,9,16,256]{3,2,1,0:T(8,128)(2,1)S(1)} collective-permute-done((bf16[2,9,16,256]{3,2,1,0:T(8,128)(2,1)S(1)}, bf16[2,9,16,256]{3,2,1,0:T(8,128)(2,1)S(1)}, u32[]{:S(2)}, u32[]{:S(2)}) %collective-permute-start.8) | collective-permute-done | bytes 147488 | tf_op jit(solution)/shard_map/ppermute | solution.py:332
  40.2 2.8 %collective-permute-start.9 = (bf16[1,9,16,256]{3,2,1,0:T(8,128)(2,1)S(1)}, bf16[1,9,16,256]{3,2,1,0:T(8,128)(2,1)S(1)}, u32[]{:S(2)}, u32[]{:S(2)}) collective-permute-start(bf16[1,9,16,256]{3,2,1,0:T(8,128)(2,1)S(1)} %slice.86), channel_id=1, source_target_pairs={{0,8},{1,9},{2,10},{3,11},{4,12},{5,13},{6,14},{7,15},{8,0},{9,1},... | collective-permute-start | bytes 221192 | tf_op jit(solution)/shard_map/ppermute | solution.py:332
  43.1 1.5 %collective-permute-start.5 = (bf16[1,9,16,256]{3,2,1,0:T(8,128)(2,1)S(1)}, bf16[1,9,16,256]{3,2,1,0:T(8,128)(2,1)S(1)}, u32[]{:S(2)}, u32[]{:S(2)}) collective-permute-start(bf16[1,9,16,256]{3,2,1,0:T(8,128)(2,1)S(1)} %slice.87), channel_id=1, source_target_pairs={{0,8},{1,9},{2,10},{3,11},{4,12},{5,13},{6,14},{7,15},{8,0},{9,1},... | collective-permute-start | bytes 221192 | tf_op jit(solution)/shard_map/ppermute | solution.py:332
  44.6 1.4 %collective-permute-done.9 = bf16[1,9,16,256]{3,2,1,0:T(8,128)(2,1)S(1)} collective-permute-done((bf16[1,9,16,256]{3,2,1,0:T(8,128)(2,1)S(1)}, bf16[1,9,16,256]{3,2,1,0:T(8,128)(2,1)S(1)}, u32[]{:S(2)}, u32[]{:S(2)}) %collective-permute-start.9) | collective-permute-done | bytes 73760 | tf_op jit(solution)/shard_map/ppermute | solution.py:332
  46.0 0.7 %fusion = f32[16,9,256]{2,0,1:T(8,128)} fusion(f32[2,9,16,256]{3,2,1,0:T(8,128)S(1)} %slice_add_fusion.2, bf16[1,9,16,256]{3,2,1,0:T(8,128)(2,1)S(1)} %collective-permute-done.9), kind=kLoop, calls=%fused_computation.12 | loop fusion | flops 73728 | bytes 368640 | tf_op jit(solution)/shard_map/transpose | solution.py:338
  46.7 2.1 %collective-permute-done.5 = bf16[1,9,16,256]{3,2,1,0:T(8,128)(2,1)S(1)} collective-permute-done((bf16[1,9,16,256]{3,2,1,0:T(8,128)(2,1)S(1)}, bf16[1,9,16,256]{3,2,1,0:T(8,128)(2,1)S(1)}, u32[]{:S(2)}, u32[]{:S(2)}) %collective-permute-start.5) | collective-permute-done | bytes 73760 | tf_op jit(solution)/shard_map/ppermute | solution.py:332
  48.7 0.7 %fusion.1 = f32[16,9,256]{2,0,1:T(8,128)} fusion(f32[2,9,16,256]{3,2,1,0:T(8,128)S(1)} %slice_add_fusion.3, bf16[1,9,16,256]{3,2,1,0:T(8,128)(2,1)S(1)} %collective-permute-done.5), kind=kLoop, calls=%fused_computation.15 | loop fusion | flops 73728 | bytes 368640 | tf_op jit(solution)/shard_map/transpose | solution.py:338
  (14 shorter events, 0.2 us)
Async XLA Ops:
  0.6 4.4 %copy-start = (bf16[256,9,256]{2,0,1:T(8,128)(2,1)S(1)}, bf16[256,9,256]{2,0,1:T(8,128)(2,1)}, u32[]{:S(2)}) copy-start(bf16[256,9,256]{2,0,1:T(8,128)(2,1)} %param.6) | copy-start | bytes 3538948
  1.9 11.4 %collective-permute-start = (bf16[4,160,256]{2,1,0:T(8,128)(2,1)S(1)}, bf16[4,160,256]{2,1,0:T(8,128)(2,1)S(1)}, u32[]{:S(2)}, u32[]{:S(2)}) collective-permute-start(bf16[4,160,256]{2,1,0:T(8,128)(2,1)S(1)} %get-tuple-element.28), channel_id=1, source_target_pairs={{0,1},{1,0},{2,3},{3,2},{4,5},{5,4},{6,7},{7,6},{8,9},{9,8},{10,11... | collective-permute-start | bytes 983048 | tf_op jit(solution)/shard_map/ppermute | solution.py:375
  2.5 10.9 %collective-permute-start.1 = (bf16[4,160,256]{2,1,0:T(8,128)(2,1)S(1)}, bf16[4,160,256]{2,1,0:T(8,128)(2,1)S(1)}, u32[]{:S(2)}, u32[]{:S(2)}) collective-permute-start(bf16[4,160,256]{2,1,0:T(8,128)(2,1)S(1)} %get-tuple-element.29), channel_id=1, source_target_pairs={{1,2},{3,4},{5,6},{7,8},{9,10},{11,12},{13,14},{2,1},{4,3},{6,5},{... | collective-permute-start | bytes 983048 | tf_op jit(solution)/shard_map/ppermute | solution.py:374
  13.4 2.2 %copy-start.1 = (bf16[256,9,256]{2,0,1:T(8,128)(2,1)S(1)}, bf16[256,9,256]{2,0,1:T(8,128)(2,1)}, u32[]{:S(2)}) copy-start(bf16[256,9,256]{2,0,1:T(8,128)(2,1)} %param.7) | copy-start | bytes 3538948
  15.4 9.6 %collective-permute-start.6 = (bf16[8,9,16,256]{3,2,1,0:T(8,128)(2,1)S(1)}, bf16[8,9,16,256]{3,2,1,0:T(8,128)(2,1)S(1)}, u32[]{:S(2)}, u32[]{:S(2)}) collective-permute-start(bf16[8,9,16,256]{3,2,1,0:T(8,128)(2,1)S(1)} %get-tuple-element.51), channel_id=1, source_target_pairs={{0,1},{1,0},{2,3},{3,2},{4,5},{5,4},{6,7},{7,6},{8,9},{9,8},{10,11... | collective-permute-start | bytes 1769480 | tf_op jit(solution)/shard_map/ppermute | solution.py:332
  18.8 8.2 %collective-permute-start.2 = (bf16[8,9,16,256]{3,2,1,0:T(8,128)(2,1)S(1)}, bf16[8,9,16,256]{3,2,1,0:T(8,128)(2,1)S(1)}, u32[]{:S(2)}, u32[]{:S(2)}) collective-permute-start(bf16[8,9,16,256]{3,2,1,0:T(8,128)(2,1)S(1)} %get-tuple-element.49), channel_id=1, source_target_pairs={{0,1},{1,0},{2,3},{3,2},{4,5},{5,4},{6,7},{7,6},{8,9},{9,8},{10,11... | collective-permute-start | bytes 1769480 | tf_op jit(solution)/shard_map/ppermute | solution.py:332
  25.2 9.1 %collective-permute-start.7 = (bf16[4,9,16,256]{3,2,1,0:T(8,128)(2,1)S(1)}, bf16[4,9,16,256]{3,2,1,0:T(8,128)(2,1)S(1)}, u32[]{:S(2)}, u32[]{:S(2)}) collective-permute-start(bf16[4,9,16,256]{3,2,1,0:T(8,128)(2,1)S(1)} %slice.82), channel_id=1, source_target_pairs={{0,2},{1,3},{2,0},{3,1},{4,6},{5,7},{6,4},{7,5},{8,10},{9,11},{10,... | collective-permute-start | bytes 884744 | tf_op jit(solution)/shard_map/ppermute | solution.py:332
  27.2 9.3 %collective-permute-start.3 = (bf16[4,9,16,256]{3,2,1,0:T(8,128)(2,1)S(1)}, bf16[4,9,16,256]{3,2,1,0:T(8,128)(2,1)S(1)}, u32[]{:S(2)}, u32[]{:S(2)}) collective-permute-start(bf16[4,9,16,256]{3,2,1,0:T(8,128)(2,1)S(1)} %slice.83), channel_id=1, source_target_pairs={{0,4},{1,5},{2,6},{3,7},{4,0},{5,1},{6,2},{7,3},{8,12},{9,13},{10,... | collective-permute-start | bytes 884744 | tf_op jit(solution)/shard_map/ppermute | solution.py:332
  34.4 5.7 %collective-permute-start.8 = (bf16[2,9,16,256]{3,2,1,0:T(8,128)(2,1)S(1)}, bf16[2,9,16,256]{3,2,1,0:T(8,128)(2,1)S(1)}, u32[]{:S(2)}, u32[]{:S(2)}) collective-permute-start(bf16[2,9,16,256]{3,2,1,0:T(8,128)(2,1)S(1)} %slice.84), channel_id=1, source_target_pairs={{0,4},{1,5},{2,6},{3,7},{4,0},{5,1},{6,2},{7,3},{8,12},{9,13},{10,... | collective-permute-start | bytes 442376 | tf_op jit(solution)/shard_map/ppermute | solution.py:332
  36.7 6.4 %collective-permute-start.4 = (bf16[2,9,16,256]{3,2,1,0:T(8,128)(2,1)S(1)}, bf16[2,9,16,256]{3,2,1,0:T(8,128)(2,1)S(1)}, u32[]{:S(2)}, u32[]{:S(2)}) collective-permute-start(bf16[2,9,16,256]{3,2,1,0:T(8,128)(2,1)S(1)} %slice.85), channel_id=1, source_target_pairs={{0,2},{1,3},{2,0},{3,1},{4,6},{5,7},{6,4},{7,5},{8,10},{9,11},{10,... | collective-permute-start | bytes 442376 | tf_op jit(solution)/shard_map/ppermute | solution.py:332
  40.2 5.7 %collective-permute-start.9 = (bf16[1,9,16,256]{3,2,1,0:T(8,128)(2,1)S(1)}, bf16[1,9,16,256]{3,2,1,0:T(8,128)(2,1)S(1)}, u32[]{:S(2)}, u32[]{:S(2)}) collective-permute-start(bf16[1,9,16,256]{3,2,1,0:T(8,128)(2,1)S(1)} %slice.86), channel_id=1, source_target_pairs={{0,8},{1,9},{2,10},{3,11},{4,12},{5,13},{6,14},{7,15},{8,0},{9,1},... | collective-permute-start | bytes 221192 | tf_op jit(solution)/shard_map/ppermute | solution.py:332
  43.1 5.6 %collective-permute-start.5 = (bf16[1,9,16,256]{3,2,1,0:T(8,128)(2,1)S(1)}, bf16[1,9,16,256]{3,2,1,0:T(8,128)(2,1)S(1)}, u32[]{:S(2)}, u32[]{:S(2)}) collective-permute-start(bf16[1,9,16,256]{3,2,1,0:T(8,128)(2,1)S(1)} %slice.87), channel_id=1, source_target_pairs={{0,8},{1,9},{2,10},{3,11},{4,12},{5,13},{6,14},{7,15},{8,0},{9,1},... | collective-permute-start | bytes 221192 | tf_op jit(solution)/shard_map/ppermute | solution.py:332

commit v8 on v7

--- a/solution.py
+++ b/solution.py
@@ -13,7 +13,7 @@
 WHOLE = pl.BlockSpec(memory_space=pltpu.VMEM)
 LIMIT = 20 << 20
 SHARES = (6, 6)
-PIECES = 4
+PIECES = 2
 
 
 def struct(shape, dtype):
@@ -298,6 +298,10 @@
 
 def ready_kernel(first, cols, hid, slope, hs, ss):
     widen_rows(hs, ss, hid, slope, first, hs.shape[0] // cols, cols)
+
+
+def gate_kernel(source, out):
+    out[...] = source[: out.shape[0], : out.shape[1]].astype(F32)
 
 
 def outputs_kernel(first, ready, *refs):
@@ -330,12 +334,16 @@
     for bit in order:
         pairs = [(i, i ^ (1 << bit)) for i in range(n)]
         got = lax.ppermute(send, "tile", pairs)
+        half = keep.shape[0] // 2
+        if not half:
+            return keep[0], got[0]
         total = keep + got.astype(F32)
-        half = total.shape[0] // 2
-        if half:
-            keep, send = total[:half], total[half:].astype(BF16)
-        else:
-            return jnp.swapaxes(total[0], 0, 1)
+        keep, send = total[:half], total[half:].astype(BF16)
+
+
+def final_kernel(kept_one, got_one, kept_two, got_two, grad_one, grad_two):
+    grad_one[...] = kept_one[...] + got_one[...].astype(F32)
+    grad_two[...] = kept_two[...] + got_two[...].astype(F32)
 
 
 def layer(features, cotangent, weight_one, weight_two):
@@ -422,10 +430,13 @@
                 (whole, whole),
                 work=1 << 20,
             ), []
+        gates = ()
+        if ready:
+            gates = call(gate_kernel, (hid,), (struct((8, 128), F32),), work=1 << 10)
         outs = pl.pallas_call(
             functools.partial(outputs_kernel, first, ready),
             out_shape=(struct(f.shape, BF16), struct(c.shape, BF16)),
-            in_specs=[WHOLE] * 6 + [hbm] * len(outs),
+            in_specs=[WHOLE] * 6 + [hbm] * len(outs) + [WHOLE] * len(gates),
             out_specs=(hbm, hbm),
             scratch_shapes=scratch
             + [pltpu.VMEM((count, cols, chans), BF16)] * 2
@@ -435,11 +446,14 @@
             cost_estimate=pl.CostEstimate(
                 flops=2 * flops * count // rows, bytes_accessed=4 << 20, transcendentals=0
             ),
-        )(*sources, xs, cs, w_two, w_one, *outs)
+        )(*sources, xs, cs, w_two, w_one, *outs, *gates)
         first += count
     block_out, input_grad = outs
-    grad_two = halve(keep_two, send_two, order_two, n)
-    grad_one = halve(keep_one, send_one, order_one, n)
+    last_two = halve(keep_two, send_two, order_two, n)
+    last_one = halve(keep_one, send_one, order_one, n)
+    slab = struct(last_one[0].shape, F32)
+    grads = call(final_kernel, last_one + last_two, (slab, slab), work=1 << 20)
+    grad_one, grad_two = (jnp.swapaxes(grad, 0, 1) for grad in grads)
     return (block_out[None], input_grad[None], grad_one, grad_two)
 
 

time: 49.6 us -> 49.6 us (level)
  other arithmetic: 1.97 us -> 0.63 us
  Pallas kernels: 23.8 us -> 24.4 us
  waiting for transfers between devices: 7.9 us -> 8.42 us
    transpose x2 -> x0, other arithmetic: 1.36 us -> none  [halve(): return jnp.swapaxes(total[0], 0, 1)]
    pallas_call x5 -> x7, Pallas kernels: 15 us -> 15.6 us  [call(): pl.pallas_call(kernel, out_shape=outs, in_specs=specs, out_specs=tuple((W...]
    ppermute x8, waiting for transfers between devices: 7.89 us -> 8.41 us  [halve(): got = lax.ppermute(send, 'tile', pairs)]
  transfers between devices with their start and end apart: 10 -> 10, of which waited for: 4 -> 4; matrix products, arithmetic and copies ran while one was open for 3% -> 2% of each run, Pallas kernels for 42% -> 41%
where the time goes in v8:
time: 49.6 us; the launch traced here: 49.5 us
  Pallas kernels  24.4 us (49%)
  starting transfers between devices  15 us (30%)
  waiting for transfers between devices  8.42 us (17%)
  between operations  0.85 us (2%)
  other arithmetic  0.63 us (1%)
    pallas_call x7, Pallas kernels, call(): pl.pallas_call(kernel, out_shape=outs, in_specs=specs, out_specs=tuple((W...  15.6 us
    ppermute x8, starting transfers between devices, halve(): got = lax.ppermute(send, 'tile', pairs)  11.9 us
    ppermute x8, waiting for transfers between devices, halve(): got = lax.ppermute(send, 'tile', pairs)  8.41 us
    pallas_call x2, Pallas kernels, layer(): pl.pallas_call(functools.partial(outputs_kernel, first, ready), out_shape...  7.53 us
    ppermute x1, starting transfers between devices, layer(): lax.ppermute(across, ('groups', 'tile'), across_pairs(lax.axis_size('grou...  2.55 us
    pallas_call x1, Pallas kernels, pack(): pl.pallas_call(pack_kernel, out_shape=(out,) * 2, in_specs=[pl.BlockSpec(...  1.28 us
  transfers between devices with their start and end apart: 10, of which 4 were waited for; matrix products, arithmetic and copies ran while one was open for 2% of the time, Pallas kernels for 41%

profile of v8, /device:TPU:0, one launch (start us, length us, event | category | flops | bytes accessed | tf_op | source)
XLA Modules:
  0.0 49.5 jit_solution(95869914210312274)
XLA Ops:
  0.6 1.3 %shard_map.75 = (bf16[4,160,256]{2,1,0:T(8,128)(2,1)S(1)}, bf16[4,160,256]{2,1,0:T(8,128)(2,1)S(1)}) custom-call(s32[1]{0:T(128)} %bitcast.me_ref, bf16[12,160,256]{2,1,0:T(8,128)(2,1)} %bitcast.31, bf16[12,160,256]{2,1,0:T(8,128)(2,1)} %bitcast.33), custom_call_target="tpu_custom_call" | custom-call | tf_op jit(solution)/shard_map/pallas_call | solution.py:59
  1.9 0.6 %collective-permute-start = (bf16[4,160,256]{2,1,0:T(8,128)(2,1)S(1)}, bf16[4,160,256]{2,1,0:T(8,128)(2,1)S(1)}, u32[]{:S(2)}, u32[]{:S(2)}) collective-permute-start(bf16[4,160,256]{2,1,0:T(8,128)(2,1)S(1)} %get-tuple-element.30), channel_id=1, source_target_pairs={{0,1},{1,0},{2,3},{3,2},{4,5},{5,4},{6,7},{7,6},{8,9},{9,8},{10,11... | collective-permute-start | bytes 983048 | tf_op jit(solution)/shard_map/ppermute | solution.py:383
  2.5 2.6 %collective-permute-start.1 = (bf16[4,160,256]{2,1,0:T(8,128)(2,1)S(1)}, bf16[4,160,256]{2,1,0:T(8,128)(2,1)S(1)}, u32[]{:S(2)}, u32[]{:S(2)}) collective-permute-start(bf16[4,160,256]{2,1,0:T(8,128)(2,1)S(1)} %get-tuple-element.31), channel_id=1, source_target_pairs={{1,2},{3,4},{5,6},{7,8},{9,10},{11,12},{13,14},{2,1},{4,3},{6,5},{... | collective-permute-start | bytes 983048 | tf_op jit(solution)/shard_map/ppermute | solution.py:382
  5.0 8.2 %shard_map.76 = (bf16[2560,768]{1,0:T(8,128)(2,1)S(1)}, bf16[2560,768]{1,0:T(8,128)(2,1)S(1)}, bf16[2240,256]{1,0:T(8,128)(2,1)S(1)}, bf16[2240,256]{1,0:T(8,128)(2,1)S(1)}, f32[3,256,768]{2,1,0:T(8,128)S(1)}) custom-call(bf16[12,160,256]{2,1,0:T(8,128)(2,1)} %bitcast.32, bf16[12,160,256]{2,1,0:T(8,128)(2,1)} %bitcast.34, bf16[2304,256]{1,0:T(8,128)(2,1)} %bitcast.24, ...), custom_call_target="tpu_custom_call" | custom-call | flops 6794772480 | bytes 4194304 | tf_op jit(solution)/shard_map/pallas_call | solution.py:370
  13.2 0.0 collective-permute-done.inside
  13.2 0.0 copy-start.1
  13.2 2.0 %shard_map.77 = (bf16[2560,768]{1,0:T(8,128)(2,1)S(1)}, bf16[2560,768]{1,0:T(8,128)(2,1)S(1)}, bf16[2240,256]{1,0:T(8,128)(2,1)S(1)}, f32[320,256]{1,0:T(8,128)S...) custom-call(s32[1]{0:T(128)} %bitcast.me_ref, ...), custom_call_target="tpu_custom_call", output_to_operand_aliasing={{0}: (4, {}), {1}: (5, {}), {2}: (6, {})} | custom-call | flops 2264924160 | bytes 4194304 | tf_op jit(solution)/shard_map/pallas_call | solution.py:370
  15.2 0.2 collective-permute-start.6
  15.5 3.2 %shard_map.78 = (bf16[2240,256]{1,0:T(8,128)(2,1)S(1)}, f32[8,9,16,256]{3,2,1,0:T(8,128)S(1)}, bf16[8,9,16,256]{3,2,1,0:T(8,128)(2,1)S(1)}) custom-call(s32[1]{0:T(128)} %bitcast.me_ref, bf16[2560,768]{1,0:T(8,128)(2,1)S(1)} %get-tuple-element.36.xs.refs_2_, bf16[2560,768]{1,0:T(8,128)(2,1)S(1)} %get-tuple-element.37.cs.refs_3_, ...), custom_call_target="tpu_custom_call", output_to_operand_aliasing={{0}: (5, {})} | custom-call | flops 2264924160 | bytes 4194304 | tf_op jit(solution)/shard_map/pallas_call | solution.py:370
  18.6 0.4 collective-permute-start.2
  19.1 1.0 %shard_map.79 = (bf16[2240,256]{1,0:T(8,128)(2,1)S(1)}, bf16[2240,256]{1,0:T(8,128)(2,1)S(1)}) custom-call(s32[1]{0:T(128)} %bitcast.me_ref, bf16[2560,768]{1,0:T(8,128)(2,1)S(1)} %get-tuple-element.36.xs.refs_2_, bf16[2560,768]{1,0:T(8,128)(2,1)S(1)} %get-tuple-element.37.cs.refs_3_, ...), custom_call_target="tpu_custom_call", output_to_operand_aliasing={{0}: (5, {}), {1}: (6, {})} | custom-call | flops 2264924160 | bytes 4194304 | tf_op jit(solution)/shard_map/pallas_call | solution.py:370
  20.1 0.6 %shard_map.80 = (bf16[1280,768]{1,0:T(8,128)(2,1)S(1)}, bf16[1280,768]{1,0:T(8,128)(2,1)S(1)}) custom-call(bf16[2240,256]{1,0:T(8,128)(2,1)S(1)} %get-tuple-element.42.hid.refs_0_.source, bf16[2240,256]{1,0:T(8,128)(2,1)S(1)} %get-tuple-element.43.slope.refs_1_), custom_call_target="tpu_custom_call" | custom-call | flops 1048576 | bytes 4194304 | tf_op jit(solution)/shard_map/pallas_call | solution.py:370
  20.6 4.1 %shard_map.81 = (bf16[12,160,256]{2,1,0:T(8,128)(2,1)}, bf16[12,160,256]{2,1,0:T(8,128)(2,1)}) custom-call(bf16[2240,256]{1,0:T(8,128)(2,1)S(1)} %get-tuple-element.42.hid.refs_0_.source, bf16[2240,256]{1,0:T(8,128)(2,1)S(1)} %get-tuple-element.43.slope.refs_1_, bf16[2560,768]{1,0:T(8,128)(2,1)S(1)} %get-tuple-element.36.xs.refs_2_, ...), custom_call_target="tpu_custom_call" | custom-call | flops 2264924160 | bytes 4194304 | tf_op jit(solution)/shard_map/pallas_call | solution.py:436
  24.8 0.0 collective-permute-done.6
  24.8 0.2 convert_add_fusion
  25.1 1.9 %collective-permute-start.7 = (bf16[4,9,16,256]{3,2,1,0:T(8,128)(2,1)S(1)}, bf16[4,9,16,256]{3,2,1,0:T(8,128)(2,1)S(1)}, u32[]{:S(2)}, u32[]{:S(2)}) collective-permute-start(bf16[4,9,16,256]{3,2,1,0:T(8,128)(2,1)S(1)} %slice.78), channel_id=1, source_target_pairs={{0,2},{1,3},{2,0},{3,1},{4,6},{5,7},{6,4},{7,5},{8,10},{9,11},{10,... | collective-permute-start | bytes 884744 | tf_op jit(solution)/shard_map/ppermute | solution.py:336
  27.0 0.0 collective-permute-done.2
  27.0 0.2 convert_add_fusion.1
  27.2 1.6 %collective-permute-start.3 = (bf16[4,9,16,256]{3,2,1,0:T(8,128)(2,1)S(1)}, bf16[4,9,16,256]{3,2,1,0:T(8,128)(2,1)S(1)}, u32[]{:S(2)}, u32[]{:S(2)}) collective-permute-start(bf16[4,9,16,256]{3,2,1,0:T(8,128)(2,1)S(1)} %slice.79), channel_id=1, source_target_pairs={{0,4},{1,5},{2,6},{3,7},{4,0},{5,1},{6,2},{7,3},{8,12},{9,13},{10,... | collective-permute-start | bytes 884744 | tf_op jit(solution)/shard_map/ppermute | solution.py:336
  28.9 3.4 %shard_map.83 = (bf16[12,160,256]{2,1,0:T(8,128)(2,1)}, bf16[12,160,256]{2,1,0:T(8,128)(2,1)}) custom-call(bf16[1280,768]{1,0:T(8,128)(2,1)S(1)} %get-tuple-element.44.refs_0_, bf16[1280,768]{1,0:T(8,128)(2,1)S(1)} %get-tuple-element.45.refs_1_, bf16[2560,768]{1,0:T(8,128)(2,1)S(1)} %get-tuple-element.36.xs.refs_2_, ...), custom_call_target="tpu_custom_call", output_to_operand_aliasing={{0}: (6, {}), {1}: (7, {})} | custom-call | flops 2264924160 | bytes 4194304 | tf_op jit(solution)/shard_map/pallas_call | solution.py:436
  32.3 1.9 %collective-permute-done.7 = bf16[4,9,16,256]{3,2,1,0:T(8,128)(2,1)S(1)} collective-permute-done((bf16[4,9,16,256]{3,2,1,0:T(8,128)(2,1)S(1)}, bf16[4,9,16,256]{3,2,1,0:T(8,128)(2,1)S(1)}, u32[]{:S(2)}, u32[]{:S(2)}) %collective-permute-start.7) | collective-permute-done | bytes 294944 | tf_op jit(solution)/shard_map/ppermute | solution.py:336
  34.2 0.1 slice_add_fusion
  34.3 2.3 %collective-permute-start.8 = (bf16[2,9,16,256]{3,2,1,0:T(8,128)(2,1)S(1)}, bf16[2,9,16,256]{3,2,1,0:T(8,128)(2,1)S(1)}, u32[]{:S(2)}, u32[]{:S(2)}) collective-permute-start(bf16[2,9,16,256]{3,2,1,0:T(8,128)(2,1)S(1)} %slice.80), channel_id=1, source_target_pairs={{0,4},{1,5},{2,6},{3,7},{4,0},{5,1},{6,2},{7,3},{8,12},{9,13},{10,... | collective-permute-start | bytes 442376 | tf_op jit(solution)/shard_map/ppermute | solution.py:336
  36.6 0.0 collective-permute-done.3
  36.6 0.1 slice_add_fusion.1
  36.7 1.2 %collective-permute-start.4 = (bf16[2,9,16,256]{3,2,1,0:T(8,128)(2,1)S(1)}, bf16[2,9,16,256]{3,2,1,0:T(8,128)(2,1)S(1)}, u32[]{:S(2)}, u32[]{:S(2)}) collective-permute-start(bf16[2,9,16,256]{3,2,1,0:T(8,128)(2,1)S(1)} %slice.81), channel_id=1, source_target_pairs={{0,2},{1,3},{2,0},{3,1},{4,6},{5,7},{6,4},{7,5},{8,10},{9,11},{10,... | collective-permute-start | bytes 442376 | tf_op jit(solution)/shard_map/ppermute | solution.py:336
  37.9 2.3 %collective-permute-done.8 = bf16[2,9,16,256]{3,2,1,0:T(8,128)(2,1)S(1)} collective-permute-done((bf16[2,9,16,256]{3,2,1,0:T(8,128)(2,1)S(1)}, bf16[2,9,16,256]{3,2,1,0:T(8,128)(2,1)S(1)}, u32[]{:S(2)}, u32[]{:S(2)}) %collective-permute-start.8) | collective-permute-done | bytes 147488 | tf_op jit(solution)/shard_map/ppermute | solution.py:336
  40.3 2.8 %collective-permute-start.9 = (bf16[1,9,16,256]{3,2,1,0:T(8,128)(2,1)S(1)}, bf16[1,9,16,256]{3,2,1,0:T(8,128)(2,1)S(1)}, u32[]{:S(2)}, u32[]{:S(2)}) collective-permute-start(bf16[1,9,16,256]{3,2,1,0:T(8,128)(2,1)S(1)} %slice.82), channel_id=1, source_target_pairs={{0,8},{1,9},{2,10},{3,11},{4,12},{5,13},{6,14},{7,15},{8,0},{9,1},... | collective-permute-start | bytes 221192 | tf_op jit(solution)/shard_map/ppermute | solution.py:336
  43.2 1.4 %collective-permute-start.5 = (bf16[1,9,16,256]{3,2,1,0:T(8,128)(2,1)S(1)}, bf16[1,9,16,256]{3,2,1,0:T(8,128)(2,1)S(1)}, u32[]{:S(2)}, u32[]{:S(2)}) collective-permute-start(bf16[1,9,16,256]{3,2,1,0:T(8,128)(2,1)S(1)} %slice.83), channel_id=1, source_target_pairs={{0,8},{1,9},{2,10},{3,11},{4,12},{5,13},{6,14},{7,15},{8,0},{9,1},... | collective-permute-start | bytes 221192 | tf_op jit(solution)/shard_map/ppermute | solution.py:336
  44.6 1.3 %collective-permute-done.9 = bf16[1,9,16,256]{3,2,1,0:T(8,128)(2,1)S(1)} collective-permute-done((bf16[1,9,16,256]{3,2,1,0:T(8,128)(2,1)S(1)}, bf16[1,9,16,256]{3,2,1,0:T(8,128)(2,1)S(1)}, u32[]{:S(2)}, u32[]{:S(2)}) %collective-permute-start.9) | collective-permute-done | bytes 73760 | tf_op jit(solution)/shard_map/ppermute | solution.py:336
  45.9 2.8 %collective-permute-done.5 = bf16[1,9,16,256]{3,2,1,0:T(8,128)(2,1)S(1)} collective-permute-done((bf16[1,9,16,256]{3,2,1,0:T(8,128)(2,1)S(1)}, bf16[1,9,16,256]{3,2,1,0:T(8,128)(2,1)S(1)}, u32[]{:S(2)}, u32[]{:S(2)}) %collective-permute-start.5) | collective-permute-done | bytes 73760 | tf_op jit(solution)/shard_map/ppermute | solution.py:336
  48.8 0.7 %shard_map.84 = (f32[9,16,256]{2,1,0:T(8,128)}, f32[9,16,256]{2,1,0:T(8,128)}) custom-call(f32[9,16,256]{2,1,0:T(8,128)S(1)} %slice_bitcast_fusion.1.kept_one, bf16[9,16,256]{2,1,0:T(8,128)(2,1)S(1)} %bitcast.30, f32[9,16,256]{2,1,0:T(8,128)S(1)} %slice_bitcast_fusion.kept_two, bf16[9,16,256]{2,1,0:T(8,128)(2,1)S(1)} %bitcast.29), custom_call_target="tpu_custom_call" | custom-call | flops 1048576 | bytes 4194304 | tf_op jit(solution)/shard_map/pallas_call | solution.py:370
  (16 shorter events, 0.2 us)
Async XLA Ops:
  0.6 4.4 %copy-start = (bf16[256,9,256]{2,0,1:T(8,128)(2,1)S(1)}, bf16[256,9,256]{2,0,1:T(8,128)(2,1)}, u32[]{:S(2)}) copy-start(bf16[256,9,256]{2,0,1:T(8,128)(2,1)} %param.6) | copy-start | bytes 3538948
  1.9 11.3 %collective-permute-start = (bf16[4,160,256]{2,1,0:T(8,128)(2,1)S(1)}, bf16[4,160,256]{2,1,0:T(8,128)(2,1)S(1)}, u32[]{:S(2)}, u32[]{:S(2)}) collective-permute-start(bf16[4,160,256]{2,1,0:T(8,128)(2,1)S(1)} %get-tuple-element.30), channel_id=1, source_target_pairs={{0,1},{1,0},{2,3},{3,2},{4,5},{5,4},{6,7},{7,6},{8,9},{9,8},{10,11... | collective-permute-start | bytes 983048 | tf_op jit(solution)/shard_map/ppermute | solution.py:383
  2.5 10.7 %collective-permute-start.1 = (bf16[4,160,256]{2,1,0:T(8,128)(2,1)S(1)}, bf16[4,160,256]{2,1,0:T(8,128)(2,1)S(1)}, u32[]{:S(2)}, u32[]{:S(2)}) collective-permute-start(bf16[4,160,256]{2,1,0:T(8,128)(2,1)S(1)} %get-tuple-element.31), channel_id=1, source_target_pairs={{1,2},{3,4},{5,6},{7,8},{9,10},{11,12},{13,14},{2,1},{4,3},{6,5},{... | collective-permute-start | bytes 983048 | tf_op jit(solution)/shard_map/ppermute | solution.py:382
  13.2 2.2 %copy-start.1 = (bf16[256,9,256]{2,0,1:T(8,128)(2,1)S(1)}, bf16[256,9,256]{2,0,1:T(8,128)(2,1)}, u32[]{:S(2)}) copy-start(bf16[256,9,256]{2,0,1:T(8,128)(2,1)} %param.7) | copy-start | bytes 3538948
  15.2 9.6 %collective-permute-start.6 = (bf16[8,9,16,256]{3,2,1,0:T(8,128)(2,1)S(1)}, bf16[8,9,16,256]{3,2,1,0:T(8,128)(2,1)S(1)}, u32[]{:S(2)}, u32[]{:S(2)}) collective-permute-start(bf16[8,9,16,256]{3,2,1,0:T(8,128)(2,1)S(1)} %get-tuple-element.53), channel_id=1, source_target_pairs={{0,1},{1,0},{2,3},{3,2},{4,5},{5,4},{6,7},{7,6},{8,9},{9,8},{10,11... | collective-permute-start | bytes 1769480 | tf_op jit(solution)/shard_map/ppermute | solution.py:336
  18.6 8.3 %collective-permute-start.2 = (bf16[8,9,16,256]{3,2,1,0:T(8,128)(2,1)S(1)}, bf16[8,9,16,256]{3,2,1,0:T(8,128)(2,1)S(1)}, u32[]{:S(2)}, u32[]{:S(2)}) collective-permute-start(bf16[8,9,16,256]{3,2,1,0:T(8,128)(2,1)S(1)} %get-tuple-element.51), channel_id=1, source_target_pairs={{0,1},{1,0},{2,3},{3,2},{4,5},{5,4},{6,7},{7,6},{8,9},{9,8},{10,11... | collective-permute-start | bytes 1769480 | tf_op jit(solution)/shard_map/ppermute | solution.py:336
  25.1 9.1 %collective-permute-start.7 = (bf16[4,9,16,256]{3,2,1,0:T(8,128)(2,1)S(1)}, bf16[4,9,16,256]{3,2,1,0:T(8,128)(2,1)S(1)}, u32[]{:S(2)}, u32[]{:S(2)}) collective-permute-start(bf16[4,9,16,256]{3,2,1,0:T(8,128)(2,1)S(1)} %slice.78), channel_id=1, source_target_pairs={{0,2},{1,3},{2,0},{3,1},{4,6},{5,7},{6,4},{7,5},{8,10},{9,11},{10,... | collective-permute-start | bytes 884744 | tf_op jit(solution)/shard_map/ppermute | solution.py:336
  27.2 9.3 %collective-permute-start.3 = (bf16[4,9,16,256]{3,2,1,0:T(8,128)(2,1)S(1)}, bf16[4,9,16,256]{3,2,1,0:T(8,128)(2,1)S(1)}, u32[]{:S(2)}, u32[]{:S(2)}) collective-permute-start(bf16[4,9,16,256]{3,2,1,0:T(8,128)(2,1)S(1)} %slice.79), channel_id=1, source_target_pairs={{0,4},{1,5},{2,6},{3,7},{4,0},{5,1},{6,2},{7,3},{8,12},{9,13},{10,... | collective-permute-start | bytes 884744 | tf_op jit(solution)/shard_map/ppermute | solution.py:336
  34.3 5.9 %collective-permute-start.8 = (bf16[2,9,16,256]{3,2,1,0:T(8,128)(2,1)S(1)}, bf16[2,9,16,256]{3,2,1,0:T(8,128)(2,1)S(1)}, u32[]{:S(2)}, u32[]{:S(2)}) collective-permute-start(bf16[2,9,16,256]{3,2,1,0:T(8,128)(2,1)S(1)} %slice.80), channel_id=1, source_target_pairs={{0,4},{1,5},{2,6},{3,7},{4,0},{5,1},{6,2},{7,3},{8,12},{9,13},{10,... | collective-permute-start | bytes 442376 | tf_op jit(solution)/shard_map/ppermute | solution.py:336
  36.7 6.4 %collective-permute-start.4 = (bf16[2,9,16,256]{3,2,1,0:T(8,128)(2,1)S(1)}, bf16[2,9,16,256]{3,2,1,0:T(8,128)(2,1)S(1)}, u32[]{:S(2)}, u32[]{:S(2)}) collective-permute-start(bf16[2,9,16,256]{3,2,1,0:T(8,128)(2,1)S(1)} %slice.81), channel_id=1, source_target_pairs={{0,2},{1,3},{2,0},{3,1},{4,6},{5,7},{6,4},{7,5},{8,10},{9,11},{10,... | collective-permute-start | bytes 442376 | tf_op jit(solution)/shard_map/ppermute | solution.py:336
  40.3 5.7 %collective-permute-start.9 = (bf16[1,9,16,256]{3,2,1,0:T(8,128)(2,1)S(1)}, bf16[1,9,16,256]{3,2,1,0:T(8,128)(2,1)S(1)}, u32[]{:S(2)}, u32[]{:S(2)}) collective-permute-start(bf16[1,9,16,256]{3,2,1,0:T(8,128)(2,1)S(1)} %slice.82), channel_id=1, source_target_pairs={{0,8},{1,9},{2,10},{3,11},{4,12},{5,13},{6,14},{7,15},{8,0},{9,1},... | collective-permute-start | bytes 221192 | tf_op jit(solution)/shard_map/ppermute | solution.py:336
  43.2 5.6 %collective-permute-start.5 = (bf16[1,9,16,256]{3,2,1,0:T(8,128)(2,1)S(1)}, bf16[1,9,16,256]{3,2,1,0:T(8,128)(2,1)S(1)}, u32[]{:S(2)}, u32[]{:S(2)}) collective-permute-start(bf16[1,9,16,256]{3,2,1,0:T(8,128)(2,1)S(1)} %slice.83), channel_id=1, source_target_pairs={{0,8},{1,9},{2,10},{3,11},{4,12},{5,13},{6,14},{7,15},{8,0},{9,1},... | collective-permute-start | bytes 221192 | tf_op jit(solution)/shard_map/ppermute | solution.py:336
